TPU v7x, 32 devices: a whole 2x2x4 slice. The times are simulated.
32 devices in a mesh: rep: 4 (over y, x), row: 8 (over z, core).
Axes of the slice: x: 2, y: 2, z: 4, core: 2. Of those that a mesh axis runs over, the one named last changes fastest.
Arguments:
- node_feat: float32 [4096, 256], P(('rep', 'row')), may hold values from -6 to 6
- weight: float32 [256, 256], replicated, may hold values from -0.375 to 0.375
- bias: float32 [256], replicated, may hold values from -0.5 to 0.5
- cotangent: float32 [4096, 256], P(('rep', 'row')), may hold values from -6 to 6
- blocks: float32 [4, 8, 64, 4096], P('rep', 'row'), may hold values from -0.1875 to 0.1875
- row_block: int32 [4, 8, 64], P('rep', 'row'), may hold values from 0 to 7
- col_block: int32 [4, 8, 64], P('rep', 'row'), may hold values from 0 to 3
- live_blocks: int32 [4, 8], P('rep', 'row'), may hold values from 12 to 64, as said below
- send_list: int32 [4, 2048], P('rep'), may hold values from 0 to 127
Outputs:
- activated: float32 [4096, 256], P(('rep', 'row'))
- feat_grad: float32 [4096, 256], P(('rep', 'row'))
- weight_grad: float32 [256, 256], replicated
- bias_grad: float32 [256], replicated
Inputs may be any that keep to these rules, and one draw needn't show every extreme that they name: `live_blocks`: each value is 64 divided by a whole number from 1 to 5, rounded down; some device has all 64 slots used.
All inputs are finite; a program needn't handle non-finite values.
Results may differ from a plain program's by a relative error of at most 0.0001.
Values sent between devices are 32-bit elements; how exact they have to be, the bound alone decides.
No kernel may reach another device: no remote copies, remote signals or barrier semaphores. Data moves between devices by JAX's collectives and lax.ppermute only.
A program may use at most 64 MiB of HBM per device.

v0:
```python
import functools

import jax
import jax.numpy as jnp
from jax import lax
from jax.experimental import pallas as pl
from jax.experimental.pallas import tpu as pltpu
from jax.sharding import PartitionSpec as P


BS = 64
LANES = 128
PAD = 8
FLOOR = 16 * 2**20
F32 = jnp.float32
BF16 = jnp.bfloat16
NN = (((1,), (0,)), ((), ()))
TN = (((0,), (0,)), ((), ()))
NT = (((1,), (1,)), ((), ()))


def split(x):
    high = x.astype(BF16)
    return high, (x - high.astype(F32)).astype(BF16)


def mm(a, b, dims):
    return lax.dot_general(a, b, dims, preferred_element_type=F32)


def mm3(a, b, dims):
    return mm(a[0], b[0], dims) + (mm(a[0], b[1], dims) + mm(a[1], b[0], dims))


def call(kernel, outs, args, scratch=(), flops=0, smem=(), hbm=()):
    out_bytes = sum(int(o.size) * o.dtype.itemsize for o in outs)
    in_bytes = sum(int(a.size) * a.dtype.itemsize for a in args)
    limit = max(FLOOR, 4 * (in_bytes + out_bytes))
    return pl.pallas_call(
        kernel,
        out_shape=outs,
        in_specs=[
            pl.BlockSpec(
                memory_space=pltpu.SMEM if k in smem else pltpu.HBM if k in hbm else pltpu.VMEM
            )
            for k in range(len(args))
        ],
        out_specs=[pl.BlockSpec(memory_space=pltpu.VMEM) for _ in outs],
        scratch_shapes=list(scratch),
        cost_estimate=pl.CostEstimate(
            flops=flops, transcendentals=0, bytes_accessed=in_bytes + out_bytes
        ),
        compiler_params=pltpu.CompilerParams(vmem_limit_bytes=limit),
    )(*args)


def rows_at(index, count):
    return pl.ds(pl.multiple_of(index * count, count), count)


def one_hot(wanted, nodes):
    node = lax.broadcasted_iota(jnp.int32, (nodes, wanted.shape[1]), 0)
    return (node == wanted).astype(BF16)


def tree_sum(terms):
    terms = list(terms)
    while len(terms) > 1:
        terms = [terms[k] + terms[k + 1] for k in range(0, len(terms), 2)]
    return terms[0]


def put_pairs(outs, buffer, me, per):
    for pair, out in enumerate(outs):
        for core in range(2):
            source = rows_at(lax.bitwise_xor(me, 2 * pair + core), per)
            out[core * per : (core + 1) * per, :] = buffer[source, :]


def take_pairs(own_ref, partner_ref, buffer, me, per):
    for pair in range(buffer.shape[0] // (2 * per)):
        rows = slice(pair * per, (pair + 1) * per)
        buffer[rows_at(lax.bitwise_xor(me, 2 * pair), per), :] = own_ref[rows, :]
        buffer[rows_at(lax.bitwise_xor(me, 2 * pair + 1), per), :] = partner_ref[rows, :]


def gather_rows(list_hbm, feat_hbm, *refs):
    outs, wanted_ref, feat_ref, buffer, sems = refs[:-4], refs[-4], refs[-3], refs[-2], refs[-1]
    me = lax.axis_index("row")
    slots = buffer.shape[0]
    copies = [
        pltpu.make_async_copy(feat_hbm, feat_ref, sems.at[0]),
        pltpu.make_async_copy(list_hbm.at[:, rows_at(me, slots)], wanted_ref, sems.at[1]),
    ]
    for copy in copies:
        copy.start()
    for copy in copies:
        copy.wait()
    pick = one_hot(wanted_ref[...], feat_ref.shape[0])
    high, low = split(feat_ref[...])
    buffer[...] = mm(pick, high, TN) + mm(pick, low, TN)
    put_pairs(outs, buffer, me, outs[0].shape[0] // 2)


def aggregate(groups, row_blocks, per, high_ref, low_ref, own_ref, partner_ref, *refs):
    outs, border, natural = refs[:groups], refs[groups], refs[groups + 1]
    me, group = lax.axis_index("row"), lax.axis_index("rep")
    take_pairs(own_ref, partner_ref, border, me, per)
    result = mm3((high_ref[...], low_ref[...]), split(border[...]), NN)
    unmix(result, natural, row_blocks)
    nodes = outs[0].shape[0]
    for s in range(groups):
        for part in range(natural.shape[0]):
            outs[s][:, part * LANES : (part + 1) * LANES] = natural[
                part, rows_at(lax.bitwise_xor(group, s), nodes), :
            ]


def unmix(result, natural, row_blocks):
    for m in range(BS):
        start = ((m % 2) * (BS // 2) + m // 2) * row_blocks
        for part in range(natural.shape[0]):
            natural[part, pl.ds(m, row_blocks, stride=BS), :] = result[
                start : start + row_blocks, part * LANES : (part + 1) * LANES
            ]


def activate(groups, members, *refs):
    pieces = refs[:groups]
    weight_ref, bias_ref, cot_ref, act_ref, grad_ref, keep_ref, send_ref, part_ref, buffer = refs[groups:]
    me = lax.axis_index("row")
    total = tree_sum([piece[...] for piece in pieces])
    total_split = split(total)
    pre = mm3(total_split, split(weight_ref[...]), NN) + bias_ref[...]
    gate = jax.nn.sigmoid(pre)
    act_ref[...] = pre * gate
    grad = cot_ref[...] * (gate * (1.0 + pre * (1.0 - gate)))
    grad_ref[...] = grad
    buffer[...] = mm3(total_split, split(grad), TN)
    chunk = buffer.shape[0] // members
    for s in range(members):
        target = send_ref if s % 2 else keep_ref
        start = (s // 2) * chunk
        target[start : start + chunk, :] = buffer[rows_at(lax.bitwise_xor(me, s), chunk), :]
    sums = jnp.sum(grad, axis=0, keepdims=True)
    part_ref[...] = jnp.broadcast_to(sums, part_ref.shape)


def spread(groups, pairs, row_blocks, high_ref, low_ref, *refs):
    pieces, outs = refs[:groups], refs[groups : groups + pairs]
    natural, border = refs[groups + pairs :]
    me, group = lax.axis_index("row"), lax.axis_index("rep")
    nodes = pieces[0].shape[0]
    for s in range(groups):
        for part in range(natural.shape[0]):
            natural[part, rows_at(lax.bitwise_xor(group, s), nodes), :] = pieces[s][
                :, part * LANES : (part + 1) * LANES
            ]
    order = []
    for parity in range(2):
        for t in range(BS // 2):
            order.append(
                jnp.concatenate(
                    [
                        natural[part, pl.ds(2 * t + parity, row_blocks, stride=BS), :]
                        for part in range(natural.shape[0])
                    ],
                    axis=1,
                )
            )
    mixed = jnp.concatenate(order, axis=0)
    border[...] = mm3((high_ref[...], low_ref[...]), split(mixed), NN)
    put_pairs(outs, border, me, outs[0].shape[0] // 2)


def collect(per, wanted_ref, weight_ref, own_ref, partner_ref, out_ref, border):
    me = lax.axis_index("row")
    take_pairs(own_ref, partner_ref, border, me, per)
    pick = one_hot(wanted_ref[...], out_ref.shape[0])
    high, low = split(border[...])
    proj = mm(pick, high, NN) + mm(pick, low, NN)
    out_ref[...] = mm3(split(proj), split(weight_ref[...]), NT)


def finish(members, own_ref, partner_ref, weight_ref, bias_ref):
    me = lax.axis_index("row")
    step = own_ref.shape[0] // (members // 2)
    chunk = step - PAD
    terms = []
    for s in range(members):
        piece = partner_ref if s % 2 else own_ref
        start = (s // 2) * step
        weight_ref[rows_at(lax.bitwise_xor(me, s), chunk), :] = piece[start : start + chunk, :]
        terms.append(piece[start + chunk : start + chunk + 1, :])
    bias_ref[...] = tree_sum(terms)


def exchange(value, axis, shift):
    size = lax.axis_size(axis)
    return lax.ppermute(value, axis, [(i, i ^ shift) for i in range(size)])


def swap_rows(sends):
    pieces = [sends[0]]
    pieces += [exchange(sends[p], "row", 2 * p) for p in range(1, len(sends))]
    per = sends[0].shape[0] // 2
    own = jnp.concatenate([piece[:per] for piece in pieces], axis=0)
    partner = jnp.concatenate([piece[per:] for piece in pieces], axis=0)
    return [own, exchange(partner, "row", 1)]


def layer(
    node_feat, weight, bias, cotangent, blocks, row_block, col_block, live_blocks, send_list
):
    nodes, width = node_feat.shape
    groups, members = lax.axis_size("rep"), lax.axis_size("row")
    capacity = blocks.shape[2]
    per = send_list.shape[-1] // (members * members)
    slots = members * per
    row_blocks = groups * nodes // BS
    col_blocks = slots // BS
    rows = row_blocks * BS
    pairs = members // 2
    shape = lambda n: jax.ShapeDtypeStruct((n, width), F32)
    vmem = lambda n: pltpu.VMEM((n, width), F32)
    tiles = pltpu.VMEM((width // LANES, rows, LANES), F32)

    *sends, wanted = call(
        gather_rows,
        [shape(2 * per)] * pairs + [jax.ShapeDtypeStruct((1, slots), jnp.int32)],
        [pltpu.with_memory_space_constraint(x, pltpu.HBM) for x in (send_list, node_feat)],
        [vmem(nodes), vmem(slots), pltpu.SemaphoreType.DMA((2,))],
        hbm=(0, 1),
    )
    border = swap_rows(sends)
    wide = jax.ShapeDtypeStruct((rows, slots), BF16)
    tall = jax.ShapeDtypeStruct((slots, rows), BF16)
    bias_row = jax.ShapeDtypeStruct((1, width), F32)
    *dense, bias_here = call(
        functools.partial(build, row_blocks, col_blocks),
        [wide, wide, tall, tall, bias_row],
        [live_blocks, row_block[0], col_block[0], blocks[0, 0], bias[None, :]],
        [pltpu.VMEM((rows, slots), F32)],
        flops=4 * row_blocks * col_blocks * capacity * BS * BS,
        smem=(0,),
    )
    partials = call(
        functools.partial(aggregate, groups, row_blocks, per),
        [shape(nodes)] * groups,
        dense[:2] + border,
        [vmem(slots), tiles],
        flops=6 * rows * slots * width,
    )
    parts = [partials[0]] + [exchange(partials[s], "rep", s) for s in range(1, groups)]
    activated, grad, keep, send, bias_part = call(
        functools.partial(activate, groups, members),
        [shape(nodes), shape(nodes), shape(width // 2), shape(width // 2), shape(PAD)],
        parts + [weight, bias_here, cotangent],
        [vmem(width)],
        flops=12 * nodes * width * width,
    )
    grads = [grad] + [exchange(grad, "rep", s) for s in range(1, groups)]
    backs = call(
        functools.partial(spread, groups, pairs, row_blocks),
        [shape(2 * per)] * pairs,
        dense[2:] + grads,
        [tiles, vmem(slots)],
        flops=6 * rows * slots * width,
    )
    returned = swap_rows(backs)
    (feat_grad,) = call(
        functools.partial(collect, per),
        [shape(nodes)],
        [wanted, weight] + returned,
        [vmem(slots)],
        flops=6 * nodes * width * width,
    )
    total = keep + exchange(send, "row", 1)
    size = width // members
    owned = [total[p * size : (p + 1) * size] for p in range(pairs)]
    owned[1:] = [exchange(owned[p], "row", 2 * p) for p in range(1, pairs)]
    chunk = jnp.concatenate([tree_sum(owned), bias_part], axis=0)
    summed = tree_sum([chunk] + [exchange(chunk, "rep", s) for s in range(1, groups)])
    chunks = [summed]
    chunks += [exchange(summed, "row", 2 * p) for p in range(1, pairs)]
    own = jnp.concatenate(chunks, axis=0)
    partner = exchange(own, "row", 1)
    weight_grad, bias_grad = call(
        functools.partial(finish, members), [shape(width), shape(1)], [own, partner]
    )
    return (activated, feat_grad, weight_grad, bias_grad[0])


def build(row_blocks, col_blocks, live_ref, rows_ref, cols_ref, blocks_ref, bias_ref, *refs):
    high_ref, low_ref, high_t_ref, low_t_ref, bias_out, out_ref = refs
    bias_out[...] = bias_ref[...]
    capacity = blocks_ref.shape[0]
    pairs = row_blocks * col_blocks
    steps = blocks_ref.shape[1] // LANES
    pair_of = cols_ref[...] * row_blocks + rows_ref[...]
    pair = lax.broadcasted_iota(jnp.int32, (pairs, capacity), 0)
    slot = lax.broadcasted_iota(jnp.int32, (pairs, capacity), 1)
    pick = ((pair == pair_of) & (slot < live_ref[0, 0])).astype(BF16)
    high, low = split(blocks_ref[...])
    dense = mm(pick, high, NN) + mm(pick, low, NN)
    left = lax.broadcasted_iota(jnp.int32, (row_blocks, LANES), 1) < BS
    for t in range(steps):
        lanes = slice(t * LANES, (t + 1) * LANES)
        for u in range(col_blocks // 2):
            first = dense[2 * u * row_blocks : (2 * u + 1) * row_blocks, lanes]
            second = dense[(2 * u + 1) * row_blocks : (2 * u + 2) * row_blocks, lanes]
            even = jnp.where(left, first, pltpu.roll(second, BS, 1))
            odd = jnp.where(left, pltpu.roll(first, BS, 1), second)
            for parity, value in ((0, even), (1, odd)):
                start = (parity * steps + t) * row_blocks
                out_ref[start : start + row_blocks, u * LANES : (u + 1) * LANES] = value
    full = out_ref[...]
    high_ref[...], low_ref[...] = split(full)
    high_t_ref[...], low_t_ref[...] = split(full.T)


def solution(mesh):
    return sharded(mesh)


def sharded(mesh):
    return jax.shard_map(
        layer,
        mesh=mesh,
        in_specs=(
            P(("rep", "row"), None),
            P(),
            P(),
            P(("rep", "row"), None),
            P("rep", "row", None, None),
            P("rep", "row", None),
            P("rep", "row", None),
            P("rep", "row"),
            P("rep", None),
        ),
        out_specs=(P(("rep", "row"), None), P(("rep", "row"), None), P(), P()),
        check_vma=False,
    )
```

profile of v0, /device:TPU:0, one launch (start us, length us, event | category | flops | bytes accessed | tf_op | source)
XLA Modules:
  0.0 60.7 jit_solution(8276058775384825099)
XLA Ops:
  0.6 1.2 %shard_map.121 = (f32[64,256]{1,0:T(8,128)S(1)}, f32[64,256]{1,0:T(8,128)S(1)}, f32[64,256]{1,0:T(8,128)S(1)}, f32[64,256]{1,0:T(8,128)S(1)}, s32[1,256]{1,0:T(1,128)S(1)}) custom-call(s32[1,2048]{1,0:T(1,128)} %list_hbm.1, f32[128,256]{1,0:T(8,128)} %feat_hbm.1), custom_call_target="tpu_custom_call" | custom-call | bytes 402432 | tf_op jit(solution)/shard_map/pallas_call | solution.py:39
  1.8 3.1 %collective-permute-start = (f32[64,256]{1,0:T(8,128)S(1)}, f32[64,256]{1,0:T(8,128)S(1)}, u32[]{:S(2)}, u32[]{:S(2)}) collective-permute-start(f32[64,256]{1,0:T(8,128)S(1)} %get-tuple-element.32), channel_id=1, source_target_pairs={{0,2},{1,3},{2,0},{3,1},{4,6},{5,7},{6,4},{7,5},{8,10},{9,11},{10,... | collective-permute-start | bytes 196616 | tf_op jit(solution)/shard_map/ppermute | solution.py:200
  5.0 2.6 %collective-permute-start.1 = (f32[64,256]{1,0:T(8,128)S(1)}, f32[64,256]{1,0:T(8,128)S(1)}, u32[]{:S(2)}, u32[]{:S(2)}) collective-permute-start(f32[64,256]{1,0:T(8,128)S(1)} %get-tuple-element.33), channel_id=1, source_target_pairs={{0,4},{1,5},{2,6},{3,7},{4,0},{5,1},{6,2},{7,3},{8,12},{9,13},{10,... | collective-permute-start | bytes 196616 | tf_op jit(solution)/shard_map/ppermute | solution.py:200
  7.5 0.0 collective-permute-start.2
  7.6 0.0 collective-permute-done
  7.6 4.6 %collective-permute-done.1 = f32[64,256]{1,0:T(8,128)S(1)} collective-permute-done((f32[64,256]{1,0:T(8,128)S(1)}, f32[64,256]{1,0:T(8,128)S(1)}, u32[]{:S(2)}, u32[]{:S(2)}) %collective-permute-start.1) | collective-permute-done | bytes 65568 | tf_op jit(solution)/shard_map/ppermute | solution.py:200
  12.2 1.4 %collective-permute-done.2 = f32[64,256]{1,0:T(8,128)S(1)} collective-permute-done((f32[64,256]{1,0:T(8,128)S(1)}, f32[64,256]{1,0:T(8,128)S(1)}, u32[]{:S(2)}, u32[]{:S(2)}) %collective-permute-start.2) | collective-permute-done | bytes 65568 | tf_op jit(solution)/shard_map/ppermute | solution.py:200
  13.6 0.1 collective-permute-start.3
  14.4 0.0 copy-start.3
  14.4 0.0 copy-start.4
  14.4 0.6 %copy-done.3 = f32[256]{0:T(256)S(1)} copy-done((f32[256]{0:T(256)S(1)}, f32[256]{0:T(256)}, u32[]{:S(2)}) %copy-start.3) | copy-done | bytes 1048
  15.1 0.0 copy-done.4
  15.1 1.2 %copy-done = f32[1,1,64,4096]{3,2,1,0:T(8,128)S(1)} copy-done((f32[1,1,64,4096]{3,2,1,0:T(8,128)S(1)}, f32[1,1,64,4096]{3,2,1,0:T(8,128)}, u32[]{:S(2)}) %copy-start) | copy-done | bytes 1048600
  16.3 0.6 %shard_map.120 = (bf16[512,256]{1,0:T(8,128)(2,1)S(1)}, bf16[512,256]{1,0:T(8,128)(2,1)S(1)}, bf16[256,512]{1,0:T(8,128)(2,1)S(1)}, bf16[256,512]{1,0:T(8,128)(2,1)S(1)}, f32[1,256]{1,0:T(1,128)S(1)}) custom-call(s32[1,1]{1,0:T(1,128)S(6)} %copy.13.live_ref, s32[1,64]{1,0:T(1,128)S(1)} %bitcast.7, s32[1,64]{1,0:T(1,128)S(1)} %bitcast.8, ...), custom_call_target="tpu_custom_call" | custom-call | flops 33554432 | bytes 2099716 | tf_op jit(solution)/shard_map/pallas_call | solution.py:39
  16.9 0.0 collective-permute-done.3.partner_ref
  16.9 0.0 copy-start.1
  16.9 0.0 copy-start.2
  17.0 0.8 %shard_map.122 = (f32[128,256]{1,0:T(8,128)S(1)}, f32[128,256]{1,0:T(8,128)S(1)}, f32[128,256]{1,0:T(8,128)S(1)}, f32[128,256]{1,0:T(8,128)S(1)}) custom-call(bf16[512,256]{1,0:T(8,128)(2,1)S(1)} %get-tuple-element.29.high_ref, bf16[512,256]{1,0:T(8,128)(2,1)S(1)} %get-tuple-element.30.low_ref, f32[128,256]{1,0:T(8,128)S(1)} %pad_maximum_fusion.1.own_ref, ...), custom_call_target="tpu_custom_call" | custom-call | flops 201326592 | bytes 1310720 | tf_op jit(solution)/shard_map/pallas_call | solution.py:39
  17.8 1.6 %collective-permute-start.4 = (f32[128,256]{1,0:T(8,128)S(1)}, f32[128,256]{1,0:T(8,128)S(1)}, u32[]{:S(2)}, u32[]{:S(2)}) collective-permute-start(f32[128,256]{1,0:T(8,128)S(1)} %get-tuple-element.36), channel_id=1, source_target_pairs={{0,8},{8,0},{16,24},{24,16},{1,9},{9,1},{17,25},{25,17},{2,10},{10... | collective-permute-start | bytes 393224 | tf_op jit(solution)/shard_map/ppermute | solution.py:200
  19.3 1.5 %collective-permute-start.5 = (f32[128,256]{1,0:T(8,128)S(1)}, f32[128,256]{1,0:T(8,128)S(1)}, u32[]{:S(2)}, u32[]{:S(2)}) collective-permute-start(f32[128,256]{1,0:T(8,128)S(1)} %get-tuple-element.37), channel_id=1, source_target_pairs={{0,16},{8,24},{16,0},{24,8},{1,17},{9,25},{17,1},{25,9},{2,18},{10... | collective-permute-start | bytes 393224 | tf_op jit(solution)/shard_map/ppermute | solution.py:200
  20.8 0.5 collective-permute-start.6
  21.3 2.8 %collective-permute-done.4.refs_1_ = f32[128,256]{1,0:T(8,128)S(1)} collective-permute-done((f32[128,256]{1,0:T(8,128)S(1)}, f32[128,256]{1,0:T(8,128)S(1)}, u32[]{:S(2)}, u32[]{:S(2)}) %collective-permute-start.4) | collective-permute-done | bytes 131104 | tf_op jit(solution)/shard_map/ppermute | solution.py:200
  24.1 3.6 %collective-permute-done.5.refs_2_ = f32[128,256]{1,0:T(8,128)S(1)} collective-permute-done((f32[128,256]{1,0:T(8,128)S(1)}, f32[128,256]{1,0:T(8,128)S(1)}, u32[]{:S(2)}, u32[]{:S(2)}) %collective-permute-start.5) | collective-permute-done | bytes 131104 | tf_op jit(solution)/shard_map/ppermute | solution.py:200
  27.8 0.0 collective-permute-done.6.refs_3_
  27.8 0.9 %shard_map.123 = (f32[128,256]{1,0:T(8,128)}, f32[128,256]{1,0:T(8,128)S(1)}, f32[128,256]{1,0:T(8,128)S(1)}, f32[128,256]{1,0:T(8,128)S(1)}, f32[8,256]{1,0:T(8,128)S(1)}) custom-call(f32[128,256]{1,0:T(8,128)S(1)} %get-tuple-element.35.refs_0_, f32[128,256]{1,0:T(8,128)S(1)} %collective-permute-done.4.refs_1_, ...), custom_call_target="tpu_custom_call" | custom-call | flops 100663296 | bytes 1451008 | tf_op jit(solution)/shard_map/pallas_call | solution.py:39
  28.7 0.0 collective-permute-start.14
  28.7 1.5 %collective-permute-start.9 = (f32[128,256]{1,0:T(8,128)S(1)}, f32[128,256]{1,0:T(8,128)S(1)}, u32[]{:S(2)}, u32[]{:S(2)}) collective-permute-start(f32[128,256]{1,0:T(8,128)S(1)} %get-tuple-element.44.refs_0_), channel_id=1, source_target_pairs={{0,24},{8,16},{16,8},{24,0},{1,25},{9,17},{17,9},{25,1},{2,26},{10... | collective-permute-start | bytes 393224 | tf_op jit(solution)/shard_map/ppermute | solution.py:200
  30.2 1.2 %collective-permute-start.8 = (f32[128,256]{1,0:T(8,128)S(1)}, f32[128,256]{1,0:T(8,128)S(1)}, u32[]{:S(2)}, u32[]{:S(2)}) collective-permute-start(f32[128,256]{1,0:T(8,128)S(1)} %get-tuple-element.44.refs_0_), channel_id=1, source_target_pairs={{0,16},{8,24},{16,0},{24,8},{1,17},{9,25},{17,1},{25,9},{2,18},{10... | collective-permute-start | bytes 393224 | tf_op jit(solution)/shard_map/ppermute | solution.py:200
  31.4 0.8 %collective-permute-start.7 = (f32[128,256]{1,0:T(8,128)S(1)}, f32[128,256]{1,0:T(8,128)S(1)}, u32[]{:S(2)}, u32[]{:S(2)}) collective-permute-start(f32[128,256]{1,0:T(8,128)S(1)} %get-tuple-element.44.refs_0_), channel_id=1, source_target_pairs={{0,8},{8,0},{16,24},{24,16},{1,9},{9,1},{17,25},{25,17},{2,10},{10... | collective-permute-start | bytes 393224 | tf_op jit(solution)/shard_map/ppermute | solution.py:200
  32.2 0.0 collective-permute-done.14
  32.2 1.9 %collective-permute-start.17 = (f32[32,256]{1,0:T(8,128)S(1)}, f32[32,256]{1,0:T(8,128)S(1)}, u32[]{:S(2)}, u32[]{:S(2)}) collective-permute-start(f32[32,256]{1,0:T(8,128)S(1)} %get-tuple-element.54), channel_id=1, source_target_pairs={{0,6},{1,7},{2,4},{3,5},{4,2},{5,3},{6,0},{7,1},{8,14},{9,15},{10,... | collective-permute-start | bytes 98312 | tf_op jit(solution)/shard_map/ppermute | solution.py:200
  34.1 0.0 collective-permute-start.16
  34.1 1.9 %collective-permute-done.9.refs_3_ = f32[128,256]{1,0:T(8,128)S(1)} collective-permute-done((f32[128,256]{1,0:T(8,128)S(1)}, f32[128,256]{1,0:T(8,128)S(1)}, u32[]{:S(2)}, u32[]{:S(2)}) %collective-permute-start.9) | collective-permute-done | bytes 131104 | tf_op jit(solution)/shard_map/ppermute | solution.py:200
  36.0 0.7 %collective-permute-start.15 = (f32[32,256]{1,0:T(8,128)S(1)}, f32[32,256]{1,0:T(8,128)S(1)}, u32[]{:S(2)}, u32[]{:S(2)}) collective-permute-start(f32[32,256]{1,0:T(8,128)S(1)} %get-tuple-element.56), channel_id=1, source_target_pairs={{0,2},{1,3},{2,0},{3,1},{4,6},{5,7},{6,4},{7,5},{8,10},{9,11},{10,... | collective-permute-start | bytes 98312 | tf_op jit(solution)/shard_map/ppermute | solution.py:200
  36.7 1.6 %collective-permute-done.8.refs_2_ = f32[128,256]{1,0:T(8,128)S(1)} collective-permute-done((f32[128,256]{1,0:T(8,128)S(1)}, f32[128,256]{1,0:T(8,128)S(1)}, u32[]{:S(2)}, u32[]{:S(2)}) %collective-permute-start.8) | collective-permute-done | bytes 131104 | tf_op jit(solution)/shard_map/ppermute | solution.py:200
  38.3 0.1 collective-permute-done.7.refs_1_
  38.4 0.7 %shard_map.124 = (f32[64,256]{1,0:T(8,128)S(1)}, f32[64,256]{1,0:T(8,128)S(1)}, f32[64,256]{1,0:T(8,128)S(1)}, f32[64,256]{1,0:T(8,128)S(1)}) custom-call(bf16[256,512]{1,0:T(8,128)(2,1)S(1)} %get-tuple-element.42.high_ref, bf16[256,512]{1,0:T(8,128)(2,1)S(1)} %get-tuple-element.43.low_ref, f32[128,256]{1,0:T(8,128)S(1)} %get-tuple-element.44.refs_0_, ...), custom_call_target="tpu_custom_call" | custom-call | flops 201326592 | bytes 1310720 | tf_op jit(solution)/shard_map/pallas_call | solution.py:39
  39.2 0.1 collective-permute-start.10
  39.3 2.4 %collective-permute-start.11 = (f32[64,256]{1,0:T(8,128)S(1)}, f32[64,256]{1,0:T(8,128)S(1)}, u32[]{:S(2)}, u32[]{:S(2)}) collective-permute-start(f32[64,256]{1,0:T(8,128)S(1)} %get-tuple-element.47), channel_id=1, source_target_pairs={{0,4},{1,5},{2,6},{3,7},{4,0},{5,1},{6,2},{7,3},{8,12},{9,13},{10,... | collective-permute-start | bytes 196616 | tf_op jit(solution)/shard_map/ppermute | solution.py:200
  41.6 0.0 collective-permute-done.17
  41.6 2.0 %collective-permute-start.12 = (f32[64,256]{1,0:T(8,128)S(1)}, f32[64,256]{1,0:T(8,128)S(1)}, u32[]{:S(2)}, u32[]{:S(2)}) collective-permute-start(f32[64,256]{1,0:T(8,128)S(1)} %get-tuple-element.48), channel_id=1, source_target_pairs={{0,6},{1,7},{2,4},{3,5},{4,2},{5,3},{6,0},{7,1},{8,14},{9,15},{10,... | collective-permute-start | bytes 196616 | tf_op jit(solution)/shard_map/ppermute | solution.py:200
  43.6 0.0 collective-permute-done.16
  43.6 0.0 collective-permute-done.15
  43.7 1.5 %collective-permute-start.19 = (f32[40,256]{1,0:T(8,128)S(1)}, f32[40,256]{1,0:T(8,128)S(1)}, u32[]{:S(2)}, u32[]{:S(2)}) collective-permute-start(f32[40,256]{1,0:T(8,128)S(1)} %pad_maximum_fusion.5), channel_id=1, source_target_pairs={{0,16},{8,24},{16,0},{24,8},{1,17},{9,25},{17,1},{25,9},{2,18},{10... | collective-permute-start | bytes 122888 | tf_op jit(solution)/shard_map/ppermute | solution.py:200
  45.1 1.2 %collective-permute-start.20 = (f32[40,256]{1,0:T(8,128)S(1)}, f32[40,256]{1,0:T(8,128)S(1)}, u32[]{:S(2)}, u32[]{:S(2)}) collective-permute-start(f32[40,256]{1,0:T(8,128)S(1)} %pad_maximum_fusion.5), channel_id=1, source_target_pairs={{0,24},{8,16},{16,8},{24,0},{1,25},{9,17},{17,9},{25,1},{2,26},{10... | collective-permute-start | bytes 122888 | tf_op jit(solution)/shard_map/ppermute | solution.py:200
  46.3 0.0 collective-permute-done.10
  46.3 0.9 %collective-permute-start.18 = (f32[40,256]{1,0:T(8,128)S(1)}, f32[40,256]{1,0:T(8,128)S(1)}, u32[]{:S(2)}, u32[]{:S(2)}) collective-permute-start(f32[40,256]{1,0:T(8,128)S(1)} %pad_maximum_fusion.5), channel_id=1, source_target_pairs={{0,8},{8,0},{16,24},{24,16},{1,9},{9,1},{17,25},{25,17},{2,10},{10... | collective-permute-start | bytes 122888 | tf_op jit(solution)/shard_map/ppermute | solution.py:200
  47.2 0.5 collective-permute-done.11
  47.7 0.5 collective-permute-done.19
  48.2 1.9 %collective-permute-done.20 = f32[40,256]{1,0:T(8,128)S(1)} collective-permute-done((f32[40,256]{1,0:T(8,128)S(1)}, f32[40,256]{1,0:T(8,128)S(1)}, u32[]{:S(2)}, u32[]{:S(2)}) %collective-permute-start.20) | collective-permute-done | bytes 40992 | tf_op jit(solution)/shard_map/ppermute | solution.py:200
  50.0 0.3 collective-permute-done.18
  50.3 1.9 %collective-permute-start.23 = (f32[40,256]{1,0:T(8,128)S(1)}, f32[40,256]{1,0:T(8,128)S(1)}, u32[]{:S(2)}, u32[]{:S(2)}) collective-permute-start(f32[40,256]{1,0:T(8,128)S(1)} %add_add_fusion), channel_id=1, source_target_pairs={{0,6},{1,7},{2,4},{3,5},{4,2},{5,3},{6,0},{7,1},{8,14},{9,15},{10,... | collective-permute-start | bytes 122888 | tf_op jit(solution)/shard_map/ppermute | solution.py:200
  52.2 0.0 collective-permute-start.22
  52.2 2.6 %collective-permute-start.21 = (f32[40,256]{1,0:T(8,128)S(1)}, f32[40,256]{1,0:T(8,128)S(1)}, u32[]{:S(2)}, u32[]{:S(2)}) collective-permute-start(f32[40,256]{1,0:T(8,128)S(1)} %add_add_fusion), channel_id=1, source_target_pairs={{0,2},{1,3},{2,0},{3,1},{4,6},{5,7},{6,4},{7,5},{8,10},{9,11},{10,... | collective-permute-start | bytes 122888 | tf_op jit(solution)/shard_map/ppermute | solution.py:200
  54.8 0.0 collective-permute-done.12
  54.8 1.4 %collective-permute-done.23 = f32[40,256]{1,0:T(8,128)S(1)} collective-permute-done((f32[40,256]{1,0:T(8,128)S(1)}, f32[40,256]{1,0:T(8,128)S(1)}, u32[]{:S(2)}, u32[]{:S(2)}) %collective-permute-start.23) | collective-permute-done | bytes 40992 | tf_op jit(solution)/shard_map/ppermute | solution.py:200
  56.2 1.0 %collective-permute-done.22 = f32[40,256]{1,0:T(8,128)S(1)} collective-permute-done((f32[40,256]{1,0:T(8,128)S(1)}, f32[40,256]{1,0:T(8,128)S(1)}, u32[]{:S(2)}, u32[]{:S(2)}) %collective-permute-start.22) | collective-permute-done | bytes 40992 | tf_op jit(solution)/shard_map/ppermute | solution.py:200
  57.2 0.0 collective-permute-done.21
  57.2 0.1 collective-permute-start.24
  57.3 0.6 collective-permute-start.13
  57.9 1.0 %collective-permute-done.13.partner_ref = f32[128,256]{1,0:T(8,128)S(1)} collective-permute-done((f32[128,256]{1,0:T(8,128)S(1)}, f32[128,256]{1,0:T(8,128)S(1)}, u32[]{:S(2)}, u32[]{:S(2)}) %collective-permute-start.13) | collective-permute-done | bytes 131104 | tf_op jit(solution)/shard_map/ppermute | solution.py:200
  58.9 1.1 %shard_map.125 = f32[128,256]{1,0:T(8,128)} custom-call(s32[1,256]{1,0:T(1,128)S(1)} %get-tuple-element.41.wanted_ref, f32[256,256]{1,0:T(8,128)S(1)} %copy-done.1, f32[128,256]{1,0:T(8,128)S(1)} %pad_maximum_fusion.3.own_ref, f32[128,256]{1,0:T(8,128)S(1)} %collective-permute-done.13.partner_ref), custom_call_target="tpu_custom_call" | custom-call | flops 50331648 | bytes 656384 | tf_op jit(solution)/shard_map/pallas_call | solution.py:39
  60.0 0.0 collective-permute-done.24.partner_ref
  60.0 0.7 %shard_map.126 = (f32[256,256]{1,0:T(8,128)}, f32[1,256]{1,0:T(1,128)}) custom-call(f32[160,256]{1,0:T(8,128)S(1)} %pad_maximum_fusion.own_ref, f32[160,256]{1,0:T(8,128)S(1)} %collective-permute-done.24.partner_ref), custom_call_target="tpu_custom_call" | custom-call | bytes 590848 | tf_op jit(solution)/shard_map/pallas_call | solution.py:39
  (23 shorter events, 0.2 us)
Async XLA Ops:
  1.8 5.7 %collective-permute-start = (f32[64,256]{1,0:T(8,128)S(1)}, f32[64,256]{1,0:T(8,128)S(1)}, u32[]{:S(2)}, u32[]{:S(2)}) collective-permute-start(f32[64,256]{1,0:T(8,128)S(1)} %get-tuple-element.32), channel_id=1, source_target_pairs={{0,2},{1,3},{2,0},{3,1},{4,6},{5,7},{6,4},{7,5},{8,10},{9,11},{10,... | collective-permute-start | bytes 196616 | tf_op jit(solution)/shard_map/ppermute | solution.py:200
  5.0 7.3 %collective-permute-start.1 = (f32[64,256]{1,0:T(8,128)S(1)}, f32[64,256]{1,0:T(8,128)S(1)}, u32[]{:S(2)}, u32[]{:S(2)}) collective-permute-start(f32[64,256]{1,0:T(8,128)S(1)} %get-tuple-element.33), channel_id=1, source_target_pairs={{0,4},{1,5},{2,6},{3,7},{4,0},{5,1},{6,2},{7,3},{8,12},{9,13},{10,... | collective-permute-start | bytes 196616 | tf_op jit(solution)/shard_map/ppermute | solution.py:200
  7.5 6.1 %collective-permute-start.2 = (f32[64,256]{1,0:T(8,128)S(1)}, f32[64,256]{1,0:T(8,128)S(1)}, u32[]{:S(2)}, u32[]{:S(2)}) collective-permute-start(f32[64,256]{1,0:T(8,128)S(1)} %get-tuple-element.34), channel_id=1, source_target_pairs={{0,6},{1,7},{2,4},{3,5},{4,2},{5,3},{6,0},{7,1},{8,14},{9,15},{10,... | collective-permute-start | bytes 196616 | tf_op jit(solution)/shard_map/ppermute | solution.py:200
  13.6 0.8 %copy-start.5 = (s32[1,1,64]{2,1,0:T(1,128)S(1)}, s32[1,1,64]{2,1,0:T(1,128)}, u32[]{:S(2)}) copy-start(s32[1,1,64]{2,1,0:T(1,128)} %param.15) | copy-start | bytes 772
  13.6 3.3 %collective-permute-start.3 = (f32[128,256]{1,0:T(8,128)S(1)}, f32[128,256]{1,0:T(8,128)S(1)}, u32[]{:S(2)}, u32[]{:S(2)}) collective-permute-start(f32[128,256]{1,0:T(8,128)S(1)} %pad_maximum_fusion.2), channel_id=1, source_target_pairs={{0,1},{1,0},{2,3},{3,2},{4,5},{5,4},{6,7},{7,6},{8,9},{9,8},{10,11... | collective-permute-start | bytes 393224 | tf_op jit(solution)/shard_map/ppermute | solution.py:200
  14.4 0.7 %copy-start.3 = (f32[256]{0:T(256)S(1)}, f32[256]{0:T(256)}, u32[]{:S(2)}) copy-start(f32[256]{0:T(256)} %param.11) | copy-start | bytes 3076
  14.4 0.7 %copy-start.4 = (s32[1,1,64]{2,1,0:T(1,128)S(1)}, s32[1,1,64]{2,1,0:T(1,128)}, u32[]{:S(2)}) copy-start(s32[1,1,64]{2,1,0:T(1,128)} %param.14) | copy-start | bytes 772
  15.1 1.2 %copy-start = (f32[1,1,64,4096]{3,2,1,0:T(8,128)S(1)}, f32[1,1,64,4096]{3,2,1,0:T(8,128)}, u32[]{:S(2)}) copy-start(f32[1,1,64,4096]{3,2,1,0:T(8,128)} %param.13) | copy-start | bytes 3145732
  16.9 10.8 %copy-start.1 = (f32[256,256]{1,0:T(8,128)S(1)}, f32[256,256]{1,0:T(8,128)}, u32[]{:S(2)}) copy-start(f32[256,256]{1,0:T(8,128)} %weight_ref.1) | copy-start | bytes 786436
  16.9 10.8 %copy-start.2 = (f32[128,256]{1,0:T(8,128)S(1)}, f32[128,256]{1,0:T(8,128)}, u32[]{:S(2)}) copy-start(f32[128,256]{1,0:T(8,128)} %refs_6_.1) | copy-start | bytes 393220
  17.8 6.4 %collective-permute-start.4 = (f32[128,256]{1,0:T(8,128)S(1)}, f32[128,256]{1,0:T(8,128)S(1)}, u32[]{:S(2)}, u32[]{:S(2)}) collective-permute-start(f32[128,256]{1,0:T(8,128)S(1)} %get-tuple-element.36), channel_id=1, source_target_pairs={{0,8},{8,0},{16,24},{24,16},{1,9},{9,1},{17,25},{25,17},{2,10},{10... | collective-permute-start | bytes 393224 | tf_op jit(solution)/shard_map/ppermute | solution.py:200
  19.3 8.4 %collective-permute-start.5 = (f32[128,256]{1,0:T(8,128)S(1)}, f32[128,256]{1,0:T(8,128)S(1)}, u32[]{:S(2)}, u32[]{:S(2)}) collective-permute-start(f32[128,256]{1,0:T(8,128)S(1)} %get-tuple-element.37), channel_id=1, source_target_pairs={{0,16},{8,24},{16,0},{24,8},{1,17},{9,25},{17,1},{25,9},{2,18},{10... | collective-permute-start | bytes 393224 | tf_op jit(solution)/shard_map/ppermute | solution.py:200
  20.8 6.9 %collective-permute-start.6 = (f32[128,256]{1,0:T(8,128)S(1)}, f32[128,256]{1,0:T(8,128)S(1)}, u32[]{:S(2)}, u32[]{:S(2)}) collective-permute-start(f32[128,256]{1,0:T(8,128)S(1)} %get-tuple-element.38), channel_id=1, source_target_pairs={{0,24},{8,16},{16,8},{24,0},{1,25},{9,17},{17,9},{25,1},{2,26},{10... | collective-permute-start | bytes 393224 | tf_op jit(solution)/shard_map/ppermute | solution.py:200
  28.7 3.5 %collective-permute-start.14 = (f32[128,256]{1,0:T(8,128)S(1)}, f32[128,256]{1,0:T(8,128)S(1)}, u32[]{:S(2)}, u32[]{:S(2)}) collective-permute-start(f32[128,256]{1,0:T(8,128)S(1)} %get-tuple-element.50), channel_id=1, source_target_pairs={{0,1},{1,0},{2,3},{3,2},{4,5},{5,4},{6,7},{7,6},{8,9},{9,8},{10,11... | collective-permute-start | bytes 393224 | tf_op jit(solution)/shard_map/ppermute | solution.py:200
  28.7 7.3 %collective-permute-start.9 = (f32[128,256]{1,0:T(8,128)S(1)}, f32[128,256]{1,0:T(8,128)S(1)}, u32[]{:S(2)}, u32[]{:S(2)}) collective-permute-start(f32[128,256]{1,0:T(8,128)S(1)} %get-tuple-element.44.refs_0_), channel_id=1, source_target_pairs={{0,24},{8,16},{16,8},{24,0},{1,25},{9,17},{17,9},{25,1},{2,26},{10... | collective-permute-start | bytes 393224 | tf_op jit(solution)/shard_map/ppermute | solution.py:200
  30.2 8.1 %collective-permute-start.8 = (f32[128,256]{1,0:T(8,128)S(1)}, f32[128,256]{1,0:T(8,128)S(1)}, u32[]{:S(2)}, u32[]{:S(2)}) collective-permute-start(f32[128,256]{1,0:T(8,128)S(1)} %get-tuple-element.44.refs_0_), channel_id=1, source_target_pairs={{0,16},{8,24},{16,0},{24,8},{1,17},{9,25},{17,1},{25,9},{2,18},{10... | collective-permute-start | bytes 393224 | tf_op jit(solution)/shard_map/ppermute | solution.py:200
  31.4 7.0 %collective-permute-start.7 = (f32[128,256]{1,0:T(8,128)S(1)}, f32[128,256]{1,0:T(8,128)S(1)}, u32[]{:S(2)}, u32[]{:S(2)}) collective-permute-start(f32[128,256]{1,0:T(8,128)S(1)} %get-tuple-element.44.refs_0_), channel_id=1, source_target_pairs={{0,8},{8,0},{16,24},{24,16},{1,9},{9,1},{17,25},{25,17},{2,10},{10... | collective-permute-start | bytes 393224 | tf_op jit(solution)/shard_map/ppermute | solution.py:200
  32.2 9.4 %collective-permute-start.17 = (f32[32,256]{1,0:T(8,128)S(1)}, f32[32,256]{1,0:T(8,128)S(1)}, u32[]{:S(2)}, u32[]{:S(2)}) collective-permute-start(f32[32,256]{1,0:T(8,128)S(1)} %get-tuple-element.54), channel_id=1, source_target_pairs={{0,6},{1,7},{2,4},{3,5},{4,2},{5,3},{6,0},{7,1},{8,14},{9,15},{10,... | collective-permute-start | bytes 98312 | tf_op jit(solution)/shard_map/ppermute | solution.py:200
  34.1 9.5 %collective-permute-start.16 = (f32[32,256]{1,0:T(8,128)S(1)}, f32[32,256]{1,0:T(8,128)S(1)}, u32[]{:S(2)}, u32[]{:S(2)}) collective-permute-start(f32[32,256]{1,0:T(8,128)S(1)} %get-tuple-element.55), channel_id=1, source_target_pairs={{0,4},{1,5},{2,6},{3,7},{4,0},{5,1},{6,2},{7,3},{8,12},{9,13},{10,... | collective-permute-start | bytes 98312 | tf_op jit(solution)/shard_map/ppermute | solution.py:200
  36.0 7.6 %collective-permute-start.15 = (f32[32,256]{1,0:T(8,128)S(1)}, f32[32,256]{1,0:T(8,128)S(1)}, u32[]{:S(2)}, u32[]{:S(2)}) collective-permute-start(f32[32,256]{1,0:T(8,128)S(1)} %get-tuple-element.56), channel_id=1, source_target_pairs={{0,2},{1,3},{2,0},{3,1},{4,6},{5,7},{6,4},{7,5},{8,10},{9,11},{10,... | collective-permute-start | bytes 98312 | tf_op jit(solution)/shard_map/ppermute | solution.py:200
  39.2 7.2 %collective-permute-start.10 = (f32[64,256]{1,0:T(8,128)S(1)}, f32[64,256]{1,0:T(8,128)S(1)}, u32[]{:S(2)}, u32[]{:S(2)}) collective-permute-start(f32[64,256]{1,0:T(8,128)S(1)} %get-tuple-element.46), channel_id=1, source_target_pairs={{0,2},{1,3},{2,0},{3,1},{4,6},{5,7},{6,4},{7,5},{8,10},{9,11},{10,... | collective-permute-start | bytes 196616 | tf_op jit(solution)/shard_map/ppermute | solution.py:200
  39.3 8.5 %collective-permute-start.11 = (f32[64,256]{1,0:T(8,128)S(1)}, f32[64,256]{1,0:T(8,128)S(1)}, u32[]{:S(2)}, u32[]{:S(2)}) collective-permute-start(f32[64,256]{1,0:T(8,128)S(1)} %get-tuple-element.47), channel_id=1, source_target_pairs={{0,4},{1,5},{2,6},{3,7},{4,0},{5,1},{6,2},{7,3},{8,12},{9,13},{10,... | collective-permute-start | bytes 196616 | tf_op jit(solution)/shard_map/ppermute | solution.py:200
  41.6 13.2 %collective-permute-start.12 = (f32[64,256]{1,0:T(8,128)S(1)}, f32[64,256]{1,0:T(8,128)S(1)}, u32[]{:S(2)}, u32[]{:S(2)}) collective-permute-start(f32[64,256]{1,0:T(8,128)S(1)} %get-tuple-element.48), channel_id=1, source_target_pairs={{0,6},{1,7},{2,4},{3,5},{4,2},{5,3},{6,0},{7,1},{8,14},{9,15},{10,... | collective-permute-start | bytes 196616 | tf_op jit(solution)/shard_map/ppermute | solution.py:200
  43.7 4.5 %collective-permute-start.19 = (f32[40,256]{1,0:T(8,128)S(1)}, f32[40,256]{1,0:T(8,128)S(1)}, u32[]{:S(2)}, u32[]{:S(2)}) collective-permute-start(f32[40,256]{1,0:T(8,128)S(1)} %pad_maximum_fusion.5), channel_id=1, source_target_pairs={{0,16},{8,24},{16,0},{24,8},{1,17},{9,25},{17,1},{25,9},{2,18},{10... | collective-permute-start | bytes 122888 | tf_op jit(solution)/shard_map/ppermute | solution.py:200
  45.1 4.9 %collective-permute-start.20 = (f32[40,256]{1,0:T(8,128)S(1)}, f32[40,256]{1,0:T(8,128)S(1)}, u32[]{:S(2)}, u32[]{:S(2)}) collective-permute-start(f32[40,256]{1,0:T(8,128)S(1)} %pad_maximum_fusion.5), channel_id=1, source_target_pairs={{0,24},{8,16},{16,8},{24,0},{1,25},{9,17},{17,9},{25,1},{2,26},{10... | collective-permute-start | bytes 122888 | tf_op jit(solution)/shard_map/ppermute | solution.py:200
  46.3 4.0 %collective-permute-start.18 = (f32[40,256]{1,0:T(8,128)S(1)}, f32[40,256]{1,0:T(8,128)S(1)}, u32[]{:S(2)}, u32[]{:S(2)}) collective-permute-start(f32[40,256]{1,0:T(8,128)S(1)} %pad_maximum_fusion.5), channel_id=1, source_target_pairs={{0,8},{8,0},{16,24},{24,16},{1,9},{9,1},{17,25},{25,17},{2,10},{10... | collective-permute-start | bytes 122888 | tf_op jit(solution)/shard_map/ppermute | solution.py:200
  50.3 5.9 %collective-permute-start.23 = (f32[40,256]{1,0:T(8,128)S(1)}, f32[40,256]{1,0:T(8,128)S(1)}, u32[]{:S(2)}, u32[]{:S(2)}) collective-permute-start(f32[40,256]{1,0:T(8,128)S(1)} %add_add_fusion), channel_id=1, source_target_pairs={{0,6},{1,7},{2,4},{3,5},{4,2},{5,3},{6,0},{7,1},{8,14},{9,15},{10,... | collective-permute-start | bytes 122888 | tf_op jit(solution)/shard_map/ppermute | solution.py:200
  52.2 5.0 %collective-permute-start.22 = (f32[40,256]{1,0:T(8,128)S(1)}, f32[40,256]{1,0:T(8,128)S(1)}, u32[]{:S(2)}, u32[]{:S(2)}) collective-permute-start(f32[40,256]{1,0:T(8,128)S(1)} %add_add_fusion), channel_id=1, source_target_pairs={{0,4},{1,5},{2,6},{3,7},{4,0},{5,1},{6,2},{7,3},{8,12},{9,13},{10,... | collective-permute-start | bytes 122888 | tf_op jit(solution)/shard_map/ppermute | solution.py:200
  52.2 5.0 %collective-permute-start.21 = (f32[40,256]{1,0:T(8,128)S(1)}, f32[40,256]{1,0:T(8,128)S(1)}, u32[]{:S(2)}, u32[]{:S(2)}) collective-permute-start(f32[40,256]{1,0:T(8,128)S(1)} %add_add_fusion), channel_id=1, source_target_pairs={{0,2},{1,3},{2,0},{3,1},{4,6},{5,7},{6,4},{7,5},{8,10},{9,11},{10,... | collective-permute-start | bytes 122888 | tf_op jit(solution)/shard_map/ppermute | solution.py:200
  57.2 2.8 %collective-permute-start.24 = (f32[160,256]{1,0:T(8,128)S(1)}, f32[160,256]{1,0:T(8,128)S(1)}, u32[]{:S(2)}, u32[]{:S(2)}) collective-permute-start(f32[160,256]{1,0:T(8,128)S(1)} %pad_maximum_fusion.own_ref), channel_id=1, source_target_pairs={{0,1},{1,0},{2,3},{3,2},{4,5},{5,4},{6,7},{7,6},{8,9},{9,8},{10,11... | collective-permute-start | bytes 491528 | tf_op jit(solution)/shard_map/ppermute | solution.py:200
  57.3 1.5 %collective-permute-start.13 = (f32[128,256]{1,0:T(8,128)S(1)}, f32[128,256]{1,0:T(8,128)S(1)}, u32[]{:S(2)}, u32[]{:S(2)}) collective-permute-start(f32[128,256]{1,0:T(8,128)S(1)} %pad_maximum_fusion.4), channel_id=1, source_target_pairs={{0,1},{1,0},{2,3},{3,2},{4,5},{5,4},{6,7},{7,6},{8,9},{9,8},{10,11... | collective-permute-start | bytes 393224 | tf_op jit(solution)/shard_map/ppermute | solution.py:200
where the time goes:
time: 60.9 us; the launch traced here: 60.7 us
  starting transfers between devices  28.4 us (47%)
  waiting for transfers between devices  22.6 us (37%)
  Pallas kernels  6.11 us (10%)
  local copies, waits for them, and re-layouts  1.95 us (3%)
  between operations  1.5 us (2%)
    ppermute x25, starting transfers between devices, exchange(): return lax.ppermute(value, axis, [(i, i ^ shift) for i in range(size)])  28.4 us
    ppermute x25, waiting for transfers between devices, exchange(): return lax.ppermute(value, axis, [(i, i ^ shift) for i in range(size)])  22.6 us
    pallas_call x7, Pallas kernels, call(): pl.pallas_call(kernel, out_shape=outs, in_specs=[pl.BlockSpec(memory_spac...  6.11 us
    unnamed x12, local copies, waits for them, and re-layouts  1.9 us
  transfers between devices with their start and end apart: 25, of which 14 were waited for; matrix products, arithmetic and copies ran while one was open for 0% of the time, Pallas kernels for 4%

commit v1 on v0

--- a/solution.py
+++ b/solution.py
@@ -17,6 +17,14 @@
 NN = (((1,), (0,)), ((), ()))
 TN = (((0,), (0,)), ((), ()))
 NT = (((1,), (1,)), ((), ()))
+
+
+def halvings(count):
+    return [2**k for k in range(count.bit_length() - 1)]
+
+
+def flipped(index, count):
+    return sum(count // (2 * k) for k in halvings(count) if index & k)
 
 
 def split(x):
@@ -140,7 +148,7 @@
     chunk = buffer.shape[0] // members
     for s in range(members):
         target = send_ref if s % 2 else keep_ref
-        start = (s // 2) * chunk
+        start = flipped(s // 2, members // 2) * chunk
         target[start : start + chunk, :] = buffer[rows_at(lax.bitwise_xor(me, s), chunk), :]
     sums = jnp.sum(grad, axis=0, keepdims=True)
     part_ref[...] = jnp.broadcast_to(sums, part_ref.shape)
@@ -189,7 +197,7 @@
     terms = []
     for s in range(members):
         piece = partner_ref if s % 2 else own_ref
-        start = (s // 2) * step
+        start = flipped(s // 2, members // 2) * step
         weight_ref[rows_at(lax.bitwise_xor(me, s), chunk), :] = piece[start : start + chunk, :]
         terms.append(piece[start + chunk : start + chunk + 1, :])
     bias_ref[...] = tree_sum(terms)
@@ -276,17 +284,18 @@
         flops=6 * nodes * width * width,
     )
     total = keep + exchange(send, "row", 1)
-    size = width // members
-    owned = [total[p * size : (p + 1) * size] for p in range(pairs)]
-    owned[1:] = [exchange(owned[p], "row", 2 * p) for p in range(1, pairs)]
-    chunk = jnp.concatenate([tree_sum(owned), bias_part], axis=0)
-    summed = tree_sum([chunk] + [exchange(chunk, "rep", s) for s in range(1, groups)])
-    chunks = [summed]
-    chunks += [exchange(summed, "row", 2 * p) for p in range(1, pairs)]
-    own = jnp.concatenate(chunks, axis=0)
-    partner = exchange(own, "row", 1)
+    for step in halvings(pairs):
+        half = total.shape[0] // 2
+        total = total[:half] + exchange(total[half:], "row", 2 * step)
+    total = jnp.concatenate([total, bias_part], axis=0)
+    for step in halvings(groups):
+        total = total + exchange(total, "rep", step)
+    for step in reversed(halvings(pairs)):
+        other = exchange(total, "row", 2 * step)
+        total = jnp.concatenate([total, other], axis=0)
+    partner = exchange(total, "row", 1)
     weight_grad, bias_grad = call(
-        functools.partial(finish, members), [shape(width), shape(1)], [own, partner]
+        functools.partial(finish, members), [shape(width), shape(1)], [total, partner]
     )
     return (activated, feat_grad, weight_grad, bias_grad[0])
 

time: 60.9 us -> 63.6 us (1.044)
  waiting for transfers between devices: 22.6 us -> 30.6 us
  starting transfers between devices: 28.4 us -> 23.2 us
    ppermute x25 -> x22, waiting for transfers between devices: 22.6 us -> 30.6 us  [exchange(): return lax.ppermute(value, axis, [(i, i ^ shift) for i in range(size)])]
    ppermute x25 -> x22, starting transfers between devices: 28.4 us -> 23.2 us  [exchange(): return lax.ppermute(value, axis, [(i, i ^ shift) for i in range(size)])]
  transfers between devices with their start and end apart: 25 -> 22, of which waited for: 14 -> 13; matrix products, arithmetic and copies ran while one was open for 0% -> 0% of each run, Pallas kernels for 4% -> 4%
where the time goes in v1:
time: 63.6 us; the launch traced here: 63.4 us
  waiting for transfers between devices  30.6 us (48%)
  starting transfers between devices  23.2 us (36%)
  Pallas kernels  6.11 us (10%)
  local copies, waits for them, and re-layouts  1.95 us (3%)
  between operations  1.51 us (2%)
    ppermute x22, waiting for transfers between devices, exchange(): return lax.ppermute(value, axis, [(i, i ^ shift) for i in range(size)])  30.6 us
    ppermute x22, starting transfers between devices, exchange(): return lax.ppermute(value, axis, [(i, i ^ shift) for i in range(size)])  23.2 us
    pallas_call x7, Pallas kernels, call(): pl.pallas_call(kernel, out_shape=outs, in_specs=[pl.BlockSpec(memory_spac...  6.11 us
    unnamed x12, local copies, waits for them, and re-layouts  1.9 us
  transfers between devices with their start and end apart: 22, of which 13 were waited for; matrix products, arithmetic and copies ran while one was open for 0% of the time, Pallas kernels for 4%

profile of v1, /device:TPU:0, one launch (start us, length us, event | category | flops | bytes accessed | tf_op | source)
XLA Modules:
  0.0 63.4 jit_solution(14053001411483954653)
XLA Ops:
  0.6 1.2 %shard_map.121 = (f32[64,256]{1,0:T(8,128)S(1)}, f32[64,256]{1,0:T(8,128)S(1)}, f32[64,256]{1,0:T(8,128)S(1)}, f32[64,256]{1,0:T(8,128)S(1)}, s32[1,256]{1,0:T(1,128)S(1)}) custom-call(s32[1,2048]{1,0:T(1,128)} %list_hbm.1, f32[128,256]{1,0:T(8,128)} %feat_hbm.1), custom_call_target="tpu_custom_call" | custom-call | bytes 402432 | tf_op jit(solution)/shard_map/pallas_call | solution.py:47
  1.8 3.1 %collective-permute-start = (f32[64,256]{1,0:T(8,128)S(1)}, f32[64,256]{1,0:T(8,128)S(1)}, u32[]{:S(2)}, u32[]{:S(2)}) collective-permute-start(f32[64,256]{1,0:T(8,128)S(1)} %get-tuple-element.32), channel_id=1, source_target_pairs={{0,2},{1,3},{2,0},{3,1},{4,6},{5,7},{6,4},{7,5},{8,10},{9,11},{10,... | collective-permute-start | bytes 196616 | tf_op jit(solution)/shard_map/ppermute | solution.py:208
  5.0 2.6 %collective-permute-start.1 = (f32[64,256]{1,0:T(8,128)S(1)}, f32[64,256]{1,0:T(8,128)S(1)}, u32[]{:S(2)}, u32[]{:S(2)}) collective-permute-start(f32[64,256]{1,0:T(8,128)S(1)} %get-tuple-element.33), channel_id=1, source_target_pairs={{0,4},{1,5},{2,6},{3,7},{4,0},{5,1},{6,2},{7,3},{8,12},{9,13},{10,... | collective-permute-start | bytes 196616 | tf_op jit(solution)/shard_map/ppermute | solution.py:208
  7.5 0.0 collective-permute-start.2
  7.6 0.0 collective-permute-done
  7.6 4.6 %collective-permute-done.1 = f32[64,256]{1,0:T(8,128)S(1)} collective-permute-done((f32[64,256]{1,0:T(8,128)S(1)}, f32[64,256]{1,0:T(8,128)S(1)}, u32[]{:S(2)}, u32[]{:S(2)}) %collective-permute-start.1) | collective-permute-done | bytes 65568 | tf_op jit(solution)/shard_map/ppermute | solution.py:208
  12.2 1.4 %collective-permute-done.2 = f32[64,256]{1,0:T(8,128)S(1)} collective-permute-done((f32[64,256]{1,0:T(8,128)S(1)}, f32[64,256]{1,0:T(8,128)S(1)}, u32[]{:S(2)}, u32[]{:S(2)}) %collective-permute-start.2) | collective-permute-done | bytes 65568 | tf_op jit(solution)/shard_map/ppermute | solution.py:208
  13.6 0.0 copy-start.5
  13.6 0.1 collective-permute-start.3
  14.4 0.0 copy-start.3
  14.4 0.0 copy-start.4
  14.4 0.0 copy-done.5
  14.4 0.6 %copy-done.3 = f32[256]{0:T(256)S(1)} copy-done((f32[256]{0:T(256)S(1)}, f32[256]{0:T(256)}, u32[]{:S(2)}) %copy-start.3) | copy-done | bytes 1048
  15.1 0.0 copy-done.4
  15.1 0.0 copy-start
  15.1 1.2 %copy-done = f32[1,1,64,4096]{3,2,1,0:T(8,128)S(1)} copy-done((f32[1,1,64,4096]{3,2,1,0:T(8,128)S(1)}, f32[1,1,64,4096]{3,2,1,0:T(8,128)}, u32[]{:S(2)}) %copy-start) | copy-done | bytes 1048600
  16.3 0.6 shard_map.120
  16.9 0.0 collective-permute-done.3.partner_ref
  16.9 0.0 copy-start.1
  16.9 0.0 copy-start.2
  17.0 0.8 %shard_map.122 = (f32[128,256]{1,0:T(8,128)S(1)}, f32[128,256]{1,0:T(8,128)S(1)}, f32[128,256]{1,0:T(8,128)S(1)}, f32[128,256]{1,0:T(8,128)S(1)}) custom-call(bf16[512,256]{1,0:T(8,128)(2,1)S(1)} %get-tuple-element.29.high_ref, bf16[512,256]{1,0:T(8,128)(2,1)S(1)} %get-tuple-element.30.low_ref, f32[128,256]{1,0:T(8,128)S(1)} %pad_maximum_fusion.1.own_ref, ...), custom_call_target="tpu_custom_call" | custom-call | flops 201326592 | bytes 1310720 | tf_op jit(solution)/shard_map/pallas_call | solution.py:47
  17.8 1.6 %collective-permute-start.4 = (f32[128,256]{1,0:T(8,128)S(1)}, f32[128,256]{1,0:T(8,128)S(1)}, u32[]{:S(2)}, u32[]{:S(2)}) collective-permute-start(f32[128,256]{1,0:T(8,128)S(1)} %get-tuple-element.36), channel_id=1, source_target_pairs={{0,8},{8,0},{16,24},{24,16},{1,9},{9,1},{17,25},{25,17},{2,10},{10... | collective-permute-start | bytes 393224 | tf_op jit(solution)/shard_map/ppermute | solution.py:208
  19.3 1.5 %collective-permute-start.5 = (f32[128,256]{1,0:T(8,128)S(1)}, f32[128,256]{1,0:T(8,128)S(1)}, u32[]{:S(2)}, u32[]{:S(2)}) collective-permute-start(f32[128,256]{1,0:T(8,128)S(1)} %get-tuple-element.37), channel_id=1, source_target_pairs={{0,16},{8,24},{16,0},{24,8},{1,17},{9,25},{17,1},{25,9},{2,18},{10... | collective-permute-start | bytes 393224 | tf_op jit(solution)/shard_map/ppermute | solution.py:208
  20.8 0.5 collective-permute-start.6
  21.3 2.8 %collective-permute-done.4.refs_1_ = f32[128,256]{1,0:T(8,128)S(1)} collective-permute-done((f32[128,256]{1,0:T(8,128)S(1)}, f32[128,256]{1,0:T(8,128)S(1)}, u32[]{:S(2)}, u32[]{:S(2)}) %collective-permute-start.4) | collective-permute-done | bytes 131104 | tf_op jit(solution)/shard_map/ppermute | solution.py:208
  24.1 3.6 %collective-permute-done.5.refs_2_ = f32[128,256]{1,0:T(8,128)S(1)} collective-permute-done((f32[128,256]{1,0:T(8,128)S(1)}, f32[128,256]{1,0:T(8,128)S(1)}, u32[]{:S(2)}, u32[]{:S(2)}) %collective-permute-start.5) | collective-permute-done | bytes 131104 | tf_op jit(solution)/shard_map/ppermute | solution.py:208
  27.8 0.0 collective-permute-done.6.refs_3_
  27.8 0.0 copy-done.1
  27.8 0.0 copy-done.2
  27.8 0.9 %shard_map.123 = (f32[128,256]{1,0:T(8,128)}, f32[128,256]{1,0:T(8,128)S(1)}, f32[128,256]{1,0:T(8,128)S(1)}, f32[128,256]{1,0:T(8,128)S(1)}, f32[8,256]{1,0:T(8,128)S(1)}) custom-call(f32[128,256]{1,0:T(8,128)S(1)} %get-tuple-element.35.refs_0_, f32[128,256]{1,0:T(8,128)S(1)} %collective-permute-done.4.refs_1_, ...), custom_call_target="tpu_custom_call" | custom-call | flops 100663296 | bytes 1451008 | tf_op jit(solution)/shard_map/pallas_call | solution.py:47
  28.7 0.0 collective-permute-start.14
  28.7 1.3 %collective-permute-done.14 = f32[128,256]{1,0:T(8,128)S(1)} collective-permute-done((f32[128,256]{1,0:T(8,128)S(1)}, f32[128,256]{1,0:T(8,128)S(1)}, u32[]{:S(2)}, u32[]{:S(2)}) %collective-permute-start.14) | collective-permute-done | bytes 131104 | tf_op jit(solution)/shard_map/ppermute | solution.py:208
  30.1 0.1 collective-permute-start.15
  30.2 1.6 %collective-permute-start.9 = (f32[128,256]{1,0:T(8,128)S(1)}, f32[128,256]{1,0:T(8,128)S(1)}, u32[]{:S(2)}, u32[]{:S(2)}) collective-permute-start(f32[128,256]{1,0:T(8,128)S(1)} %get-tuple-element.44.refs_0_), channel_id=1, source_target_pairs={{0,24},{8,16},{16,8},{24,0},{1,25},{9,17},{17,9},{25,1},{2,26},{10... | collective-permute-start | bytes 393224 | tf_op jit(solution)/shard_map/ppermute | solution.py:208
  31.7 1.2 %collective-permute-start.8 = (f32[128,256]{1,0:T(8,128)S(1)}, f32[128,256]{1,0:T(8,128)S(1)}, u32[]{:S(2)}, u32[]{:S(2)}) collective-permute-start(f32[128,256]{1,0:T(8,128)S(1)} %get-tuple-element.44.refs_0_), channel_id=1, source_target_pairs={{0,16},{8,24},{16,0},{24,8},{1,17},{9,25},{17,1},{25,9},{2,18},{10... | collective-permute-start | bytes 393224 | tf_op jit(solution)/shard_map/ppermute | solution.py:208
  32.9 0.8 %collective-permute-start.7 = (f32[128,256]{1,0:T(8,128)S(1)}, f32[128,256]{1,0:T(8,128)S(1)}, u32[]{:S(2)}, u32[]{:S(2)}) collective-permute-start(f32[128,256]{1,0:T(8,128)S(1)} %get-tuple-element.44.refs_0_), channel_id=1, source_target_pairs={{0,8},{8,0},{16,24},{24,16},{1,9},{9,1},{17,25},{25,17},{2,10},{10... | collective-permute-start | bytes 393224 | tf_op jit(solution)/shard_map/ppermute | solution.py:208
  33.7 0.7 %collective-permute-done.15 = f32[64,256]{1,0:T(8,128)S(1)} collective-permute-done((f32[64,256]{1,0:T(8,128)S(1)}, f32[64,256]{1,0:T(8,128)S(1)}, u32[]{:S(2)}, u32[]{:S(2)}) %collective-permute-start.15) | collective-permute-done | bytes 65568 | tf_op jit(solution)/shard_map/ppermute | solution.py:208
  34.5 1.7 %collective-permute-start.16 = (f32[32,256]{1,0:T(8,128)S(1)}, f32[32,256]{1,0:T(8,128)S(1)}, u32[]{:S(2)}, u32[]{:S(2)}) collective-permute-start(f32[32,256]{1,0:T(8,128)S(1)} %slice.95), channel_id=1, source_target_pairs={{0,4},{1,5},{2,6},{3,7},{4,0},{5,1},{6,2},{7,3},{8,12},{9,13},{10,... | collective-permute-start | bytes 98312 | tf_op jit(solution)/shard_map/ppermute | solution.py:208
  36.1 1.4 %collective-permute-done.9.refs_3_ = f32[128,256]{1,0:T(8,128)S(1)} collective-permute-done((f32[128,256]{1,0:T(8,128)S(1)}, f32[128,256]{1,0:T(8,128)S(1)}, u32[]{:S(2)}, u32[]{:S(2)}) %collective-permute-start.9) | collective-permute-done | bytes 131104 | tf_op jit(solution)/shard_map/ppermute | solution.py:208
  37.5 2.0 %collective-permute-done.8.refs_2_ = f32[128,256]{1,0:T(8,128)S(1)} collective-permute-done((f32[128,256]{1,0:T(8,128)S(1)}, f32[128,256]{1,0:T(8,128)S(1)}, u32[]{:S(2)}, u32[]{:S(2)}) %collective-permute-start.8) | collective-permute-done | bytes 131104 | tf_op jit(solution)/shard_map/ppermute | solution.py:208
  39.5 0.1 collective-permute-done.7.refs_1_
  39.6 0.7 %shard_map.124 = (f32[64,256]{1,0:T(8,128)S(1)}, f32[64,256]{1,0:T(8,128)S(1)}, f32[64,256]{1,0:T(8,128)S(1)}, f32[64,256]{1,0:T(8,128)S(1)}) custom-call(bf16[256,512]{1,0:T(8,128)(2,1)S(1)} %get-tuple-element.42.high_ref, bf16[256,512]{1,0:T(8,128)(2,1)S(1)} %get-tuple-element.43.low_ref, f32[128,256]{1,0:T(8,128)S(1)} %get-tuple-element.44.refs_0_, ...), custom_call_target="tpu_custom_call" | custom-call | flops 201326592 | bytes 1310720 | tf_op jit(solution)/shard_map/pallas_call | solution.py:47
  40.3 0.0 collective-permute-done.16
  40.4 1.2 %collective-permute-start.17 = (f32[40,256]{1,0:T(8,128)S(1)}, f32[40,256]{1,0:T(8,128)S(1)}, u32[]{:S(2)}, u32[]{:S(2)}) collective-permute-start(f32[40,256]{1,0:T(8,128)S(1)} %pad_maximum_fusion.6), channel_id=1, source_target_pairs={{0,8},{8,0},{16,24},{24,16},{1,9},{9,1},{17,25},{25,17},{2,10},{10... | collective-permute-start | bytes 122888 | tf_op jit(solution)/shard_map/ppermute | solution.py:208
  41.6 1.7 %collective-permute-start.10 = (f32[64,256]{1,0:T(8,128)S(1)}, f32[64,256]{1,0:T(8,128)S(1)}, u32[]{:S(2)}, u32[]{:S(2)}) collective-permute-start(f32[64,256]{1,0:T(8,128)S(1)} %get-tuple-element.46), channel_id=1, source_target_pairs={{0,2},{1,3},{2,0},{3,1},{4,6},{5,7},{6,4},{7,5},{8,10},{9,11},{10,... | collective-permute-start | bytes 196616 | tf_op jit(solution)/shard_map/ppermute | solution.py:208
  43.2 1.6 %collective-permute-start.11 = (f32[64,256]{1,0:T(8,128)S(1)}, f32[64,256]{1,0:T(8,128)S(1)}, u32[]{:S(2)}, u32[]{:S(2)}) collective-permute-start(f32[64,256]{1,0:T(8,128)S(1)} %get-tuple-element.47), channel_id=1, source_target_pairs={{0,4},{1,5},{2,6},{3,7},{4,0},{5,1},{6,2},{7,3},{8,12},{9,13},{10,... | collective-permute-start | bytes 196616 | tf_op jit(solution)/shard_map/ppermute | solution.py:208
  44.8 1.1 %collective-permute-start.12 = (f32[64,256]{1,0:T(8,128)S(1)}, f32[64,256]{1,0:T(8,128)S(1)}, u32[]{:S(2)}, u32[]{:S(2)}) collective-permute-start(f32[64,256]{1,0:T(8,128)S(1)} %get-tuple-element.48), channel_id=1, source_target_pairs={{0,6},{1,7},{2,4},{3,5},{4,2},{5,3},{6,0},{7,1},{8,14},{9,15},{10,... | collective-permute-start | bytes 196616 | tf_op jit(solution)/shard_map/ppermute | solution.py:208
  46.0 0.0 collective-permute-done.17
  46.0 0.9 %collective-permute-start.18 = (f32[40,256]{1,0:T(8,128)S(1)}, f32[40,256]{1,0:T(8,128)S(1)}, u32[]{:S(2)}, u32[]{:S(2)}) collective-permute-start(f32[40,256]{1,0:T(8,128)S(1)} %fusion), channel_id=1, source_target_pairs={{0,16},{8,24},{16,0},{24,8},{1,17},{9,25},{17,1},{25,9},{2,18},{10... | collective-permute-start | bytes 122888 | tf_op jit(solution)/shard_map/ppermute | solution.py:208
  46.9 0.0 collective-permute-done.10
  46.9 3.2 %collective-permute-done.18 = f32[40,256]{1,0:T(8,128)S(1)} collective-permute-done((f32[40,256]{1,0:T(8,128)S(1)}, f32[40,256]{1,0:T(8,128)S(1)}, u32[]{:S(2)}, u32[]{:S(2)}) %collective-permute-start.18) | collective-permute-done | bytes 40992 | tf_op jit(solution)/shard_map/ppermute | solution.py:208
  50.0 1.1 %collective-permute-start.19 = (f32[40,256]{1,0:T(8,128)S(1)}, f32[40,256]{1,0:T(8,128)S(1)}, u32[]{:S(2)}, u32[]{:S(2)}) collective-permute-start(f32[40,256]{1,0:T(8,128)S(1)} %add.19), channel_id=1, source_target_pairs={{0,4},{1,5},{2,6},{3,7},{4,0},{5,1},{6,2},{7,3},{8,12},{9,13},{10,... | collective-permute-start | bytes 122888 | tf_op jit(solution)/shard_map/ppermute | solution.py:208
  51.1 0.0 collective-permute-done.11
  51.2 4.3 %collective-permute-done.19 = f32[40,256]{1,0:T(8,128)S(1)} collective-permute-done((f32[40,256]{1,0:T(8,128)S(1)}, f32[40,256]{1,0:T(8,128)S(1)}, u32[]{:S(2)}, u32[]{:S(2)}) %collective-permute-start.19) | collective-permute-done | bytes 40992 | tf_op jit(solution)/shard_map/ppermute | solution.py:208
  55.5 0.3 collective-permute-start.20
  55.8 0.0 collective-permute-done.12
  55.8 4.1 %collective-permute-done.20 = f32[80,256]{1,0:T(8,128)S(1)} collective-permute-done((f32[80,256]{1,0:T(8,128)S(1)}, f32[80,256]{1,0:T(8,128)S(1)}, u32[]{:S(2)}, u32[]{:S(2)}) %collective-permute-start.20) | collective-permute-done | bytes 81952 | tf_op jit(solution)/shard_map/ppermute | solution.py:208
  60.0 0.1 collective-permute-start.21
  60.0 0.6 collective-permute-start.13
  60.6 1.0 %collective-permute-done.13.partner_ref = f32[128,256]{1,0:T(8,128)S(1)} collective-permute-done((f32[128,256]{1,0:T(8,128)S(1)}, f32[128,256]{1,0:T(8,128)S(1)}, u32[]{:S(2)}, u32[]{:S(2)}) %collective-permute-start.13) | collective-permute-done | bytes 131104 | tf_op jit(solution)/shard_map/ppermute | solution.py:208
  61.6 1.1 %shard_map.125 = f32[128,256]{1,0:T(8,128)} custom-call(s32[1,256]{1,0:T(1,128)S(1)} %get-tuple-element.41.wanted_ref, f32[256,256]{1,0:T(8,128)S(1)} %copy-done.1, f32[128,256]{1,0:T(8,128)S(1)} %pad_maximum_fusion.3.own_ref, f32[128,256]{1,0:T(8,128)S(1)} %collective-permute-done.13.partner_ref), custom_call_target="tpu_custom_call" | custom-call | flops 50331648 | bytes 656384 | tf_op jit(solution)/shard_map/pallas_call | solution.py:47
  62.7 0.0 collective-permute-done.21.partner_ref
  62.7 0.7 %shard_map.126 = (f32[256,256]{1,0:T(8,128)}, f32[1,256]{1,0:T(1,128)}) custom-call(f32[160,256]{1,0:T(8,128)S(1)} %pad_maximum_fusion.own_ref, f32[160,256]{1,0:T(8,128)S(1)} %collective-permute-done.21.partner_ref), custom_call_target="tpu_custom_call" | custom-call | bytes 590848 | tf_op jit(solution)/shard_map/pallas_call | solution.py:47
  (22 shorter events, 0.2 us)
Async XLA Ops:
  1.8 5.7 %collective-permute-start = (f32[64,256]{1,0:T(8,128)S(1)}, f32[64,256]{1,0:T(8,128)S(1)}, u32[]{:S(2)}, u32[]{:S(2)}) collective-permute-start(f32[64,256]{1,0:T(8,128)S(1)} %get-tuple-element.32), channel_id=1, source_target_pairs={{0,2},{1,3},{2,0},{3,1},{4,6},{5,7},{6,4},{7,5},{8,10},{9,11},{10,... | collective-permute-start | bytes 196616 | tf_op jit(solution)/shard_map/ppermute | solution.py:208
  5.0 7.3 %collective-permute-start.1 = (f32[64,256]{1,0:T(8,128)S(1)}, f32[64,256]{1,0:T(8,128)S(1)}, u32[]{:S(2)}, u32[]{:S(2)}) collective-permute-start(f32[64,256]{1,0:T(8,128)S(1)} %get-tuple-element.33), channel_id=1, source_target_pairs={{0,4},{1,5},{2,6},{3,7},{4,0},{5,1},{6,2},{7,3},{8,12},{9,13},{10,... | collective-permute-start | bytes 196616 | tf_op jit(solution)/shard_map/ppermute | solution.py:208
  7.5 6.1 %collective-permute-start.2 = (f32[64,256]{1,0:T(8,128)S(1)}, f32[64,256]{1,0:T(8,128)S(1)}, u32[]{:S(2)}, u32[]{:S(2)}) collective-permute-start(f32[64,256]{1,0:T(8,128)S(1)} %get-tuple-element.34), channel_id=1, source_target_pairs={{0,6},{1,7},{2,4},{3,5},{4,2},{5,3},{6,0},{7,1},{8,14},{9,15},{10,... | collective-permute-start | bytes 196616 | tf_op jit(solution)/shard_map/ppermute | solution.py:208
  13.6 0.8 %copy-start.5 = (s32[1,1,64]{2,1,0:T(1,128)S(1)}, s32[1,1,64]{2,1,0:T(1,128)}, u32[]{:S(2)}) copy-start(s32[1,1,64]{2,1,0:T(1,128)} %param.15) | copy-start | bytes 772
  13.6 3.3 %collective-permute-start.3 = (f32[128,256]{1,0:T(8,128)S(1)}, f32[128,256]{1,0:T(8,128)S(1)}, u32[]{:S(2)}, u32[]{:S(2)}) collective-permute-start(f32[128,256]{1,0:T(8,128)S(1)} %pad_maximum_fusion.2), channel_id=1, source_target_pairs={{0,1},{1,0},{2,3},{3,2},{4,5},{5,4},{6,7},{7,6},{8,9},{9,8},{10,11... | collective-permute-start | bytes 393224 | tf_op jit(solution)/shard_map/ppermute | solution.py:208
  14.4 0.7 %copy-start.3 = (f32[256]{0:T(256)S(1)}, f32[256]{0:T(256)}, u32[]{:S(2)}) copy-start(f32[256]{0:T(256)} %param.11) | copy-start | bytes 3076
  14.4 0.7 %copy-start.4 = (s32[1,1,64]{2,1,0:T(1,128)S(1)}, s32[1,1,64]{2,1,0:T(1,128)}, u32[]{:S(2)}) copy-start(s32[1,1,64]{2,1,0:T(1,128)} %param.14) | copy-start | bytes 772
  15.1 1.2 %copy-start = (f32[1,1,64,4096]{3,2,1,0:T(8,128)S(1)}, f32[1,1,64,4096]{3,2,1,0:T(8,128)}, u32[]{:S(2)}) copy-start(f32[1,1,64,4096]{3,2,1,0:T(8,128)} %param.13) | copy-start | bytes 3145732
  16.9 10.8 %copy-start.1 = (f32[256,256]{1,0:T(8,128)S(1)}, f32[256,256]{1,0:T(8,128)}, u32[]{:S(2)}) copy-start(f32[256,256]{1,0:T(8,128)} %weight_ref.1) | copy-start | bytes 786436
  16.9 10.8 %copy-start.2 = (f32[128,256]{1,0:T(8,128)S(1)}, f32[128,256]{1,0:T(8,128)}, u32[]{:S(2)}) copy-start(f32[128,256]{1,0:T(8,128)} %refs_6_.1) | copy-start | bytes 393220
  17.8 6.4 %collective-permute-start.4 = (f32[128,256]{1,0:T(8,128)S(1)}, f32[128,256]{1,0:T(8,128)S(1)}, u32[]{:S(2)}, u32[]{:S(2)}) collective-permute-start(f32[128,256]{1,0:T(8,128)S(1)} %get-tuple-element.36), channel_id=1, source_target_pairs={{0,8},{8,0},{16,24},{24,16},{1,9},{9,1},{17,25},{25,17},{2,10},{10... | collective-permute-start | bytes 393224 | tf_op jit(solution)/shard_map/ppermute | solution.py:208
  19.3 8.4 %collective-permute-start.5 = (f32[128,256]{1,0:T(8,128)S(1)}, f32[128,256]{1,0:T(8,128)S(1)}, u32[]{:S(2)}, u32[]{:S(2)}) collective-permute-start(f32[128,256]{1,0:T(8,128)S(1)} %get-tuple-element.37), channel_id=1, source_target_pairs={{0,16},{8,24},{16,0},{24,8},{1,17},{9,25},{17,1},{25,9},{2,18},{10... | collective-permute-start | bytes 393224 | tf_op jit(solution)/shard_map/ppermute | solution.py:208
  20.8 6.9 %collective-permute-start.6 = (f32[128,256]{1,0:T(8,128)S(1)}, f32[128,256]{1,0:T(8,128)S(1)}, u32[]{:S(2)}, u32[]{:S(2)}) collective-permute-start(f32[128,256]{1,0:T(8,128)S(1)} %get-tuple-element.38), channel_id=1, source_target_pairs={{0,24},{8,16},{16,8},{24,0},{1,25},{9,17},{17,9},{25,1},{2,26},{10... | collective-permute-start | bytes 393224 | tf_op jit(solution)/shard_map/ppermute | solution.py:208
  28.7 1.3 %collective-permute-start.14 = (f32[128,256]{1,0:T(8,128)S(1)}, f32[128,256]{1,0:T(8,128)S(1)}, u32[]{:S(2)}, u32[]{:S(2)}) collective-permute-start(f32[128,256]{1,0:T(8,128)S(1)} %get-tuple-element.50), channel_id=1, source_target_pairs={{0,1},{1,0},{2,3},{3,2},{4,5},{5,4},{6,7},{7,6},{8,9},{9,8},{10,11... | collective-permute-start | bytes 393224 | tf_op jit(solution)/shard_map/ppermute | solution.py:208
  30.1 4.3 %collective-permute-start.15 = (f32[64,256]{1,0:T(8,128)S(1)}, f32[64,256]{1,0:T(8,128)S(1)}, u32[]{:S(2)}, u32[]{:S(2)}) collective-permute-start(f32[64,256]{1,0:T(8,128)S(1)} %slice.93), channel_id=1, source_target_pairs={{0,2},{1,3},{2,0},{3,1},{4,6},{5,7},{6,4},{7,5},{8,10},{9,11},{10,... | collective-permute-start | bytes 196616 | tf_op jit(solution)/shard_map/ppermute | solution.py:208
  30.2 7.4 %collective-permute-start.9 = (f32[128,256]{1,0:T(8,128)S(1)}, f32[128,256]{1,0:T(8,128)S(1)}, u32[]{:S(2)}, u32[]{:S(2)}) collective-permute-start(f32[128,256]{1,0:T(8,128)S(1)} %get-tuple-element.44.refs_0_), channel_id=1, source_target_pairs={{0,24},{8,16},{16,8},{24,0},{1,25},{9,17},{17,9},{25,1},{2,26},{10... | collective-permute-start | bytes 393224 | tf_op jit(solution)/shard_map/ppermute | solution.py:208
  31.7 7.8 %collective-permute-start.8 = (f32[128,256]{1,0:T(8,128)S(1)}, f32[128,256]{1,0:T(8,128)S(1)}, u32[]{:S(2)}, u32[]{:S(2)}) collective-permute-start(f32[128,256]{1,0:T(8,128)S(1)} %get-tuple-element.44.refs_0_), channel_id=1, source_target_pairs={{0,16},{8,24},{16,0},{24,8},{1,17},{9,25},{17,1},{25,9},{2,18},{10... | collective-permute-start | bytes 393224 | tf_op jit(solution)/shard_map/ppermute | solution.py:208
  32.9 6.7 %collective-permute-start.7 = (f32[128,256]{1,0:T(8,128)S(1)}, f32[128,256]{1,0:T(8,128)S(1)}, u32[]{:S(2)}, u32[]{:S(2)}) collective-permute-start(f32[128,256]{1,0:T(8,128)S(1)} %get-tuple-element.44.refs_0_), channel_id=1, source_target_pairs={{0,8},{8,0},{16,24},{24,16},{1,9},{9,1},{17,25},{25,17},{2,10},{10... | collective-permute-start | bytes 393224 | tf_op jit(solution)/shard_map/ppermute | solution.py:208
  34.5 5.9 %collective-permute-start.16 = (f32[32,256]{1,0:T(8,128)S(1)}, f32[32,256]{1,0:T(8,128)S(1)}, u32[]{:S(2)}, u32[]{:S(2)}) collective-permute-start(f32[32,256]{1,0:T(8,128)S(1)} %slice.95), channel_id=1, source_target_pairs={{0,4},{1,5},{2,6},{3,7},{4,0},{5,1},{6,2},{7,3},{8,12},{9,13},{10,... | collective-permute-start | bytes 98312 | tf_op jit(solution)/shard_map/ppermute | solution.py:208
  40.4 5.6 %collective-permute-start.17 = (f32[40,256]{1,0:T(8,128)S(1)}, f32[40,256]{1,0:T(8,128)S(1)}, u32[]{:S(2)}, u32[]{:S(2)}) collective-permute-start(f32[40,256]{1,0:T(8,128)S(1)} %pad_maximum_fusion.6), channel_id=1, source_target_pairs={{0,8},{8,0},{16,24},{24,16},{1,9},{9,1},{17,25},{25,17},{2,10},{10... | collective-permute-start | bytes 122888 | tf_op jit(solution)/shard_map/ppermute | solution.py:208
  41.6 5.3 %collective-permute-start.10 = (f32[64,256]{1,0:T(8,128)S(1)}, f32[64,256]{1,0:T(8,128)S(1)}, u32[]{:S(2)}, u32[]{:S(2)}) collective-permute-start(f32[64,256]{1,0:T(8,128)S(1)} %get-tuple-element.46), channel_id=1, source_target_pairs={{0,2},{1,3},{2,0},{3,1},{4,6},{5,7},{6,4},{7,5},{8,10},{9,11},{10,... | collective-permute-start | bytes 196616 | tf_op jit(solution)/shard_map/ppermute | solution.py:208
  43.2 7.9 %collective-permute-start.11 = (f32[64,256]{1,0:T(8,128)S(1)}, f32[64,256]{1,0:T(8,128)S(1)}, u32[]{:S(2)}, u32[]{:S(2)}) collective-permute-start(f32[64,256]{1,0:T(8,128)S(1)} %get-tuple-element.47), channel_id=1, source_target_pairs={{0,4},{1,5},{2,6},{3,7},{4,0},{5,1},{6,2},{7,3},{8,12},{9,13},{10,... | collective-permute-start | bytes 196616 | tf_op jit(solution)/shard_map/ppermute | solution.py:208
  44.8 11.0 %collective-permute-start.12 = (f32[64,256]{1,0:T(8,128)S(1)}, f32[64,256]{1,0:T(8,128)S(1)}, u32[]{:S(2)}, u32[]{:S(2)}) collective-permute-start(f32[64,256]{1,0:T(8,128)S(1)} %get-tuple-element.48), channel_id=1, source_target_pairs={{0,6},{1,7},{2,4},{3,5},{4,2},{5,3},{6,0},{7,1},{8,14},{9,15},{10,... | collective-permute-start | bytes 196616 | tf_op jit(solution)/shard_map/ppermute | solution.py:208
  46.0 4.1 %collective-permute-start.18 = (f32[40,256]{1,0:T(8,128)S(1)}, f32[40,256]{1,0:T(8,128)S(1)}, u32[]{:S(2)}, u32[]{:S(2)}) collective-permute-start(f32[40,256]{1,0:T(8,128)S(1)} %fusion), channel_id=1, source_target_pairs={{0,16},{8,24},{16,0},{24,8},{1,17},{9,25},{17,1},{25,9},{2,18},{10... | collective-permute-start | bytes 122888 | tf_op jit(solution)/shard_map/ppermute | solution.py:208
  50.0 5.4 %collective-permute-start.19 = (f32[40,256]{1,0:T(8,128)S(1)}, f32[40,256]{1,0:T(8,128)S(1)}, u32[]{:S(2)}, u32[]{:S(2)}) collective-permute-start(f32[40,256]{1,0:T(8,128)S(1)} %add.19), channel_id=1, source_target_pairs={{0,4},{1,5},{2,6},{3,7},{4,0},{5,1},{6,2},{7,3},{8,12},{9,13},{10,... | collective-permute-start | bytes 122888 | tf_op jit(solution)/shard_map/ppermute | solution.py:208
  55.5 4.4 %collective-permute-start.20 = (f32[80,256]{1,0:T(8,128)S(1)}, f32[80,256]{1,0:T(8,128)S(1)}, u32[]{:S(2)}, u32[]{:S(2)}) collective-permute-start(f32[80,256]{1,0:T(8,128)S(1)} %pad_maximum_fusion.5), channel_id=1, source_target_pairs={{0,2},{1,3},{2,0},{3,1},{4,6},{5,7},{6,4},{7,5},{8,10},{9,11},{10,... | collective-permute-start | bytes 245768 | tf_op jit(solution)/shard_map/ppermute | solution.py:208
  60.0 2.8 %collective-permute-start.21 = (f32[160,256]{1,0:T(8,128)S(1)}, f32[160,256]{1,0:T(8,128)S(1)}, u32[]{:S(2)}, u32[]{:S(2)}) collective-permute-start(f32[160,256]{1,0:T(8,128)S(1)} %pad_maximum_fusion.own_ref), channel_id=1, source_target_pairs={{0,1},{1,0},{2,3},{3,2},{4,5},{5,4},{6,7},{7,6},{8,9},{9,8},{10,11... | collective-permute-start | bytes 491528 | tf_op jit(solution)/shard_map/ppermute | solution.py:208
  60.0 1.5 %collective-permute-start.13 = (f32[128,256]{1,0:T(8,128)S(1)}, f32[128,256]{1,0:T(8,128)S(1)}, u32[]{:S(2)}, u32[]{:S(2)}) collective-permute-start(f32[128,256]{1,0:T(8,128)S(1)} %pad_maximum_fusion.4), channel_id=1, source_target_pairs={{0,1},{1,0},{2,3},{3,2},{4,5},{5,4},{6,7},{7,6},{8,9},{9,8},{10,11... | collective-permute-start | bytes 393224 | tf_op jit(solution)/shard_map/ppermute | solution.py:208

commit v2 on v0

--- a/solution.py
+++ b/solution.py
@@ -127,7 +127,7 @@
 
 def activate(groups, members, *refs):
     pieces = refs[:groups]
-    weight_ref, bias_ref, cot_ref, act_ref, grad_ref, keep_ref, send_ref, part_ref, buffer = refs[groups:]
+    weight_ref, bias_ref, cot_ref, act_ref, grad_ref, keep_ref, send_ref, buffer = refs[groups:]
     me = lax.axis_index("row")
     total = tree_sum([piece[...] for piece in pieces])
     total_split = split(total)
@@ -138,12 +138,12 @@
     grad_ref[...] = grad
     buffer[...] = mm3(total_split, split(grad), TN)
     chunk = buffer.shape[0] // members
+    sums = jnp.broadcast_to(jnp.sum(grad, axis=0, keepdims=True), (PAD, grad.shape[1]))
     for s in range(members):
         target = send_ref if s % 2 else keep_ref
-        start = (s // 2) * chunk
+        start = (s // 2) * (chunk + PAD)
         target[start : start + chunk, :] = buffer[rows_at(lax.bitwise_xor(me, s), chunk), :]
-    sums = jnp.sum(grad, axis=0, keepdims=True)
-    part_ref[...] = jnp.broadcast_to(sums, part_ref.shape)
+        target[start + chunk : start + chunk + PAD, :] = sums
 
 
 def spread(groups, pairs, row_blocks, high_ref, low_ref, *refs):
@@ -182,17 +182,14 @@
     out_ref[...] = mm3(split(proj), split(weight_ref[...]), NT)
 
 
-def finish(members, own_ref, partner_ref, weight_ref, bias_ref):
+def finish(members, summed_ref, own_ref, partner_ref, weight_ref, bias_ref):
     me = lax.axis_index("row")
-    step = own_ref.shape[0] // (members // 2)
-    chunk = step - PAD
-    terms = []
+    chunk = weight_ref.shape[0] // members
     for s in range(members):
         piece = partner_ref if s % 2 else own_ref
-        start = (s // 2) * step
+        start = (s // 2) * chunk
         weight_ref[rows_at(lax.bitwise_xor(me, s), chunk), :] = piece[start : start + chunk, :]
-        terms.append(piece[start + chunk : start + chunk + 1, :])
-    bias_ref[...] = tree_sum(terms)
+    bias_ref[...] = summed_ref[chunk : chunk + 1, :]
 
 
 def exchange(value, axis, shift):
@@ -252,9 +249,11 @@
         flops=6 * rows * slots * width,
     )
     parts = [partials[0]] + [exchange(partials[s], "rep", s) for s in range(1, groups)]
-    activated, grad, keep, send, bias_part = call(
+    chunk = width // members
+    padded = pairs * (chunk + PAD)
+    activated, grad, keep, send = call(
         functools.partial(activate, groups, members),
-        [shape(nodes), shape(nodes), shape(width // 2), shape(width // 2), shape(PAD)],
+        [shape(nodes), shape(nodes), shape(padded), shape(padded)],
         parts + [weight, bias_here, cotangent],
         [vmem(width)],
         flops=12 * nodes * width * width,
@@ -276,17 +275,17 @@
         flops=6 * nodes * width * width,
     )
     total = keep + exchange(send, "row", 1)
-    size = width // members
+    size = chunk + PAD
     owned = [total[p * size : (p + 1) * size] for p in range(pairs)]
     owned[1:] = [exchange(owned[p], "row", 2 * p) for p in range(1, pairs)]
-    chunk = jnp.concatenate([tree_sum(owned), bias_part], axis=0)
-    summed = tree_sum([chunk] + [exchange(chunk, "rep", s) for s in range(1, groups)])
-    chunks = [summed]
-    chunks += [exchange(summed, "row", 2 * p) for p in range(1, pairs)]
+    part = tree_sum(owned)
+    summed = tree_sum([part] + [exchange(part, "rep", s) for s in range(1, groups)])
+    done = summed[:chunk]
+    chunks = [done] + [exchange(done, "row", 2 * p) for p in range(1, pairs)]
     own = jnp.concatenate(chunks, axis=0)
     partner = exchange(own, "row", 1)
     weight_grad, bias_grad = call(
-        functools.partial(finish, members), [shape(width), shape(1)], [own, partner]
+        functools.partial(finish, members), [shape(width), shape(1)], [summed, own, partner]
     )
     return (activated, feat_grad, weight_grad, bias_grad[0])
 

time: 60.9 us -> 67.4 us (1.11)
  waiting for transfers between devices: 22.6 us -> 27.7 us
  starting transfers between devices: 28.4 us -> 29.9 us
    ppermute x25, waiting for transfers between devices: 22.6 us -> 27.7 us  [exchange(): return lax.ppermute(value, axis, [(i, i ^ shift) for i in range(size)])]
    ppermute x25, starting transfers between devices: 28.4 us -> 29.9 us  [exchange(): return lax.ppermute(value, axis, [(i, i ^ shift) for i in range(size)])]
  transfers between devices with their start and end apart: 25 -> 25, of which waited for: 14 -> 16; matrix products, arithmetic and copies ran while one was open for 0% -> 0% of each run, Pallas kernels for 4% -> 4%
where the time goes in v2:
time: 67.4 us; the launch traced here: 67.2 us
  starting transfers between devices  29.9 us (44%)
  waiting for transfers between devices  27.7 us (41%)
  Pallas kernels  6.09 us (9%)
  local copies, waits for them, and re-layouts  1.96 us (3%)
  between operations  1.51 us (2%)
    ppermute x25, starting transfers between devices, exchange(): return lax.ppermute(value, axis, [(i, i ^ shift) for i in range(size)])  29.9 us
    ppermute x25, waiting for transfers between devices, exchange(): return lax.ppermute(value, axis, [(i, i ^ shift) for i in range(size)])  27.7 us
    pallas_call x7, Pallas kernels, call(): pl.pallas_call(kernel, out_shape=outs, in_specs=[pl.BlockSpec(memory_spac...  6.09 us
    unnamed x12, local copies, waits for them, and re-layouts  1.9 us
  transfers between devices with their start and end apart: 25, of which 16 were waited for; matrix products, arithmetic and copies ran while one was open for 0% of the time, Pallas kernels for 4%

profile of v2, /device:TPU:0, one launch (start us, length us, event | category | flops | bytes accessed | tf_op | source)
XLA Modules:
  0.0 67.2 jit_solution(4751096436592609231)
XLA Ops:
  0.6 1.2 %shard_map.121 = (f32[64,256]{1,0:T(8,128)S(1)}, f32[64,256]{1,0:T(8,128)S(1)}, f32[64,256]{1,0:T(8,128)S(1)}, f32[64,256]{1,0:T(8,128)S(1)}, s32[1,256]{1,0:T(1,128)S(1)}) custom-call(s32[1,2048]{1,0:T(1,128)} %list_hbm.1, f32[128,256]{1,0:T(8,128)} %feat_hbm.1), custom_call_target="tpu_custom_call" | custom-call | bytes 402432 | tf_op jit(solution)/shard_map/pallas_call | solution.py:39
  1.8 3.1 %collective-permute-start = (f32[64,256]{1,0:T(8,128)S(1)}, f32[64,256]{1,0:T(8,128)S(1)}, u32[]{:S(2)}, u32[]{:S(2)}) collective-permute-start(f32[64,256]{1,0:T(8,128)S(1)} %get-tuple-element.31), channel_id=1, source_target_pairs={{0,2},{1,3},{2,0},{3,1},{4,6},{5,7},{6,4},{7,5},{8,10},{9,11},{10,... | collective-permute-start | bytes 196616 | tf_op jit(solution)/shard_map/ppermute | solution.py:197
  5.0 2.6 %collective-permute-start.1 = (f32[64,256]{1,0:T(8,128)S(1)}, f32[64,256]{1,0:T(8,128)S(1)}, u32[]{:S(2)}, u32[]{:S(2)}) collective-permute-start(f32[64,256]{1,0:T(8,128)S(1)} %get-tuple-element.32), channel_id=1, source_target_pairs={{0,4},{1,5},{2,6},{3,7},{4,0},{5,1},{6,2},{7,3},{8,12},{9,13},{10,... | collective-permute-start | bytes 196616 | tf_op jit(solution)/shard_map/ppermute | solution.py:197
  7.5 0.0 collective-permute-start.2
  7.6 0.0 collective-permute-done
  7.6 4.6 %collective-permute-done.1 = f32[64,256]{1,0:T(8,128)S(1)} collective-permute-done((f32[64,256]{1,0:T(8,128)S(1)}, f32[64,256]{1,0:T(8,128)S(1)}, u32[]{:S(2)}, u32[]{:S(2)}) %collective-permute-start.1) | collective-permute-done | bytes 65568 | tf_op jit(solution)/shard_map/ppermute | solution.py:197
  12.2 1.4 %collective-permute-done.2 = f32[64,256]{1,0:T(8,128)S(1)} collective-permute-done((f32[64,256]{1,0:T(8,128)S(1)}, f32[64,256]{1,0:T(8,128)S(1)}, u32[]{:S(2)}, u32[]{:S(2)}) %collective-permute-start.2) | collective-permute-done | bytes 65568 | tf_op jit(solution)/shard_map/ppermute | solution.py:197
  13.6 0.1 collective-permute-start.3
  14.4 0.0 copy-start.3
  14.4 0.0 copy-start.4
  14.4 0.6 copy-done.3
  15.1 0.0 copy-done.4
  15.1 1.2 %copy-done = f32[1,1,64,4096]{3,2,1,0:T(8,128)S(1)} copy-done((f32[1,1,64,4096]{3,2,1,0:T(8,128)S(1)}, f32[1,1,64,4096]{3,2,1,0:T(8,128)}, u32[]{:S(2)}) %copy-start) | copy-done | bytes 1048600
  16.3 0.6 shard_map.120
  16.9 0.0 collective-permute-done.3.partner_ref
  16.9 0.0 copy-start.1
  16.9 0.0 copy-start.2
  17.0 0.8 %shard_map.122 = (f32[128,256]{1,0:T(8,128)S(1)}, f32[128,256]{1,0:T(8,128)S(1)}, f32[128,256]{1,0:T(8,128)S(1)}, f32[128,256]{1,0:T(8,128)S(1)}) custom-call(bf16[512,256]{1,0:T(8,128)(2,1)S(1)} %get-tuple-element.28.high_ref, bf16[512,256]{1,0:T(8,128)(2,1)S(1)} %get-tuple-element.29.low_ref, f32[128,256]{1,0:T(8,128)S(1)} %pad_maximum_fusion.own_ref, ...), custom_call_target="tpu_custom_call" | custom-call | flops 201326592 | bytes 1310720 | tf_op jit(solution)/shard_map/pallas_call | solution.py:39
  17.8 1.6 %collective-permute-start.4 = (f32[128,256]{1,0:T(8,128)S(1)}, f32[128,256]{1,0:T(8,128)S(1)}, u32[]{:S(2)}, u32[]{:S(2)}) collective-permute-start(f32[128,256]{1,0:T(8,128)S(1)} %get-tuple-element.35), channel_id=1, source_target_pairs={{0,8},{8,0},{16,24},{24,16},{1,9},{9,1},{17,25},{25,17},{2,10},{10... | collective-permute-start | bytes 393224 | tf_op jit(solution)/shard_map/ppermute | solution.py:197
  19.3 1.5 %collective-permute-start.5 = (f32[128,256]{1,0:T(8,128)S(1)}, f32[128,256]{1,0:T(8,128)S(1)}, u32[]{:S(2)}, u32[]{:S(2)}) collective-permute-start(f32[128,256]{1,0:T(8,128)S(1)} %get-tuple-element.36), channel_id=1, source_target_pairs={{0,16},{8,24},{16,0},{24,8},{1,17},{9,25},{17,1},{25,9},{2,18},{10... | collective-permute-start | bytes 393224 | tf_op jit(solution)/shard_map/ppermute | solution.py:197
  20.8 0.5 collective-permute-start.6
  21.3 2.8 %collective-permute-done.4.refs_1_ = f32[128,256]{1,0:T(8,128)S(1)} collective-permute-done((f32[128,256]{1,0:T(8,128)S(1)}, f32[128,256]{1,0:T(8,128)S(1)}, u32[]{:S(2)}, u32[]{:S(2)}) %collective-permute-start.4) | collective-permute-done | bytes 131104 | tf_op jit(solution)/shard_map/ppermute | solution.py:197
  24.1 3.6 %collective-permute-done.5.refs_2_ = f32[128,256]{1,0:T(8,128)S(1)} collective-permute-done((f32[128,256]{1,0:T(8,128)S(1)}, f32[128,256]{1,0:T(8,128)S(1)}, u32[]{:S(2)}, u32[]{:S(2)}) %collective-permute-start.5) | collective-permute-done | bytes 131104 | tf_op jit(solution)/shard_map/ppermute | solution.py:197
  27.7 0.0 collective-permute-done.6.refs_3_
  27.8 0.9 %shard_map.123 = (f32[128,256]{1,0:T(8,128)}, f32[128,256]{1,0:T(8,128)S(1)}, f32[160,256]{1,0:T(8,128)S(1)}, f32[160,256]{1,0:T(8,128)S(1)}) custom-call(f32[128,256]{1,0:T(8,128)S(1)} %get-tuple-element.34.refs_0_, f32[128,256]{1,0:T(8,128)S(1)} %collective-permute-done.4.refs_1_, f32[128,256]{1,0:T(8,128)S(1)} %collective-permute-done.5.refs_2_, ...), custom_call_target="tpu_custom_call" | custom-call | flops 100663296 | bytes 1508352 | tf_op jit(solution)/shard_map/pallas_call | solution.py:39
  28.7 1.5 %collective-permute-start.9 = (f32[128,256]{1,0:T(8,128)S(1)}, f32[128,256]{1,0:T(8,128)S(1)}, u32[]{:S(2)}, u32[]{:S(2)}) collective-permute-start(f32[128,256]{1,0:T(8,128)S(1)} %get-tuple-element.43.refs_0_), channel_id=1, source_target_pairs={{0,24},{8,16},{16,8},{24,0},{1,25},{9,17},{17,9},{25,1},{2,26},{10... | collective-permute-start | bytes 393224 | tf_op jit(solution)/shard_map/ppermute | solution.py:197
  30.2 1.2 %collective-permute-start.8 = (f32[128,256]{1,0:T(8,128)S(1)}, f32[128,256]{1,0:T(8,128)S(1)}, u32[]{:S(2)}, u32[]{:S(2)}) collective-permute-start(f32[128,256]{1,0:T(8,128)S(1)} %get-tuple-element.43.refs_0_), channel_id=1, source_target_pairs={{0,16},{8,24},{16,0},{24,8},{1,17},{9,25},{17,1},{25,9},{2,18},{10... | collective-permute-start | bytes 393224 | tf_op jit(solution)/shard_map/ppermute | solution.py:197
  31.4 0.8 %collective-permute-start.7 = (f32[128,256]{1,0:T(8,128)S(1)}, f32[128,256]{1,0:T(8,128)S(1)}, u32[]{:S(2)}, u32[]{:S(2)}) collective-permute-start(f32[128,256]{1,0:T(8,128)S(1)} %get-tuple-element.43.refs_0_), channel_id=1, source_target_pairs={{0,8},{8,0},{16,24},{24,16},{1,9},{9,1},{17,25},{25,17},{2,10},{10... | collective-permute-start | bytes 393224 | tf_op jit(solution)/shard_map/ppermute | solution.py:197
  32.2 0.0 collective-permute-start.14
  32.2 3.7 %collective-permute-done.9.refs_3_ = f32[128,256]{1,0:T(8,128)S(1)} collective-permute-done((f32[128,256]{1,0:T(8,128)S(1)}, f32[128,256]{1,0:T(8,128)S(1)}, u32[]{:S(2)}, u32[]{:S(2)}) %collective-permute-start.9) | collective-permute-done | bytes 131104 | tf_op jit(solution)/shard_map/ppermute | solution.py:197
  35.9 1.2 %collective-permute-done.8.refs_2_ = f32[128,256]{1,0:T(8,128)S(1)} collective-permute-done((f32[128,256]{1,0:T(8,128)S(1)}, f32[128,256]{1,0:T(8,128)S(1)}, u32[]{:S(2)}, u32[]{:S(2)}) %collective-permute-start.8) | collective-permute-done | bytes 131104 | tf_op jit(solution)/shard_map/ppermute | solution.py:197
  37.1 0.2 collective-permute-done.7.refs_1_
  37.3 0.7 %shard_map.124 = (f32[64,256]{1,0:T(8,128)S(1)}, f32[64,256]{1,0:T(8,128)S(1)}, f32[64,256]{1,0:T(8,128)S(1)}, f32[64,256]{1,0:T(8,128)S(1)}) custom-call(bf16[256,512]{1,0:T(8,128)(2,1)S(1)} %get-tuple-element.41.high_ref, bf16[256,512]{1,0:T(8,128)(2,1)S(1)} %get-tuple-element.42.low_ref, f32[128,256]{1,0:T(8,128)S(1)} %get-tuple-element.43.refs_0_, ...), custom_call_target="tpu_custom_call" | custom-call | flops 201326592 | bytes 1310720 | tf_op jit(solution)/shard_map/pallas_call | solution.py:39
  38.0 0.1 collective-permute-start.10
  38.1 2.4 %collective-permute-start.11 = (f32[64,256]{1,0:T(8,128)S(1)}, f32[64,256]{1,0:T(8,128)S(1)}, u32[]{:S(2)}, u32[]{:S(2)}) collective-permute-start(f32[64,256]{1,0:T(8,128)S(1)} %get-tuple-element.46), channel_id=1, source_target_pairs={{0,4},{1,5},{2,6},{3,7},{4,0},{5,1},{6,2},{7,3},{8,12},{9,13},{10,... | collective-permute-start | bytes 196616 | tf_op jit(solution)/shard_map/ppermute | solution.py:197
  40.4 2.0 %collective-permute-start.12 = (f32[64,256]{1,0:T(8,128)S(1)}, f32[64,256]{1,0:T(8,128)S(1)}, u32[]{:S(2)}, u32[]{:S(2)}) collective-permute-start(f32[64,256]{1,0:T(8,128)S(1)} %get-tuple-element.47), channel_id=1, source_target_pairs={{0,6},{1,7},{2,4},{3,5},{4,2},{5,3},{6,0},{7,1},{8,14},{9,15},{10,... | collective-permute-start | bytes 196616 | tf_op jit(solution)/shard_map/ppermute | solution.py:197
  42.5 0.0 collective-permute-done.14
  42.5 1.9 %collective-permute-start.17 = (f32[40,256]{1,0:T(8,128)S(1)}, f32[40,256]{1,0:T(8,128)S(1)}, u32[]{:S(2)}, u32[]{:S(2)}) collective-permute-start(f32[40,256]{1,0:T(8,128)S(1)} %get-tuple-element.52), channel_id=1, source_target_pairs={{0,6},{1,7},{2,4},{3,5},{4,2},{5,3},{6,0},{7,1},{8,14},{9,15},{10,... | collective-permute-start | bytes 122888 | tf_op jit(solution)/shard_map/ppermute | solution.py:197
  44.4 0.0 collective-permute-start.16
  44.4 0.0 collective-permute-done.10
  44.4 2.6 %collective-permute-start.15 = (f32[40,256]{1,0:T(8,128)S(1)}, f32[40,256]{1,0:T(8,128)S(1)}, u32[]{:S(2)}, u32[]{:S(2)}) collective-permute-start(f32[40,256]{1,0:T(8,128)S(1)} %get-tuple-element.54), channel_id=1, source_target_pairs={{0,2},{1,3},{2,0},{3,1},{4,6},{5,7},{6,4},{7,5},{8,10},{9,11},{10,... | collective-permute-start | bytes 122888 | tf_op jit(solution)/shard_map/ppermute | solution.py:197
  47.0 0.2 collective-permute-done.11
  47.2 1.3 %collective-permute-done.17 = f32[40,256]{1,0:T(8,128)S(1)} collective-permute-done((f32[40,256]{1,0:T(8,128)S(1)}, f32[40,256]{1,0:T(8,128)S(1)}, u32[]{:S(2)}, u32[]{:S(2)}) %collective-permute-start.17) | collective-permute-done | bytes 40992 | tf_op jit(solution)/shard_map/ppermute | solution.py:197
  48.5 2.0 %collective-permute-done.16 = f32[40,256]{1,0:T(8,128)S(1)} collective-permute-done((f32[40,256]{1,0:T(8,128)S(1)}, f32[40,256]{1,0:T(8,128)S(1)}, u32[]{:S(2)}, u32[]{:S(2)}) %collective-permute-start.16) | collective-permute-done | bytes 40992 | tf_op jit(solution)/shard_map/ppermute | solution.py:197
  50.5 0.0 collective-permute-done.15
  50.5 1.8 %collective-permute-start.20 = (f32[40,256]{1,0:T(8,128)S(1)}, f32[40,256]{1,0:T(8,128)S(1)}, u32[]{:S(2)}, u32[]{:S(2)}) collective-permute-start(f32[40,256]{1,0:T(8,128)S(1)} %fusion), channel_id=1, source_target_pairs={{0,24},{8,16},{16,8},{24,0},{1,25},{9,17},{17,9},{25,1},{2,26},{10... | collective-permute-start | bytes 122888 | tf_op jit(solution)/shard_map/ppermute | solution.py:197
  52.3 1.6 %collective-permute-start.19 = (f32[40,256]{1,0:T(8,128)S(1)}, f32[40,256]{1,0:T(8,128)S(1)}, u32[]{:S(2)}, u32[]{:S(2)}) collective-permute-start(f32[40,256]{1,0:T(8,128)S(1)} %fusion), channel_id=1, source_target_pairs={{0,16},{8,24},{16,0},{24,8},{1,17},{9,25},{17,1},{25,9},{2,18},{10... | collective-permute-start | bytes 122888 | tf_op jit(solution)/shard_map/ppermute | solution.py:197
  53.9 0.2 collective-permute-start.18
  54.1 0.0 collective-permute-done.12
  54.1 1.8 %collective-permute-done.20 = f32[40,256]{1,0:T(8,128)S(1)} collective-permute-done((f32[40,256]{1,0:T(8,128)S(1)}, f32[40,256]{1,0:T(8,128)S(1)}, u32[]{:S(2)}, u32[]{:S(2)}) %collective-permute-start.20) | collective-permute-done | bytes 40992 | tf_op jit(solution)/shard_map/ppermute | solution.py:197
  55.9 0.4 collective-permute-done.19
  56.3 1.6 %collective-permute-done.18 = f32[40,256]{1,0:T(8,128)S(1)} collective-permute-done((f32[40,256]{1,0:T(8,128)S(1)}, f32[40,256]{1,0:T(8,128)S(1)}, u32[]{:S(2)}, u32[]{:S(2)}) %collective-permute-start.18) | collective-permute-done | bytes 40992 | tf_op jit(solution)/shard_map/ppermute | solution.py:197
  57.9 2.3 %collective-permute-start.23 = (f32[32,256]{1,0:T(8,128)S(1)}, f32[32,256]{1,0:T(8,128)S(1)}, u32[]{:S(2)}, u32[]{:S(2)}) collective-permute-start(f32[32,256]{1,0:T(8,128)S(1)} %slice.100), channel_id=1, source_target_pairs={{0,6},{1,7},{2,4},{3,5},{4,2},{5,3},{6,0},{7,1},{8,14},{9,15},{10,... | collective-permute-start | bytes 98312 | tf_op jit(solution)/shard_map/ppermute | solution.py:197
  60.3 0.0 collective-permute-start.22
  60.3 2.1 %collective-permute-start.21 = (f32[32,256]{1,0:T(8,128)S(1)}, f32[32,256]{1,0:T(8,128)S(1)}, u32[]{:S(2)}, u32[]{:S(2)}) collective-permute-start(f32[32,256]{1,0:T(8,128)S(1)} %slice.100), channel_id=1, source_target_pairs={{0,2},{1,3},{2,0},{3,1},{4,6},{5,7},{6,4},{7,5},{8,10},{9,11},{10,... | collective-permute-start | bytes 98312 | tf_op jit(solution)/shard_map/ppermute | solution.py:197
  62.4 0.1 collective-permute-start.13
  62.5 1.2 %collective-permute-done.23 = f32[32,256]{1,0:T(8,128)S(1)} collective-permute-done((f32[32,256]{1,0:T(8,128)S(1)}, f32[32,256]{1,0:T(8,128)S(1)}, u32[]{:S(2)}, u32[]{:S(2)}) %collective-permute-start.23) | collective-permute-done | bytes 32800 | tf_op jit(solution)/shard_map/ppermute | solution.py:197
  63.7 1.4 %collective-permute-done.22 = f32[32,256]{1,0:T(8,128)S(1)} collective-permute-done((f32[32,256]{1,0:T(8,128)S(1)}, f32[32,256]{1,0:T(8,128)S(1)}, u32[]{:S(2)}, u32[]{:S(2)}) %collective-permute-start.22) | collective-permute-done | bytes 32800 | tf_op jit(solution)/shard_map/ppermute | solution.py:197
  65.1 0.0 collective-permute-done.21
  65.1 0.1 collective-permute-start.24
  65.2 0.0 collective-permute-done.13.partner_ref
  65.2 1.1 %shard_map.125 = f32[128,256]{1,0:T(8,128)} custom-call(s32[1,256]{1,0:T(1,128)S(1)} %get-tuple-element.40.wanted_ref, f32[256,256]{1,0:T(8,128)S(1)} %copy-done.1, f32[128,256]{1,0:T(8,128)S(1)} %pad_maximum_fusion.2.own_ref, f32[128,256]{1,0:T(8,128)S(1)} %collective-permute-done.13.partner_ref), custom_call_target="tpu_custom_call" | custom-call | flops 50331648 | bytes 656384 | tf_op jit(solution)/shard_map/pallas_call | solution.py:39
  66.3 0.2 collective-permute-done.24.partner_ref
  66.5 0.7 %shard_map.126 = (f32[256,256]{1,0:T(8,128)}, f32[1,256]{1,0:T(1,128)}) custom-call(f32[40,256]{1,0:T(8,128)S(1)} %add_add_fusion.summed_ref, f32[128,256]{1,0:T(8,128)S(1)} %pad_maximum_fusion.4.own_ref, f32[128,256]{1,0:T(8,128)S(1)} %collective-permute-done.24.partner_ref), custom_call_target="tpu_custom_call" | custom-call | bytes 566272 | tf_op jit(solution)/shard_map/pallas_call | solution.py:39
  (23 shorter events, 0.2 us)
Async XLA Ops:
  1.8 5.7 %collective-permute-start = (f32[64,256]{1,0:T(8,128)S(1)}, f32[64,256]{1,0:T(8,128)S(1)}, u32[]{:S(2)}, u32[]{:S(2)}) collective-permute-start(f32[64,256]{1,0:T(8,128)S(1)} %get-tuple-element.31), channel_id=1, source_target_pairs={{0,2},{1,3},{2,0},{3,1},{4,6},{5,7},{6,4},{7,5},{8,10},{9,11},{10,... | collective-permute-start | bytes 196616 | tf_op jit(solution)/shard_map/ppermute | solution.py:197
  5.0 7.3 %collective-permute-start.1 = (f32[64,256]{1,0:T(8,128)S(1)}, f32[64,256]{1,0:T(8,128)S(1)}, u32[]{:S(2)}, u32[]{:S(2)}) collective-permute-start(f32[64,256]{1,0:T(8,128)S(1)} %get-tuple-element.32), channel_id=1, source_target_pairs={{0,4},{1,5},{2,6},{3,7},{4,0},{5,1},{6,2},{7,3},{8,12},{9,13},{10,... | collective-permute-start | bytes 196616 | tf_op jit(solution)/shard_map/ppermute | solution.py:197
  7.5 6.1 %collective-permute-start.2 = (f32[64,256]{1,0:T(8,128)S(1)}, f32[64,256]{1,0:T(8,128)S(1)}, u32[]{:S(2)}, u32[]{:S(2)}) collective-permute-start(f32[64,256]{1,0:T(8,128)S(1)} %get-tuple-element.33), channel_id=1, source_target_pairs={{0,6},{1,7},{2,4},{3,5},{4,2},{5,3},{6,0},{7,1},{8,14},{9,15},{10,... | collective-permute-start | bytes 196616 | tf_op jit(solution)/shard_map/ppermute | solution.py:197
  13.6 0.8 %copy-start.5 = (s32[1,1,64]{2,1,0:T(1,128)S(1)}, s32[1,1,64]{2,1,0:T(1,128)}, u32[]{:S(2)}) copy-start(s32[1,1,64]{2,1,0:T(1,128)} %param.15) | copy-start | bytes 772
  13.6 3.3 %collective-permute-start.3 = (f32[128,256]{1,0:T(8,128)S(1)}, f32[128,256]{1,0:T(8,128)S(1)}, u32[]{:S(2)}, u32[]{:S(2)}) collective-permute-start(f32[128,256]{1,0:T(8,128)S(1)} %pad_maximum_fusion.1), channel_id=1, source_target_pairs={{0,1},{1,0},{2,3},{3,2},{4,5},{5,4},{6,7},{7,6},{8,9},{9,8},{10,11... | collective-permute-start | bytes 393224 | tf_op jit(solution)/shard_map/ppermute | solution.py:197
  14.4 0.7 %copy-start.3 = (f32[256]{0:T(256)S(1)}, f32[256]{0:T(256)}, u32[]{:S(2)}) copy-start(f32[256]{0:T(256)} %param.11) | copy-start | bytes 3076
  14.4 0.7 %copy-start.4 = (s32[1,1,64]{2,1,0:T(1,128)S(1)}, s32[1,1,64]{2,1,0:T(1,128)}, u32[]{:S(2)}) copy-start(s32[1,1,64]{2,1,0:T(1,128)} %param.14) | copy-start | bytes 772
  15.1 1.2 %copy-start = (f32[1,1,64,4096]{3,2,1,0:T(8,128)S(1)}, f32[1,1,64,4096]{3,2,1,0:T(8,128)}, u32[]{:S(2)}) copy-start(f32[1,1,64,4096]{3,2,1,0:T(8,128)} %param.13) | copy-start | bytes 3145732
  16.9 10.8 %copy-start.1 = (f32[256,256]{1,0:T(8,128)S(1)}, f32[256,256]{1,0:T(8,128)}, u32[]{:S(2)}) copy-start(f32[256,256]{1,0:T(8,128)} %weight_ref.1) | copy-start | bytes 786436
  16.9 10.8 %copy-start.2 = (f32[128,256]{1,0:T(8,128)S(1)}, f32[128,256]{1,0:T(8,128)}, u32[]{:S(2)}) copy-start(f32[128,256]{1,0:T(8,128)} %refs_6_.1) | copy-start | bytes 393220
  17.8 6.4 %collective-permute-start.4 = (f32[128,256]{1,0:T(8,128)S(1)}, f32[128,256]{1,0:T(8,128)S(1)}, u32[]{:S(2)}, u32[]{:S(2)}) collective-permute-start(f32[128,256]{1,0:T(8,128)S(1)} %get-tuple-element.35), channel_id=1, source_target_pairs={{0,8},{8,0},{16,24},{24,16},{1,9},{9,1},{17,25},{25,17},{2,10},{10... | collective-permute-start | bytes 393224 | tf_op jit(solution)/shard_map/ppermute | solution.py:197
  19.3 8.4 %collective-permute-start.5 = (f32[128,256]{1,0:T(8,128)S(1)}, f32[128,256]{1,0:T(8,128)S(1)}, u32[]{:S(2)}, u32[]{:S(2)}) collective-permute-start(f32[128,256]{1,0:T(8,128)S(1)} %get-tuple-element.36), channel_id=1, source_target_pairs={{0,16},{8,24},{16,0},{24,8},{1,17},{9,25},{17,1},{25,9},{2,18},{10... | collective-permute-start | bytes 393224 | tf_op jit(solution)/shard_map/ppermute | solution.py:197
  20.8 6.9 %collective-permute-start.6 = (f32[128,256]{1,0:T(8,128)S(1)}, f32[128,256]{1,0:T(8,128)S(1)}, u32[]{:S(2)}, u32[]{:S(2)}) collective-permute-start(f32[128,256]{1,0:T(8,128)S(1)} %get-tuple-element.37), channel_id=1, source_target_pairs={{0,24},{8,16},{16,8},{24,0},{1,25},{9,17},{17,9},{25,1},{2,26},{10... | collective-permute-start | bytes 393224 | tf_op jit(solution)/shard_map/ppermute | solution.py:197
  28.7 7.2 %collective-permute-start.9 = (f32[128,256]{1,0:T(8,128)S(1)}, f32[128,256]{1,0:T(8,128)S(1)}, u32[]{:S(2)}, u32[]{:S(2)}) collective-permute-start(f32[128,256]{1,0:T(8,128)S(1)} %get-tuple-element.43.refs_0_), channel_id=1, source_target_pairs={{0,24},{8,16},{16,8},{24,0},{1,25},{9,17},{17,9},{25,1},{2,26},{10... | collective-permute-start | bytes 393224 | tf_op jit(solution)/shard_map/ppermute | solution.py:197
  30.2 6.9 %collective-permute-start.8 = (f32[128,256]{1,0:T(8,128)S(1)}, f32[128,256]{1,0:T(8,128)S(1)}, u32[]{:S(2)}, u32[]{:S(2)}) collective-permute-start(f32[128,256]{1,0:T(8,128)S(1)} %get-tuple-element.43.refs_0_), channel_id=1, source_target_pairs={{0,16},{8,24},{16,0},{24,8},{1,17},{9,25},{17,1},{25,9},{2,18},{10... | collective-permute-start | bytes 393224 | tf_op jit(solution)/shard_map/ppermute | solution.py:197
  31.4 5.9 %collective-permute-start.7 = (f32[128,256]{1,0:T(8,128)S(1)}, f32[128,256]{1,0:T(8,128)S(1)}, u32[]{:S(2)}, u32[]{:S(2)}) collective-permute-start(f32[128,256]{1,0:T(8,128)S(1)} %get-tuple-element.43.refs_0_), channel_id=1, source_target_pairs={{0,8},{8,0},{16,24},{24,16},{1,9},{9,1},{17,25},{25,17},{2,10},{10... | collective-permute-start | bytes 393224 | tf_op jit(solution)/shard_map/ppermute | solution.py:197
  32.2 10.3 %collective-permute-start.14 = (f32[160,256]{1,0:T(8,128)S(1)}, f32[160,256]{1,0:T(8,128)S(1)}, u32[]{:S(2)}, u32[]{:S(2)}) collective-permute-start(f32[160,256]{1,0:T(8,128)S(1)} %get-tuple-element.49), channel_id=1, source_target_pairs={{0,1},{1,0},{2,3},{3,2},{4,5},{5,4},{6,7},{7,6},{8,9},{9,8},{10,11... | collective-permute-start | bytes 491528 | tf_op jit(solution)/shard_map/ppermute | solution.py:197
  38.0 6.4 %collective-permute-start.10 = (f32[64,256]{1,0:T(8,128)S(1)}, f32[64,256]{1,0:T(8,128)S(1)}, u32[]{:S(2)}, u32[]{:S(2)}) collective-permute-start(f32[64,256]{1,0:T(8,128)S(1)} %get-tuple-element.45), channel_id=1, source_target_pairs={{0,2},{1,3},{2,0},{3,1},{4,6},{5,7},{6,4},{7,5},{8,10},{9,11},{10,... | collective-permute-start | bytes 196616 | tf_op jit(solution)/shard_map/ppermute | solution.py:197
  38.1 9.1 %collective-permute-start.11 = (f32[64,256]{1,0:T(8,128)S(1)}, f32[64,256]{1,0:T(8,128)S(1)}, u32[]{:S(2)}, u32[]{:S(2)}) collective-permute-start(f32[64,256]{1,0:T(8,128)S(1)} %get-tuple-element.46), channel_id=1, source_target_pairs={{0,4},{1,5},{2,6},{3,7},{4,0},{5,1},{6,2},{7,3},{8,12},{9,13},{10,... | collective-permute-start | bytes 196616 | tf_op jit(solution)/shard_map/ppermute | solution.py:197
  40.4 13.6 %collective-permute-start.12 = (f32[64,256]{1,0:T(8,128)S(1)}, f32[64,256]{1,0:T(8,128)S(1)}, u32[]{:S(2)}, u32[]{:S(2)}) collective-permute-start(f32[64,256]{1,0:T(8,128)S(1)} %get-tuple-element.47), channel_id=1, source_target_pairs={{0,6},{1,7},{2,4},{3,5},{4,2},{5,3},{6,0},{7,1},{8,14},{9,15},{10,... | collective-permute-start | bytes 196616 | tf_op jit(solution)/shard_map/ppermute | solution.py:197
  42.5 6.0 %collective-permute-start.17 = (f32[40,256]{1,0:T(8,128)S(1)}, f32[40,256]{1,0:T(8,128)S(1)}, u32[]{:S(2)}, u32[]{:S(2)}) collective-permute-start(f32[40,256]{1,0:T(8,128)S(1)} %get-tuple-element.52), channel_id=1, source_target_pairs={{0,6},{1,7},{2,4},{3,5},{4,2},{5,3},{6,0},{7,1},{8,14},{9,15},{10,... | collective-permute-start | bytes 122888 | tf_op jit(solution)/shard_map/ppermute | solution.py:197
  44.4 6.1 %collective-permute-start.16 = (f32[40,256]{1,0:T(8,128)S(1)}, f32[40,256]{1,0:T(8,128)S(1)}, u32[]{:S(2)}, u32[]{:S(2)}) collective-permute-start(f32[40,256]{1,0:T(8,128)S(1)} %get-tuple-element.53), channel_id=1, source_target_pairs={{0,4},{1,5},{2,6},{3,7},{4,0},{5,1},{6,2},{7,3},{8,12},{9,13},{10,... | collective-permute-start | bytes 122888 | tf_op jit(solution)/shard_map/ppermute | solution.py:197
  44.4 6.1 %collective-permute-start.15 = (f32[40,256]{1,0:T(8,128)S(1)}, f32[40,256]{1,0:T(8,128)S(1)}, u32[]{:S(2)}, u32[]{:S(2)}) collective-permute-start(f32[40,256]{1,0:T(8,128)S(1)} %get-tuple-element.54), channel_id=1, source_target_pairs={{0,2},{1,3},{2,0},{3,1},{4,6},{5,7},{6,4},{7,5},{8,10},{9,11},{10,... | collective-permute-start | bytes 122888 | tf_op jit(solution)/shard_map/ppermute | solution.py:197
  50.5 5.3 %collective-permute-start.20 = (f32[40,256]{1,0:T(8,128)S(1)}, f32[40,256]{1,0:T(8,128)S(1)}, u32[]{:S(2)}, u32[]{:S(2)}) collective-permute-start(f32[40,256]{1,0:T(8,128)S(1)} %fusion), channel_id=1, source_target_pairs={{0,24},{8,16},{16,8},{24,0},{1,25},{9,17},{17,9},{25,1},{2,26},{10... | collective-permute-start | bytes 122888 | tf_op jit(solution)/shard_map/ppermute | solution.py:197
  52.3 4.0 %collective-permute-start.19 = (f32[40,256]{1,0:T(8,128)S(1)}, f32[40,256]{1,0:T(8,128)S(1)}, u32[]{:S(2)}, u32[]{:S(2)}) collective-permute-start(f32[40,256]{1,0:T(8,128)S(1)} %fusion), channel_id=1, source_target_pairs={{0,16},{8,24},{16,0},{24,8},{1,17},{9,25},{17,1},{25,9},{2,18},{10... | collective-permute-start | bytes 122888 | tf_op jit(solution)/shard_map/ppermute | solution.py:197
  53.9 4.0 %collective-permute-start.18 = (f32[40,256]{1,0:T(8,128)S(1)}, f32[40,256]{1,0:T(8,128)S(1)}, u32[]{:S(2)}, u32[]{:S(2)}) collective-permute-start(f32[40,256]{1,0:T(8,128)S(1)} %fusion), channel_id=1, source_target_pairs={{0,8},{8,0},{16,24},{24,16},{1,9},{9,1},{17,25},{25,17},{2,10},{10... | collective-permute-start | bytes 122888 | tf_op jit(solution)/shard_map/ppermute | solution.py:197
  57.9 5.8 %collective-permute-start.23 = (f32[32,256]{1,0:T(8,128)S(1)}, f32[32,256]{1,0:T(8,128)S(1)}, u32[]{:S(2)}, u32[]{:S(2)}) collective-permute-start(f32[32,256]{1,0:T(8,128)S(1)} %slice.100), channel_id=1, source_target_pairs={{0,6},{1,7},{2,4},{3,5},{4,2},{5,3},{6,0},{7,1},{8,14},{9,15},{10,... | collective-permute-start | bytes 98312 | tf_op jit(solution)/shard_map/ppermute | solution.py:197
  60.3 4.8 %collective-permute-start.22 = (f32[32,256]{1,0:T(8,128)S(1)}, f32[32,256]{1,0:T(8,128)S(1)}, u32[]{:S(2)}, u32[]{:S(2)}) collective-permute-start(f32[32,256]{1,0:T(8,128)S(1)} %slice.100), channel_id=1, source_target_pairs={{0,4},{1,5},{2,6},{3,7},{4,0},{5,1},{6,2},{7,3},{8,12},{9,13},{10,... | collective-permute-start | bytes 98312 | tf_op jit(solution)/shard_map/ppermute | solution.py:197
  60.3 4.8 %collective-permute-start.21 = (f32[32,256]{1,0:T(8,128)S(1)}, f32[32,256]{1,0:T(8,128)S(1)}, u32[]{:S(2)}, u32[]{:S(2)}) collective-permute-start(f32[32,256]{1,0:T(8,128)S(1)} %slice.100), channel_id=1, source_target_pairs={{0,2},{1,3},{2,0},{3,1},{4,6},{5,7},{6,4},{7,5},{8,10},{9,11},{10,... | collective-permute-start | bytes 98312 | tf_op jit(solution)/shard_map/ppermute | solution.py:197
  62.4 2.8 %collective-permute-start.13 = (f32[128,256]{1,0:T(8,128)S(1)}, f32[128,256]{1,0:T(8,128)S(1)}, u32[]{:S(2)}, u32[]{:S(2)}) collective-permute-start(f32[128,256]{1,0:T(8,128)S(1)} %pad_maximum_fusion.3), channel_id=1, source_target_pairs={{0,1},{1,0},{2,3},{3,2},{4,5},{5,4},{6,7},{7,6},{8,9},{9,8},{10,11... | collective-permute-start | bytes 393224 | tf_op jit(solution)/shard_map/ppermute | solution.py:197
  65.1 1.4 %collective-permute-start.24 = (f32[128,256]{1,0:T(8,128)S(1)}, f32[128,256]{1,0:T(8,128)S(1)}, u32[]{:S(2)}, u32[]{:S(2)}) collective-permute-start(f32[128,256]{1,0:T(8,128)S(1)} %pad_maximum_fusion.4.own_ref), channel_id=1, source_target_pairs={{0,1},{1,0},{2,3},{3,2},{4,5},{5,4},{6,7},{7,6},{8,9},{9,8},{10,11... | collective-permute-start | bytes 393224 | tf_op jit(solution)/shard_map/ppermute | solution.py:197

commit v3 on v2

--- a/solution.py
+++ b/solution.py
@@ -32,7 +32,7 @@
     return mm(a[0], b[0], dims) + (mm(a[0], b[1], dims) + mm(a[1], b[0], dims))
 
 
-def call(kernel, outs, args, scratch=(), flops=0, smem=(), hbm=()):
+def call(kernel, outs, args, scratch=(), flops=0, smem=(), hbm=(), hbm_out=()):
     out_bytes = sum(int(o.size) * o.dtype.itemsize for o in outs)
     in_bytes = sum(int(a.size) * a.dtype.itemsize for a in args)
     limit = max(FLOOR, 4 * (in_bytes + out_bytes))
@@ -45,7 +45,10 @@
             )
             for k in range(len(args))
         ],
-        out_specs=[pl.BlockSpec(memory_space=pltpu.VMEM) for _ in outs],
+        out_specs=[
+            pl.BlockSpec(memory_space=pltpu.HBM if k in hbm_out else pltpu.VMEM)
+            for k in range(len(outs))
+        ],
         scratch_shapes=list(scratch),
         cost_estimate=pl.CostEstimate(
             flops=flops, transcendentals=0, bytes_accessed=in_bytes + out_bytes
@@ -102,36 +105,25 @@
     put_pairs(outs, buffer, me, outs[0].shape[0] // 2)
 
 
-def aggregate(groups, row_blocks, per, high_ref, low_ref, own_ref, partner_ref, *refs):
-    outs, border, natural = refs[:groups], refs[groups], refs[groups + 1]
-    me, group = lax.axis_index("row"), lax.axis_index("rep")
-    take_pairs(own_ref, partner_ref, border, me, per)
-    result = mm3((high_ref[...], low_ref[...]), split(border[...]), NN)
-    unmix(result, natural, row_blocks)
-    nodes = outs[0].shape[0]
-    for s in range(groups):
-        for part in range(natural.shape[0]):
-            outs[s][:, part * LANES : (part + 1) * LANES] = natural[
-                part, rows_at(lax.bitwise_xor(group, s), nodes), :
-            ]
-
-
-def unmix(result, natural, row_blocks):
-    for m in range(BS):
-        start = ((m % 2) * (BS // 2) + m // 2) * row_blocks
-        for part in range(natural.shape[0]):
-            natural[part, pl.ds(m, row_blocks, stride=BS), :] = result[
-                start : start + row_blocks, part * LANES : (part + 1) * LANES
-            ]
+def aggregate(pairs, high_ref, low_ref, own_ref, partner_ref, *outs):
+    per = own_ref.shape[0] // pairs
+    pieces = []
+    for pair in range(pairs):
+        for ref in (own_ref, partner_ref):
+            pieces.append(ref[pair * per : (pair + 1) * per, :])
+    border = jnp.concatenate(pieces, axis=0)
+    result = mm3((high_ref[...], low_ref[...]), split(border), NN)
+    for s, out in enumerate(outs):
+        out[...] = result[s * out.shape[0] : (s + 1) * out.shape[0], :]
 
 
 def activate(groups, members, *refs):
     pieces = refs[:groups]
-    weight_ref, bias_ref, cot_ref, act_ref, grad_ref, keep_ref, send_ref, buffer = refs[groups:]
+    high_ref, low_ref, bias_ref, cot_ref, act_ref, grad_ref, keep_ref, send_ref, buffer = refs[groups:]
     me = lax.axis_index("row")
     total = tree_sum([piece[...] for piece in pieces])
     total_split = split(total)
-    pre = mm3(total_split, split(weight_ref[...]), NN) + bias_ref[...]
+    pre = mm3(total_split, (high_ref[...], low_ref[...]), NN) + bias_ref[...]
     gate = jax.nn.sigmoid(pre)
     act_ref[...] = pre * gate
     grad = cot_ref[...] * (gate * (1.0 + pre * (1.0 - gate)))
@@ -146,50 +138,37 @@
         target[start + chunk : start + chunk + PAD, :] = sums
 
 
-def spread(groups, pairs, row_blocks, high_ref, low_ref, *refs):
-    pieces, outs = refs[:groups], refs[groups : groups + pairs]
-    natural, border = refs[groups + pairs :]
-    me, group = lax.axis_index("row"), lax.axis_index("rep")
-    nodes = pieces[0].shape[0]
-    for s in range(groups):
-        for part in range(natural.shape[0]):
-            natural[part, rows_at(lax.bitwise_xor(group, s), nodes), :] = pieces[s][
-                :, part * LANES : (part + 1) * LANES
-            ]
-    order = []
-    for parity in range(2):
-        for t in range(BS // 2):
-            order.append(
-                jnp.concatenate(
-                    [
-                        natural[part, pl.ds(2 * t + parity, row_blocks, stride=BS), :]
-                        for part in range(natural.shape[0])
-                    ],
-                    axis=1,
-                )
-            )
-    mixed = jnp.concatenate(order, axis=0)
-    border[...] = mm3((high_ref[...], low_ref[...]), split(mixed), NN)
-    put_pairs(outs, border, me, outs[0].shape[0] // 2)
-
-
-def collect(per, wanted_ref, weight_ref, own_ref, partner_ref, out_ref, border):
+def spread(groups, high_ref, low_ref, *refs):
+    pieces, outs = refs[:groups], refs[groups:]
+    grads = jnp.concatenate([piece[...] for piece in pieces], axis=0)
+    result = mm3((high_ref[...], low_ref[...]), split(grads), NN)
+    for pair, out in enumerate(outs):
+        out[...] = result[pair * out.shape[0] : (pair + 1) * out.shape[0], :]
+
+
+def collect(per, wanted_ref, high_ref, low_ref, own_ref, partner_ref, out_ref, border):
     me = lax.axis_index("row")
     take_pairs(own_ref, partner_ref, border, me, per)
     pick = one_hot(wanted_ref[...], out_ref.shape[0])
     high, low = split(border[...])
     proj = mm(pick, high, NN) + mm(pick, low, NN)
-    out_ref[...] = mm3(split(proj), split(weight_ref[...]), NT)
-
-
-def finish(members, summed_ref, own_ref, partner_ref, weight_ref, bias_ref):
+    out_ref[...] = mm3(split(proj), (high_ref[...], low_ref[...]), NT)
+
+
+def finish(members, summed_ref, own_ref, partner_ref, weight_hbm, bias_ref, sems):
     me = lax.axis_index("row")
-    chunk = weight_ref.shape[0] // members
+    chunk = weight_hbm.shape[0] // members
+    copies = []
     for s in range(members):
         piece = partner_ref if s % 2 else own_ref
-        start = (s // 2) * chunk
-        weight_ref[rows_at(lax.bitwise_xor(me, s), chunk), :] = piece[start : start + chunk, :]
+        source = piece.at[(s // 2) * chunk : (s // 2 + 1) * chunk, :]
+        target = weight_hbm.at[rows_at(lax.bitwise_xor(me, s), chunk), :]
+        copies.append(pltpu.make_async_copy(source, target, sems.at[s]))
+    for copy in copies:
+        copy.start()
     bias_ref[...] = summed_ref[chunk : chunk + 1, :]
+    for copy in copies:
+        copy.wait()
 
 
 def exchange(value, axis, shift):
@@ -217,10 +196,10 @@
     row_blocks = groups * nodes // BS
     col_blocks = slots // BS
     rows = row_blocks * BS
+    assert 2 * per == BS and nodes % BS == 0
     pairs = members // 2
     shape = lambda n: jax.ShapeDtypeStruct((n, width), F32)
     vmem = lambda n: pltpu.VMEM((n, width), F32)
-    tiles = pltpu.VMEM((width // LANES, rows, LANES), F32)
 
     *sends, wanted = call(
         gather_rows,
@@ -233,19 +212,19 @@
     wide = jax.ShapeDtypeStruct((rows, slots), BF16)
     tall = jax.ShapeDtypeStruct((slots, rows), BF16)
     bias_row = jax.ShapeDtypeStruct((1, width), F32)
-    *dense, bias_here = call(
-        functools.partial(build, row_blocks, col_blocks),
-        [wide, wide, tall, tall, bias_row],
-        [live_blocks, row_block[0], col_block[0], blocks[0, 0], bias[None, :]],
-        [pltpu.VMEM((rows, slots), F32)],
+    half_weight = jax.ShapeDtypeStruct(weight.shape, BF16)
+    *dense, bias_here, weight_high, weight_low = call(
+        functools.partial(build, nodes // BS),
+        [wide, wide, tall, tall, bias_row, half_weight, half_weight],
+        [live_blocks, row_block[0], col_block[0], blocks[0, 0], bias[None, :], weight],
+        [pltpu.VMEM((slots // LANES, rows, LANES), F32)],
         flops=4 * row_blocks * col_blocks * capacity * BS * BS,
         smem=(0,),
     )
     partials = call(
-        functools.partial(aggregate, groups, row_blocks, per),
+        functools.partial(aggregate, pairs),
         [shape(nodes)] * groups,
         dense[:2] + border,
-        [vmem(slots), tiles],
         flops=6 * rows * slots * width,
     )
     parts = [partials[0]] + [exchange(partials[s], "rep", s) for s in range(1, groups)]
@@ -254,23 +233,22 @@
     activated, grad, keep, send = call(
         functools.partial(activate, groups, members),
         [shape(nodes), shape(nodes), shape(padded), shape(padded)],
-        parts + [weight, bias_here, cotangent],
+        parts + [weight_high, weight_low, bias_here, cotangent],
         [vmem(width)],
         flops=12 * nodes * width * width,
     )
     grads = [grad] + [exchange(grad, "rep", s) for s in range(1, groups)]
     backs = call(
-        functools.partial(spread, groups, pairs, row_blocks),
+        functools.partial(spread, groups),
         [shape(2 * per)] * pairs,
         dense[2:] + grads,
-        [tiles, vmem(slots)],
         flops=6 * rows * slots * width,
     )
     returned = swap_rows(backs)
     (feat_grad,) = call(
         functools.partial(collect, per),
         [shape(nodes)],
-        [wanted, weight] + returned,
+        [wanted, weight_high, weight_low] + returned,
         [vmem(slots)],
         flops=6 * nodes * width * width,
     )
@@ -285,35 +263,49 @@
     own = jnp.concatenate(chunks, axis=0)
     partner = exchange(own, "row", 1)
     weight_grad, bias_grad = call(
-        functools.partial(finish, members), [shape(width), shape(1)], [summed, own, partner]
+        functools.partial(finish, members),
+        [shape(width), shape(1)],
+        [summed, own, partner],
+        [pltpu.SemaphoreType.DMA((members,))],
+        hbm_out=(0,),
     )
     return (activated, feat_grad, weight_grad, bias_grad[0])
 
 
-def build(row_blocks, col_blocks, live_ref, rows_ref, cols_ref, blocks_ref, bias_ref, *refs):
-    high_ref, low_ref, high_t_ref, low_t_ref, bias_out, out_ref = refs
+def build(shard_blocks, live_ref, rows_ref, cols_ref, blocks_ref, bias_ref, weight_ref, *refs):
+    high_ref, low_ref, high_t_ref, low_t_ref, bias_out, weight_high, weight_low, dense = refs
     bias_out[...] = bias_ref[...]
+    weight_high[...], weight_low[...] = split(weight_ref[...])
+    row_blocks = high_ref.shape[0] // BS
+    col_blocks = high_ref.shape[1] // BS
     capacity = blocks_ref.shape[0]
     pairs = row_blocks * col_blocks
-    steps = blocks_ref.shape[1] // LANES
-    pair_of = cols_ref[...] * row_blocks + rows_ref[...]
+    me, group = lax.axis_index("row"), lax.axis_index("rep")
+    rows = lax.bitwise_xor(rows_ref[...], group * shard_blocks)
+    cols = lax.bitwise_xor(cols_ref[...], me // 2)
     pair = lax.broadcasted_iota(jnp.int32, (pairs, capacity), 0)
     slot = lax.broadcasted_iota(jnp.int32, (pairs, capacity), 1)
-    pick = ((pair == pair_of) & (slot < live_ref[0, 0])).astype(BF16)
+    pick = ((pair == cols * row_blocks + rows) & (slot < live_ref[0, 0])).astype(BF16)
     high, low = split(blocks_ref[...])
-    dense = mm(pick, high, NN) + mm(pick, low, NN)
-    left = lax.broadcasted_iota(jnp.int32, (row_blocks, LANES), 1) < BS
-    for t in range(steps):
+    product = mm(pick, high, NN) + mm(pick, low, NN)
+    lane = lax.broadcasted_iota(jnp.int32, (row_blocks, LANES), 1)
+    left = lane < BS
+    upper = lane % BS < BS // 2
+    same = me % 2 == 0
+    for t in range(blocks_ref.shape[1] // LANES):
         lanes = slice(t * LANES, (t + 1) * LANES)
         for u in range(col_blocks // 2):
-            first = dense[2 * u * row_blocks : (2 * u + 1) * row_blocks, lanes]
-            second = dense[(2 * u + 1) * row_blocks : (2 * u + 2) * row_blocks, lanes]
+            first = product[2 * u * row_blocks : (2 * u + 1) * row_blocks, lanes]
+            second = product[(2 * u + 1) * row_blocks : (2 * u + 2) * row_blocks, lanes]
             even = jnp.where(left, first, pltpu.roll(second, BS, 1))
             odd = jnp.where(left, pltpu.roll(first, BS, 1), second)
             for parity, value in ((0, even), (1, odd)):
-                start = (parity * steps + t) * row_blocks
-                out_ref[start : start + row_blocks, u * LANES : (u + 1) * LANES] = value
-    full = out_ref[...]
+                swapped = jnp.where(
+                    upper, pltpu.roll(value, LANES - BS // 2, 1), pltpu.roll(value, BS // 2, 1)
+                )
+                value = jnp.where(same, value, swapped)
+                dense[u, pl.ds(2 * t + parity, row_blocks, stride=BS), :] = value
+    full = jnp.concatenate([dense[u] for u in range(col_blocks // 2)], axis=1)
     high_ref[...], low_ref[...] = split(full)
     high_t_ref[...], low_t_ref[...] = split(full.T)
 

time: 67.4 us -> 68.5 us (1.016)
  Pallas kernels: 6.09 us -> 7.2 us
    pallas_call x7, Pallas kernels: 6.09 us -> 7.2 us  [call(): pl.pallas_call(kernel, out_shape=outs, in_specs=[pl.BlockSpec(memory_spac...]
  transfers between devices with their start and end apart: 25 -> 25, of which waited for: 16 -> 16; matrix products, arithmetic and copies ran while one was open for 0% -> 0% of each run, Pallas kernels for 4% -> 5%
where the time goes in v3:
time: 68.5 us; the launch traced here: 68.3 us
  starting transfers between devices  29.9 us (44%)
  waiting for transfers between devices  27.7 us (40%)
  Pallas kernels  7.2 us (11%)
  local copies, waits for them, and re-layouts  1.95 us (3%)
  between operations  1.51 us (2%)
    ppermute x25, starting transfers between devices, exchange(): return lax.ppermute(value, axis, [(i, i ^ shift) for i in range(size)])  29.9 us
    ppermute x25, waiting for transfers between devices, exchange(): return lax.ppermute(value, axis, [(i, i ^ shift) for i in range(size)])  27.7 us
    pallas_call x7, Pallas kernels, call(): pl.pallas_call(kernel, out_shape=outs, in_specs=[pl.BlockSpec(memory_spac...  7.2 us
    unnamed x12, local copies, waits for them, and re-layouts  1.89 us
  transfers between devices with their start and end apart: 25, of which 16 were waited for; matrix products, arithmetic and copies ran while one was open for 0% of the time, Pallas kernels for 5%

profile of v3, /device:TPU:0, one launch (start us, length us, event | category | flops | bytes accessed | tf_op | source)
XLA Modules:
  0.0 68.3 jit_solution(14975576737552196065)
XLA Ops:
  0.6 1.2 %shard_map.121 = (f32[64,256]{1,0:T(8,128)S(1)}, f32[64,256]{1,0:T(8,128)S(1)}, f32[64,256]{1,0:T(8,128)S(1)}, f32[64,256]{1,0:T(8,128)S(1)}, s32[1,256]{1,0:T(1,128)S(1)}) custom-call(s32[1,2048]{1,0:T(1,128)} %list_hbm.1, f32[128,256]{1,0:T(8,128)} %feat_hbm.1), custom_call_target="tpu_custom_call" | custom-call | bytes 402432 | tf_op jit(solution)/shard_map/pallas_call | solution.py:39
  1.8 3.1 %collective-permute-start = (f32[64,256]{1,0:T(8,128)S(1)}, f32[64,256]{1,0:T(8,128)S(1)}, u32[]{:S(2)}, u32[]{:S(2)}) collective-permute-start(f32[64,256]{1,0:T(8,128)S(1)} %get-tuple-element.33), channel_id=1, source_target_pairs={{0,2},{1,3},{2,0},{3,1},{4,6},{5,7},{6,4},{7,5},{8,10},{9,11},{10,... | collective-permute-start | bytes 196616 | tf_op jit(solution)/shard_map/ppermute | solution.py:176
  5.0 2.6 %collective-permute-start.1 = (f32[64,256]{1,0:T(8,128)S(1)}, f32[64,256]{1,0:T(8,128)S(1)}, u32[]{:S(2)}, u32[]{:S(2)}) collective-permute-start(f32[64,256]{1,0:T(8,128)S(1)} %get-tuple-element.34), channel_id=1, source_target_pairs={{0,4},{1,5},{2,6},{3,7},{4,0},{5,1},{6,2},{7,3},{8,12},{9,13},{10,... | collective-permute-start | bytes 196616 | tf_op jit(solution)/shard_map/ppermute | solution.py:176
  7.5 0.0 collective-permute-start.2
  7.6 0.0 collective-permute-done
  7.6 0.0 copy-start.1
  7.6 4.6 %collective-permute-done.1 = f32[64,256]{1,0:T(8,128)S(1)} collective-permute-done((f32[64,256]{1,0:T(8,128)S(1)}, f32[64,256]{1,0:T(8,128)S(1)}, u32[]{:S(2)}, u32[]{:S(2)}) %collective-permute-start.1) | collective-permute-done | bytes 65568 | tf_op jit(solution)/shard_map/ppermute | solution.py:176
  12.2 1.4 %collective-permute-done.2 = f32[64,256]{1,0:T(8,128)S(1)} collective-permute-done((f32[64,256]{1,0:T(8,128)S(1)}, f32[64,256]{1,0:T(8,128)S(1)}, u32[]{:S(2)}, u32[]{:S(2)}) %collective-permute-start.2) | collective-permute-done | bytes 65568 | tf_op jit(solution)/shard_map/ppermute | solution.py:176
  13.6 0.1 collective-permute-start.3
  14.4 0.0 copy-start.3
  14.4 0.0 copy-start.4
  14.4 0.6 copy-done.3
  15.1 0.0 copy-done.4
  15.1 1.2 %copy-done = f32[1,1,64,4096]{3,2,1,0:T(8,128)S(1)} copy-done((f32[1,1,64,4096]{3,2,1,0:T(8,128)S(1)}, f32[1,1,64,4096]{3,2,1,0:T(8,128)}, u32[]{:S(2)}) %copy-start) | copy-done | bytes 1048600
  16.3 1.9 %shard_map.120 = (bf16[512,256]{1,0:T(8,128)(2,1)S(1)}, bf16[512,256]{1,0:T(8,128)(2,1)S(1)}, bf16[256,512]{1,0:T(8,128)(2,1)S(1)}, bf16[256,512]{1,0:T(8,128)(2...) custom-call(s32[1,1]{1,0:T(1,128)S(6)} %copy.13.live_ref, ...), custom_call_target="tpu_custom_call" | custom-call | flops 33554432 | bytes 2624004 | tf_op jit(solution)/shard_map/pallas_call | solution.py:39
  18.2 0.0 collective-permute-done.3.partner_ref
  18.2 0.0 copy-start.2
  18.2 0.4 shard_map.122
  18.6 1.6 %collective-permute-start.4 = (f32[128,256]{1,0:T(8,128)S(1)}, f32[128,256]{1,0:T(8,128)S(1)}, u32[]{:S(2)}, u32[]{:S(2)}) collective-permute-start(f32[128,256]{1,0:T(8,128)S(1)} %get-tuple-element.37), channel_id=1, source_target_pairs={{0,8},{8,0},{16,24},{24,16},{1,9},{9,1},{17,25},{25,17},{2,10},{10... | collective-permute-start | bytes 393224 | tf_op jit(solution)/shard_map/ppermute | solution.py:176
  20.1 1.5 %collective-permute-start.5 = (f32[128,256]{1,0:T(8,128)S(1)}, f32[128,256]{1,0:T(8,128)S(1)}, u32[]{:S(2)}, u32[]{:S(2)}) collective-permute-start(f32[128,256]{1,0:T(8,128)S(1)} %get-tuple-element.38), channel_id=1, source_target_pairs={{0,16},{8,24},{16,0},{24,8},{1,17},{9,25},{17,1},{25,9},{2,18},{10... | collective-permute-start | bytes 393224 | tf_op jit(solution)/shard_map/ppermute | solution.py:176
  21.7 0.5 collective-permute-start.6
  22.1 2.8 %collective-permute-done.4.refs_1_ = f32[128,256]{1,0:T(8,128)S(1)} collective-permute-done((f32[128,256]{1,0:T(8,128)S(1)}, f32[128,256]{1,0:T(8,128)S(1)}, u32[]{:S(2)}, u32[]{:S(2)}) %collective-permute-start.4) | collective-permute-done | bytes 131104 | tf_op jit(solution)/shard_map/ppermute | solution.py:176
  24.9 3.6 %collective-permute-done.5.refs_2_ = f32[128,256]{1,0:T(8,128)S(1)} collective-permute-done((f32[128,256]{1,0:T(8,128)S(1)}, f32[128,256]{1,0:T(8,128)S(1)}, u32[]{:S(2)}, u32[]{:S(2)}) %collective-permute-start.5) | collective-permute-done | bytes 131104 | tf_op jit(solution)/shard_map/ppermute | solution.py:176
  28.6 0.0 collective-permute-done.6.refs_3_
  28.6 0.9 %shard_map.123 = (f32[128,256]{1,0:T(8,128)}, f32[128,256]{1,0:T(8,128)S(1)}, f32[160,256]{1,0:T(8,128)S(1)}, f32[160,256]{1,0:T(8,128)S(1)}) custom-call(f32[128,256]{1,0:T(8,128)S(1)} %get-tuple-element.36.refs_0_, f32[128,256]{1,0:T(8,128)S(1)} %collective-permute-done.4.refs_1_, f32[128,256]{1,0:T(8,128)S(1)} %collective-permute-done.5.refs_2_, ...), custom_call_target="tpu_custom_call" | custom-call | flops 100663296 | bytes 1508352 | tf_op jit(solution)/shard_map/pallas_call | solution.py:39
  29.5 1.5 %collective-permute-start.9 = (f32[128,256]{1,0:T(8,128)S(1)}, f32[128,256]{1,0:T(8,128)S(1)}, u32[]{:S(2)}, u32[]{:S(2)}) collective-permute-start(f32[128,256]{1,0:T(8,128)S(1)} %get-tuple-element.47.refs_0_), channel_id=1, source_target_pairs={{0,24},{8,16},{16,8},{24,0},{1,25},{9,17},{17,9},{25,1},{2,26},{10... | collective-permute-start | bytes 393224 | tf_op jit(solution)/shard_map/ppermute | solution.py:176
  31.0 1.2 %collective-permute-start.8 = (f32[128,256]{1,0:T(8,128)S(1)}, f32[128,256]{1,0:T(8,128)S(1)}, u32[]{:S(2)}, u32[]{:S(2)}) collective-permute-start(f32[128,256]{1,0:T(8,128)S(1)} %get-tuple-element.47.refs_0_), channel_id=1, source_target_pairs={{0,16},{8,24},{16,0},{24,8},{1,17},{9,25},{17,1},{25,9},{2,18},{10... | collective-permute-start | bytes 393224 | tf_op jit(solution)/shard_map/ppermute | solution.py:176
  32.2 0.8 %collective-permute-start.7 = (f32[128,256]{1,0:T(8,128)S(1)}, f32[128,256]{1,0:T(8,128)S(1)}, u32[]{:S(2)}, u32[]{:S(2)}) collective-permute-start(f32[128,256]{1,0:T(8,128)S(1)} %get-tuple-element.47.refs_0_), channel_id=1, source_target_pairs={{0,8},{8,0},{16,24},{24,16},{1,9},{9,1},{17,25},{25,17},{2,10},{10... | collective-permute-start | bytes 393224 | tf_op jit(solution)/shard_map/ppermute | solution.py:176
  33.0 0.0 collective-permute-start.14
  33.0 3.7 %collective-permute-done.9.refs_3_ = f32[128,256]{1,0:T(8,128)S(1)} collective-permute-done((f32[128,256]{1,0:T(8,128)S(1)}, f32[128,256]{1,0:T(8,128)S(1)}, u32[]{:S(2)}, u32[]{:S(2)}) %collective-permute-start.9) | collective-permute-done | bytes 131104 | tf_op jit(solution)/shard_map/ppermute | solution.py:176
  36.7 1.2 %collective-permute-done.8.refs_2_ = f32[128,256]{1,0:T(8,128)S(1)} collective-permute-done((f32[128,256]{1,0:T(8,128)S(1)}, f32[128,256]{1,0:T(8,128)S(1)}, u32[]{:S(2)}, u32[]{:S(2)}) %collective-permute-start.8) | collective-permute-done | bytes 131104 | tf_op jit(solution)/shard_map/ppermute | solution.py:176
  37.9 0.2 collective-permute-done.7.refs_1_
  38.1 0.4 shard_map.124
  38.5 0.1 collective-permute-start.10
  38.6 2.4 %collective-permute-start.11 = (f32[64,256]{1,0:T(8,128)S(1)}, f32[64,256]{1,0:T(8,128)S(1)}, u32[]{:S(2)}, u32[]{:S(2)}) collective-permute-start(f32[64,256]{1,0:T(8,128)S(1)} %get-tuple-element.50), channel_id=1, source_target_pairs={{0,4},{1,5},{2,6},{3,7},{4,0},{5,1},{6,2},{7,3},{8,12},{9,13},{10,... | collective-permute-start | bytes 196616 | tf_op jit(solution)/shard_map/ppermute | solution.py:176
  40.9 2.0 %collective-permute-start.12 = (f32[64,256]{1,0:T(8,128)S(1)}, f32[64,256]{1,0:T(8,128)S(1)}, u32[]{:S(2)}, u32[]{:S(2)}) collective-permute-start(f32[64,256]{1,0:T(8,128)S(1)} %get-tuple-element.51), channel_id=1, source_target_pairs={{0,6},{1,7},{2,4},{3,5},{4,2},{5,3},{6,0},{7,1},{8,14},{9,15},{10,... | collective-permute-start | bytes 196616 | tf_op jit(solution)/shard_map/ppermute | solution.py:176
  43.0 0.0 collective-permute-done.14
  43.0 1.9 %collective-permute-start.17 = (f32[40,256]{1,0:T(8,128)S(1)}, f32[40,256]{1,0:T(8,128)S(1)}, u32[]{:S(2)}, u32[]{:S(2)}) collective-permute-start(f32[40,256]{1,0:T(8,128)S(1)} %get-tuple-element.56), channel_id=1, source_target_pairs={{0,6},{1,7},{2,4},{3,5},{4,2},{5,3},{6,0},{7,1},{8,14},{9,15},{10,... | collective-permute-start | bytes 122888 | tf_op jit(solution)/shard_map/ppermute | solution.py:176
  44.9 0.0 collective-permute-start.16
  44.9 0.0 collective-permute-done.10
  44.9 2.6 %collective-permute-start.15 = (f32[40,256]{1,0:T(8,128)S(1)}, f32[40,256]{1,0:T(8,128)S(1)}, u32[]{:S(2)}, u32[]{:S(2)}) collective-permute-start(f32[40,256]{1,0:T(8,128)S(1)} %get-tuple-element.58), channel_id=1, source_target_pairs={{0,2},{1,3},{2,0},{3,1},{4,6},{5,7},{6,4},{7,5},{8,10},{9,11},{10,... | collective-permute-start | bytes 122888 | tf_op jit(solution)/shard_map/ppermute | solution.py:176
  47.5 0.2 collective-permute-done.11
  47.7 1.3 %collective-permute-done.17 = f32[40,256]{1,0:T(8,128)S(1)} collective-permute-done((f32[40,256]{1,0:T(8,128)S(1)}, f32[40,256]{1,0:T(8,128)S(1)}, u32[]{:S(2)}, u32[]{:S(2)}) %collective-permute-start.17) | collective-permute-done | bytes 40992 | tf_op jit(solution)/shard_map/ppermute | solution.py:176
  49.0 2.0 %collective-permute-done.16 = f32[40,256]{1,0:T(8,128)S(1)} collective-permute-done((f32[40,256]{1,0:T(8,128)S(1)}, f32[40,256]{1,0:T(8,128)S(1)}, u32[]{:S(2)}, u32[]{:S(2)}) %collective-permute-start.16) | collective-permute-done | bytes 40992 | tf_op jit(solution)/shard_map/ppermute | solution.py:176
  51.0 0.0 collective-permute-done.15
  51.0 1.8 %collective-permute-start.20 = (f32[40,256]{1,0:T(8,128)S(1)}, f32[40,256]{1,0:T(8,128)S(1)}, u32[]{:S(2)}, u32[]{:S(2)}) collective-permute-start(f32[40,256]{1,0:T(8,128)S(1)} %fusion), channel_id=1, source_target_pairs={{0,24},{8,16},{16,8},{24,0},{1,25},{9,17},{17,9},{25,1},{2,26},{10... | collective-permute-start | bytes 122888 | tf_op jit(solution)/shard_map/ppermute | solution.py:176
  52.8 1.6 %collective-permute-start.19 = (f32[40,256]{1,0:T(8,128)S(1)}, f32[40,256]{1,0:T(8,128)S(1)}, u32[]{:S(2)}, u32[]{:S(2)}) collective-permute-start(f32[40,256]{1,0:T(8,128)S(1)} %fusion), channel_id=1, source_target_pairs={{0,16},{8,24},{16,0},{24,8},{1,17},{9,25},{17,1},{25,9},{2,18},{10... | collective-permute-start | bytes 122888 | tf_op jit(solution)/shard_map/ppermute | solution.py:176
  54.4 0.2 collective-permute-start.18
  54.6 0.0 collective-permute-done.12
  54.6 1.8 %collective-permute-done.20 = f32[40,256]{1,0:T(8,128)S(1)} collective-permute-done((f32[40,256]{1,0:T(8,128)S(1)}, f32[40,256]{1,0:T(8,128)S(1)}, u32[]{:S(2)}, u32[]{:S(2)}) %collective-permute-start.20) | collective-permute-done | bytes 40992 | tf_op jit(solution)/shard_map/ppermute | solution.py:176
  56.4 0.4 collective-permute-done.19
  56.8 1.6 %collective-permute-done.18 = f32[40,256]{1,0:T(8,128)S(1)} collective-permute-done((f32[40,256]{1,0:T(8,128)S(1)}, f32[40,256]{1,0:T(8,128)S(1)}, u32[]{:S(2)}, u32[]{:S(2)}) %collective-permute-start.18) | collective-permute-done | bytes 40992 | tf_op jit(solution)/shard_map/ppermute | solution.py:176
  58.4 2.3 %collective-permute-start.23 = (f32[32,256]{1,0:T(8,128)S(1)}, f32[32,256]{1,0:T(8,128)S(1)}, u32[]{:S(2)}, u32[]{:S(2)}) collective-permute-start(f32[32,256]{1,0:T(8,128)S(1)} %slice.100), channel_id=1, source_target_pairs={{0,6},{1,7},{2,4},{3,5},{4,2},{5,3},{6,0},{7,1},{8,14},{9,15},{10,... | collective-permute-start | bytes 98312 | tf_op jit(solution)/shard_map/ppermute | solution.py:176
  60.7 0.0 collective-permute-start.22
  60.8 2.1 %collective-permute-start.21 = (f32[32,256]{1,0:T(8,128)S(1)}, f32[32,256]{1,0:T(8,128)S(1)}, u32[]{:S(2)}, u32[]{:S(2)}) collective-permute-start(f32[32,256]{1,0:T(8,128)S(1)} %slice.100), channel_id=1, source_target_pairs={{0,2},{1,3},{2,0},{3,1},{4,6},{5,7},{6,4},{7,5},{8,10},{9,11},{10,... | collective-permute-start | bytes 98312 | tf_op jit(solution)/shard_map/ppermute | solution.py:176
  62.9 0.1 collective-permute-start.13
  63.0 1.2 %collective-permute-done.23 = f32[32,256]{1,0:T(8,128)S(1)} collective-permute-done((f32[32,256]{1,0:T(8,128)S(1)}, f32[32,256]{1,0:T(8,128)S(1)}, u32[]{:S(2)}, u32[]{:S(2)}) %collective-permute-start.23) | collective-permute-done | bytes 32800 | tf_op jit(solution)/shard_map/ppermute | solution.py:176
  64.2 1.4 %collective-permute-done.22 = f32[32,256]{1,0:T(8,128)S(1)} collective-permute-done((f32[32,256]{1,0:T(8,128)S(1)}, f32[32,256]{1,0:T(8,128)S(1)}, u32[]{:S(2)}, u32[]{:S(2)}) %collective-permute-start.22) | collective-permute-done | bytes 32800 | tf_op jit(solution)/shard_map/ppermute | solution.py:176
  65.6 0.0 collective-permute-done.21
  65.6 0.1 collective-permute-start.24
  65.7 0.0 collective-permute-done.13.partner_ref
  65.7 1.1 %shard_map.125 = f32[128,256]{1,0:T(8,128)} custom-call(s32[1,256]{1,0:T(1,128)S(1)} %get-tuple-element.44.wanted_ref, bf16[256,256]{1,0:T(8,128)(2,1)S(1)} %get-tuple-element.40.refs_4_.high_ref, bf16[256,256]{1,0:T(8,128)(2,1)S(1)} %get-tuple-element.41.refs_5_.low_ref, f32[128,256]{1,0:T(8,128)S(1)} %pad_maximum_fusion.2.own_ref, ...), custom_call_target="tpu_custom_call" | custom-call | flops 50331648 | bytes 656384 | tf_op jit(solution)/shard_map/pallas_call | solution.py:39
  66.8 0.2 collective-permute-done.24.partner_ref
  67.0 1.3 %shard_map.126 = (f32[256,256]{1,0:T(8,128)}, f32[1,256]{1,0:T(1,128)}) custom-call(f32[40,256]{1,0:T(8,128)S(1)} %add_add_fusion.summed_ref, f32[128,256]{1,0:T(8,128)S(1)} %pad_maximum_fusion.4.own_ref, f32[128,256]{1,0:T(8,128)S(1)} %collective-permute-done.24.partner_ref), custom_call_target="tpu_custom_call" | custom-call | bytes 566272 | tf_op jit(solution)/shard_map/pallas_call | solution.py:39
  (23 shorter events, 0.2 us)
Async XLA Ops:
  1.8 5.7 %collective-permute-start = (f32[64,256]{1,0:T(8,128)S(1)}, f32[64,256]{1,0:T(8,128)S(1)}, u32[]{:S(2)}, u32[]{:S(2)}) collective-permute-start(f32[64,256]{1,0:T(8,128)S(1)} %get-tuple-element.33), channel_id=1, source_target_pairs={{0,2},{1,3},{2,0},{3,1},{4,6},{5,7},{6,4},{7,5},{8,10},{9,11},{10,... | collective-permute-start | bytes 196616 | tf_op jit(solution)/shard_map/ppermute | solution.py:176
  5.0 7.3 %collective-permute-start.1 = (f32[64,256]{1,0:T(8,128)S(1)}, f32[64,256]{1,0:T(8,128)S(1)}, u32[]{:S(2)}, u32[]{:S(2)}) collective-permute-start(f32[64,256]{1,0:T(8,128)S(1)} %get-tuple-element.34), channel_id=1, source_target_pairs={{0,4},{1,5},{2,6},{3,7},{4,0},{5,1},{6,2},{7,3},{8,12},{9,13},{10,... | collective-permute-start | bytes 196616 | tf_op jit(solution)/shard_map/ppermute | solution.py:176
  7.5 6.1 %collective-permute-start.2 = (f32[64,256]{1,0:T(8,128)S(1)}, f32[64,256]{1,0:T(8,128)S(1)}, u32[]{:S(2)}, u32[]{:S(2)}) collective-permute-start(f32[64,256]{1,0:T(8,128)S(1)} %get-tuple-element.35), channel_id=1, source_target_pairs={{0,6},{1,7},{2,4},{3,5},{4,2},{5,3},{6,0},{7,1},{8,14},{9,15},{10,... | collective-permute-start | bytes 196616 | tf_op jit(solution)/shard_map/ppermute | solution.py:176
  7.6 6.8 %copy-start.1 = (f32[256,256]{1,0:T(8,128)S(1)}, f32[256,256]{1,0:T(8,128)}, u32[]{:S(2)}) copy-start(f32[256,256]{1,0:T(8,128)} %weight_ref.1) | copy-start | bytes 786436
  13.6 0.8 %copy-start.5 = (s32[1,1,64]{2,1,0:T(1,128)S(1)}, s32[1,1,64]{2,1,0:T(1,128)}, u32[]{:S(2)}) copy-start(s32[1,1,64]{2,1,0:T(1,128)} %param.15) | copy-start | bytes 772
  13.6 4.5 %collective-permute-start.3 = (f32[128,256]{1,0:T(8,128)S(1)}, f32[128,256]{1,0:T(8,128)S(1)}, u32[]{:S(2)}, u32[]{:S(2)}) collective-permute-start(f32[128,256]{1,0:T(8,128)S(1)} %pad_maximum_fusion.1), channel_id=1, source_target_pairs={{0,1},{1,0},{2,3},{3,2},{4,5},{5,4},{6,7},{7,6},{8,9},{9,8},{10,11... | collective-permute-start | bytes 393224 | tf_op jit(solution)/shard_map/ppermute | solution.py:176
  14.4 0.7 copy-start.3
  14.4 0.7 copy-start.4
  15.1 1.2 %copy-start = (f32[1,1,64,4096]{3,2,1,0:T(8,128)S(1)}, f32[1,1,64,4096]{3,2,1,0:T(8,128)}, u32[]{:S(2)}) copy-start(f32[1,1,64,4096]{3,2,1,0:T(8,128)} %param.13) | copy-start | bytes 3145732
  18.2 10.4 %copy-start.2 = (f32[128,256]{1,0:T(8,128)S(1)}, f32[128,256]{1,0:T(8,128)}, u32[]{:S(2)}) copy-start(f32[128,256]{1,0:T(8,128)} %refs_7_.1) | copy-start | bytes 393220
  18.6 6.4 %collective-permute-start.4 = (f32[128,256]{1,0:T(8,128)S(1)}, f32[128,256]{1,0:T(8,128)S(1)}, u32[]{:S(2)}, u32[]{:S(2)}) collective-permute-start(f32[128,256]{1,0:T(8,128)S(1)} %get-tuple-element.37), channel_id=1, source_target_pairs={{0,8},{8,0},{16,24},{24,16},{1,9},{9,1},{17,25},{25,17},{2,10},{10... | collective-permute-start | bytes 393224 | tf_op jit(solution)/shard_map/ppermute | solution.py:176
  20.1 8.4 %collective-permute-start.5 = (f32[128,256]{1,0:T(8,128)S(1)}, f32[128,256]{1,0:T(8,128)S(1)}, u32[]{:S(2)}, u32[]{:S(2)}) collective-permute-start(f32[128,256]{1,0:T(8,128)S(1)} %get-tuple-element.38), channel_id=1, source_target_pairs={{0,16},{8,24},{16,0},{24,8},{1,17},{9,25},{17,1},{25,9},{2,18},{10... | collective-permute-start | bytes 393224 | tf_op jit(solution)/shard_map/ppermute | solution.py:176
  21.7 6.9 %collective-permute-start.6 = (f32[128,256]{1,0:T(8,128)S(1)}, f32[128,256]{1,0:T(8,128)S(1)}, u32[]{:S(2)}, u32[]{:S(2)}) collective-permute-start(f32[128,256]{1,0:T(8,128)S(1)} %get-tuple-element.39), channel_id=1, source_target_pairs={{0,24},{8,16},{16,8},{24,0},{1,25},{9,17},{17,9},{25,1},{2,26},{10... | collective-permute-start | bytes 393224 | tf_op jit(solution)/shard_map/ppermute | solution.py:176
  29.5 7.2 %collective-permute-start.9 = (f32[128,256]{1,0:T(8,128)S(1)}, f32[128,256]{1,0:T(8,128)S(1)}, u32[]{:S(2)}, u32[]{:S(2)}) collective-permute-start(f32[128,256]{1,0:T(8,128)S(1)} %get-tuple-element.47.refs_0_), channel_id=1, source_target_pairs={{0,24},{8,16},{16,8},{24,0},{1,25},{9,17},{17,9},{25,1},{2,26},{10... | collective-permute-start | bytes 393224 | tf_op jit(solution)/shard_map/ppermute | solution.py:176
  31.0 6.9 %collective-permute-start.8 = (f32[128,256]{1,0:T(8,128)S(1)}, f32[128,256]{1,0:T(8,128)S(1)}, u32[]{:S(2)}, u32[]{:S(2)}) collective-permute-start(f32[128,256]{1,0:T(8,128)S(1)} %get-tuple-element.47.refs_0_), channel_id=1, source_target_pairs={{0,16},{8,24},{16,0},{24,8},{1,17},{9,25},{17,1},{25,9},{2,18},{10... | collective-permute-start | bytes 393224 | tf_op jit(solution)/shard_map/ppermute | solution.py:176
  32.2 5.9 %collective-permute-start.7 = (f32[128,256]{1,0:T(8,128)S(1)}, f32[128,256]{1,0:T(8,128)S(1)}, u32[]{:S(2)}, u32[]{:S(2)}) collective-permute-start(f32[128,256]{1,0:T(8,128)S(1)} %get-tuple-element.47.refs_0_), channel_id=1, source_target_pairs={{0,8},{8,0},{16,24},{24,16},{1,9},{9,1},{17,25},{25,17},{2,10},{10... | collective-permute-start | bytes 393224 | tf_op jit(solution)/shard_map/ppermute | solution.py:176
  33.0 10.0 %collective-permute-start.14 = (f32[160,256]{1,0:T(8,128)S(1)}, f32[160,256]{1,0:T(8,128)S(1)}, u32[]{:S(2)}, u32[]{:S(2)}) collective-permute-start(f32[160,256]{1,0:T(8,128)S(1)} %get-tuple-element.53), channel_id=1, source_target_pairs={{0,1},{1,0},{2,3},{3,2},{4,5},{5,4},{6,7},{7,6},{8,9},{9,8},{10,11... | collective-permute-start | bytes 491528 | tf_op jit(solution)/shard_map/ppermute | solution.py:176
  38.5 6.4 %collective-permute-start.10 = (f32[64,256]{1,0:T(8,128)S(1)}, f32[64,256]{1,0:T(8,128)S(1)}, u32[]{:S(2)}, u32[]{:S(2)}) collective-permute-start(f32[64,256]{1,0:T(8,128)S(1)} %get-tuple-element.49), channel_id=1, source_target_pairs={{0,2},{1,3},{2,0},{3,1},{4,6},{5,7},{6,4},{7,5},{8,10},{9,11},{10,... | collective-permute-start | bytes 196616 | tf_op jit(solution)/shard_map/ppermute | solution.py:176
  38.6 9.1 %collective-permute-start.11 = (f32[64,256]{1,0:T(8,128)S(1)}, f32[64,256]{1,0:T(8,128)S(1)}, u32[]{:S(2)}, u32[]{:S(2)}) collective-permute-start(f32[64,256]{1,0:T(8,128)S(1)} %get-tuple-element.50), channel_id=1, source_target_pairs={{0,4},{1,5},{2,6},{3,7},{4,0},{5,1},{6,2},{7,3},{8,12},{9,13},{10,... | collective-permute-start | bytes 196616 | tf_op jit(solution)/shard_map/ppermute | solution.py:176
  40.9 13.7 %collective-permute-start.12 = (f32[64,256]{1,0:T(8,128)S(1)}, f32[64,256]{1,0:T(8,128)S(1)}, u32[]{:S(2)}, u32[]{:S(2)}) collective-permute-start(f32[64,256]{1,0:T(8,128)S(1)} %get-tuple-element.51), channel_id=1, source_target_pairs={{0,6},{1,7},{2,4},{3,5},{4,2},{5,3},{6,0},{7,1},{8,14},{9,15},{10,... | collective-permute-start | bytes 196616 | tf_op jit(solution)/shard_map/ppermute | solution.py:176
  43.0 6.0 %collective-permute-start.17 = (f32[40,256]{1,0:T(8,128)S(1)}, f32[40,256]{1,0:T(8,128)S(1)}, u32[]{:S(2)}, u32[]{:S(2)}) collective-permute-start(f32[40,256]{1,0:T(8,128)S(1)} %get-tuple-element.56), channel_id=1, source_target_pairs={{0,6},{1,7},{2,4},{3,5},{4,2},{5,3},{6,0},{7,1},{8,14},{9,15},{10,... | collective-permute-start | bytes 122888 | tf_op jit(solution)/shard_map/ppermute | solution.py:176
  44.9 6.1 %collective-permute-start.16 = (f32[40,256]{1,0:T(8,128)S(1)}, f32[40,256]{1,0:T(8,128)S(1)}, u32[]{:S(2)}, u32[]{:S(2)}) collective-permute-start(f32[40,256]{1,0:T(8,128)S(1)} %get-tuple-element.57), channel_id=1, source_target_pairs={{0,4},{1,5},{2,6},{3,7},{4,0},{5,1},{6,2},{7,3},{8,12},{9,13},{10,... | collective-permute-start | bytes 122888 | tf_op jit(solution)/shard_map/ppermute | solution.py:176
  44.9 6.1 %collective-permute-start.15 = (f32[40,256]{1,0:T(8,128)S(1)}, f32[40,256]{1,0:T(8,128)S(1)}, u32[]{:S(2)}, u32[]{:S(2)}) collective-permute-start(f32[40,256]{1,0:T(8,128)S(1)} %get-tuple-element.58), channel_id=1, source_target_pairs={{0,2},{1,3},{2,0},{3,1},{4,6},{5,7},{6,4},{7,5},{8,10},{9,11},{10,... | collective-permute-start | bytes 122888 | tf_op jit(solution)/shard_map/ppermute | solution.py:176
  51.0 5.3 %collective-permute-start.20 = (f32[40,256]{1,0:T(8,128)S(1)}, f32[40,256]{1,0:T(8,128)S(1)}, u32[]{:S(2)}, u32[]{:S(2)}) collective-permute-start(f32[40,256]{1,0:T(8,128)S(1)} %fusion), channel_id=1, source_target_pairs={{0,24},{8,16},{16,8},{24,0},{1,25},{9,17},{17,9},{25,1},{2,26},{10... | collective-permute-start | bytes 122888 | tf_op jit(solution)/shard_map/ppermute | solution.py:176
  52.8 4.0 %collective-permute-start.19 = (f32[40,256]{1,0:T(8,128)S(1)}, f32[40,256]{1,0:T(8,128)S(1)}, u32[]{:S(2)}, u32[]{:S(2)}) collective-permute-start(f32[40,256]{1,0:T(8,128)S(1)} %fusion), channel_id=1, source_target_pairs={{0,16},{8,24},{16,0},{24,8},{1,17},{9,25},{17,1},{25,9},{2,18},{10... | collective-permute-start | bytes 122888 | tf_op jit(solution)/shard_map/ppermute | solution.py:176
  54.4 4.0 %collective-permute-start.18 = (f32[40,256]{1,0:T(8,128)S(1)}, f32[40,256]{1,0:T(8,128)S(1)}, u32[]{:S(2)}, u32[]{:S(2)}) collective-permute-start(f32[40,256]{1,0:T(8,128)S(1)} %fusion), channel_id=1, source_target_pairs={{0,8},{8,0},{16,24},{24,16},{1,9},{9,1},{17,25},{25,17},{2,10},{10... | collective-permute-start | bytes 122888 | tf_op jit(solution)/shard_map/ppermute | solution.py:176
  58.4 5.8 %collective-permute-start.23 = (f32[32,256]{1,0:T(8,128)S(1)}, f32[32,256]{1,0:T(8,128)S(1)}, u32[]{:S(2)}, u32[]{:S(2)}) collective-permute-start(f32[32,256]{1,0:T(8,128)S(1)} %slice.100), channel_id=1, source_target_pairs={{0,6},{1,7},{2,4},{3,5},{4,2},{5,3},{6,0},{7,1},{8,14},{9,15},{10,... | collective-permute-start | bytes 98312 | tf_op jit(solution)/shard_map/ppermute | solution.py:176
  60.7 4.8 %collective-permute-start.22 = (f32[32,256]{1,0:T(8,128)S(1)}, f32[32,256]{1,0:T(8,128)S(1)}, u32[]{:S(2)}, u32[]{:S(2)}) collective-permute-start(f32[32,256]{1,0:T(8,128)S(1)} %slice.100), channel_id=1, source_target_pairs={{0,4},{1,5},{2,6},{3,7},{4,0},{5,1},{6,2},{7,3},{8,12},{9,13},{10,... | collective-permute-start | bytes 98312 | tf_op jit(solution)/shard_map/ppermute | solution.py:176
  60.8 4.8 %collective-permute-start.21 = (f32[32,256]{1,0:T(8,128)S(1)}, f32[32,256]{1,0:T(8,128)S(1)}, u32[]{:S(2)}, u32[]{:S(2)}) collective-permute-start(f32[32,256]{1,0:T(8,128)S(1)} %slice.100), channel_id=1, source_target_pairs={{0,2},{1,3},{2,0},{3,1},{4,6},{5,7},{6,4},{7,5},{8,10},{9,11},{10,... | collective-permute-start | bytes 98312 | tf_op jit(solution)/shard_map/ppermute | solution.py:176
  62.9 2.8 %collective-permute-start.13 = (f32[128,256]{1,0:T(8,128)S(1)}, f32[128,256]{1,0:T(8,128)S(1)}, u32[]{:S(2)}, u32[]{:S(2)}) collective-permute-start(f32[128,256]{1,0:T(8,128)S(1)} %pad_maximum_fusion.3), channel_id=1, source_target_pairs={{0,1},{1,0},{2,3},{3,2},{4,5},{5,4},{6,7},{7,6},{8,9},{9,8},{10,11... | collective-permute-start | bytes 393224 | tf_op jit(solution)/shard_map/ppermute | solution.py:176
  65.6 1.4 %collective-permute-start.24 = (f32[128,256]{1,0:T(8,128)S(1)}, f32[128,256]{1,0:T(8,128)S(1)}, u32[]{:S(2)}, u32[]{:S(2)}) collective-permute-start(f32[128,256]{1,0:T(8,128)S(1)} %pad_maximum_fusion.4.own_ref), channel_id=1, source_target_pairs={{0,1},{1,0},{2,3},{3,2},{4,5},{5,4},{6,7},{7,6},{8,9},{9,8},{10,11... | collective-permute-start | bytes 393224 | tf_op jit(solution)/shard_map/ppermute | solution.py:176

commit v4 on v3

--- a/solution.py
+++ b/solution.py
@@ -32,7 +32,7 @@
     return mm(a[0], b[0], dims) + (mm(a[0], b[1], dims) + mm(a[1], b[0], dims))
 
 
-def call(kernel, outs, args, scratch=(), flops=0, smem=(), hbm=(), hbm_out=()):
+def call(kernel, outs, args, scratch=(), flops=0, smem=(), hbm=()):
     out_bytes = sum(int(o.size) * o.dtype.itemsize for o in outs)
     in_bytes = sum(int(a.size) * a.dtype.itemsize for a in args)
     limit = max(FLOOR, 4 * (in_bytes + out_bytes))
@@ -45,10 +45,7 @@
             )
             for k in range(len(args))
         ],
-        out_specs=[
-            pl.BlockSpec(memory_space=pltpu.HBM if k in hbm_out else pltpu.VMEM)
-            for k in range(len(outs))
-        ],
+        out_specs=[pl.BlockSpec(memory_space=pltpu.VMEM) for _ in outs],
         scratch_shapes=list(scratch),
         cost_estimate=pl.CostEstimate(
             flops=flops, transcendentals=0, bytes_accessed=in_bytes + out_bytes
@@ -119,13 +116,13 @@
 
 def activate(groups, members, *refs):
     pieces = refs[:groups]
-    high_ref, low_ref, bias_ref, cot_ref, act_ref, grad_ref, keep_ref, send_ref, buffer = refs[groups:]
+    high_ref, low_ref, bias_ref, cot_ref, pre_ref, grad_ref, keep_ref, send_ref, buffer = refs[groups:]
     me = lax.axis_index("row")
     total = tree_sum([piece[...] for piece in pieces])
     total_split = split(total)
     pre = mm3(total_split, (high_ref[...], low_ref[...]), NN) + bias_ref[...]
     gate = jax.nn.sigmoid(pre)
-    act_ref[...] = pre * gate
+    pre_ref[...] = pre
     grad = cot_ref[...] * (gate * (1.0 + pre * (1.0 - gate)))
     grad_ref[...] = grad
     buffer[...] = mm3(total_split, split(grad), TN)
@@ -155,20 +152,19 @@
     out_ref[...] = mm3(split(proj), (high_ref[...], low_ref[...]), NT)
 
 
-def finish(members, summed_ref, own_ref, partner_ref, weight_hbm, bias_ref, sems):
+def finish(members, summed_ref, own_ref, partner_ref, weight_ref, bias_ref):
     me = lax.axis_index("row")
-    chunk = weight_hbm.shape[0] // members
-    copies = []
+    chunk = weight_ref.shape[0] // members
     for s in range(members):
         piece = partner_ref if s % 2 else own_ref
-        source = piece.at[(s // 2) * chunk : (s // 2 + 1) * chunk, :]
-        target = weight_hbm.at[rows_at(lax.bitwise_xor(me, s), chunk), :]
-        copies.append(pltpu.make_async_copy(source, target, sems.at[s]))
-    for copy in copies:
-        copy.start()
+        start = (s // 2) * chunk
+        weight_ref[rows_at(lax.bitwise_xor(me, s), chunk), :] = piece[start : start + chunk, :]
     bias_ref[...] = summed_ref[chunk : chunk + 1, :]
-    for copy in copies:
-        copy.wait()
+
+
+def emit(pre_ref, act_ref):
+    pre = pre_ref[...]
+    act_ref[...] = pre * jax.nn.sigmoid(pre)
 
 
 def exchange(value, axis, shift):
@@ -230,13 +226,14 @@
     parts = [partials[0]] + [exchange(partials[s], "rep", s) for s in range(1, groups)]
     chunk = width // members
     padded = pairs * (chunk + PAD)
-    activated, grad, keep, send = call(
+    pre, grad, keep, send = call(
         functools.partial(activate, groups, members),
         [shape(nodes), shape(nodes), shape(padded), shape(padded)],
         parts + [weight_high, weight_low, bias_here, cotangent],
         [vmem(width)],
         flops=12 * nodes * width * width,
     )
+    (activated,) = call(emit, [shape(nodes)], [pre])
     grads = [grad] + [exchange(grad, "rep", s) for s in range(1, groups)]
     backs = call(
         functools.partial(spread, groups),
@@ -266,8 +263,6 @@
         functools.partial(finish, members),
         [shape(width), shape(1)],
         [summed, own, partner],
-        [pltpu.SemaphoreType.DMA((members,))],
-        hbm_out=(0,),
     )
     return (activated, feat_grad, weight_grad, bias_grad[0])
 

time: 68.5 us -> 68.1 us (level)
    pallas_call x7 -> x8, Pallas kernels: 7.2 us -> 6.94 us  [call(): pl.pallas_call(kernel, out_shape=outs, in_specs=[pl.BlockSpec(memory_spac...]
  transfers between devices with their start and end apart: 25 -> 25, of which waited for: 16 -> 15; matrix products, arithmetic and copies ran while one was open for 0% -> 0% of each run, Pallas kernels for 5% -> 6%
where the time goes in v4:
time: 68.1 us; the launch traced here: 67.9 us
  starting transfers between devices  29.9 us (44%)
  waiting for transfers between devices  27.5 us (40%)
  Pallas kernels  6.94 us (10%)
  local copies, waits for them, and re-layouts  1.95 us (3%)
  between operations  1.52 us (2%)
    ppermute x25, starting transfers between devices, exchange(): return lax.ppermute(value, axis, [(i, i ^ shift) for i in range(size)])  29.9 us
    ppermute x25, waiting for transfers between devices, exchange(): return lax.ppermute(value, axis, [(i, i ^ shift) for i in range(size)])  27.5 us
    pallas_call x8, Pallas kernels, call(): pl.pallas_call(kernel, out_shape=outs, in_specs=[pl.BlockSpec(memory_spac...  6.94 us
    unnamed x12, local copies, waits for them, and re-layouts  1.89 us
  transfers between devices with their start and end apart: 25, of which 15 were waited for; matrix products, arithmetic and copies ran while one was open for 0% of the time, Pallas kernels for 6%

profile of v4, /device:TPU:0, one launch (start us, length us, event | category | flops | bytes accessed | tf_op | source)
XLA Modules:
  0.0 67.9 jit_solution(1736543673587829985)
XLA Ops:
  0.6 1.2 %shard_map.121 = (f32[64,256]{1,0:T(8,128)S(1)}, f32[64,256]{1,0:T(8,128)S(1)}, f32[64,256]{1,0:T(8,128)S(1)}, f32[64,256]{1,0:T(8,128)S(1)}, s32[1,256]{1,0:T(1,128)S(1)}) custom-call(s32[1,2048]{1,0:T(1,128)} %list_hbm.1, f32[128,256]{1,0:T(8,128)} %feat_hbm.1), custom_call_target="tpu_custom_call" | custom-call | bytes 402432 | tf_op jit(solution)/shard_map/pallas_call | solution.py:39
  1.8 3.1 %collective-permute-start = (f32[64,256]{1,0:T(8,128)S(1)}, f32[64,256]{1,0:T(8,128)S(1)}, u32[]{:S(2)}, u32[]{:S(2)}) collective-permute-start(f32[64,256]{1,0:T(8,128)S(1)} %get-tuple-element.33), channel_id=1, source_target_pairs={{0,2},{1,3},{2,0},{3,1},{4,6},{5,7},{6,4},{7,5},{8,10},{9,11},{10,... | collective-permute-start | bytes 196616 | tf_op jit(solution)/shard_map/ppermute | solution.py:172
  5.0 2.6 %collective-permute-start.1 = (f32[64,256]{1,0:T(8,128)S(1)}, f32[64,256]{1,0:T(8,128)S(1)}, u32[]{:S(2)}, u32[]{:S(2)}) collective-permute-start(f32[64,256]{1,0:T(8,128)S(1)} %get-tuple-element.34), channel_id=1, source_target_pairs={{0,4},{1,5},{2,6},{3,7},{4,0},{5,1},{6,2},{7,3},{8,12},{9,13},{10,... | collective-permute-start | bytes 196616 | tf_op jit(solution)/shard_map/ppermute | solution.py:172
  7.5 0.0 collective-permute-start.2
  7.6 0.0 collective-permute-done
  7.6 0.0 copy-start.1
  7.6 4.6 %collective-permute-done.1 = f32[64,256]{1,0:T(8,128)S(1)} collective-permute-done((f32[64,256]{1,0:T(8,128)S(1)}, f32[64,256]{1,0:T(8,128)S(1)}, u32[]{:S(2)}, u32[]{:S(2)}) %collective-permute-start.1) | collective-permute-done | bytes 65568 | tf_op jit(solution)/shard_map/ppermute | solution.py:172
  12.2 1.4 %collective-permute-done.2 = f32[64,256]{1,0:T(8,128)S(1)} collective-permute-done((f32[64,256]{1,0:T(8,128)S(1)}, f32[64,256]{1,0:T(8,128)S(1)}, u32[]{:S(2)}, u32[]{:S(2)}) %collective-permute-start.2) | collective-permute-done | bytes 65568 | tf_op jit(solution)/shard_map/ppermute | solution.py:172
  13.7 0.1 collective-permute-start.3
  14.4 0.0 copy-start.3
  14.4 0.0 copy-start.4
  14.4 0.6 copy-done.3
  15.1 1.2 %copy-done = f32[1,1,64,4096]{3,2,1,0:T(8,128)S(1)} copy-done((f32[1,1,64,4096]{3,2,1,0:T(8,128)S(1)}, f32[1,1,64,4096]{3,2,1,0:T(8,128)}, u32[]{:S(2)}) %copy-start) | copy-done | bytes 1048600
  16.3 1.9 %shard_map.120 = (bf16[512,256]{1,0:T(8,128)(2,1)S(1)}, bf16[512,256]{1,0:T(8,128)(2,1)S(1)}, bf16[256,512]{1,0:T(8,128)(2,1)S(1)}, bf16[256,512]{1,0:T(8,128)(2...) custom-call(s32[1,1]{1,0:T(1,128)S(6)} %copy.13.live_ref, ...), custom_call_target="tpu_custom_call" | custom-call | flops 33554432 | bytes 2624004 | tf_op jit(solution)/shard_map/pallas_call | solution.py:39
  18.2 0.0 collective-permute-done.3.partner_ref
  18.2 0.0 copy-start.2
  18.2 0.4 shard_map.122
  18.6 1.6 %collective-permute-start.4 = (f32[128,256]{1,0:T(8,128)S(1)}, f32[128,256]{1,0:T(8,128)S(1)}, u32[]{:S(2)}, u32[]{:S(2)}) collective-permute-start(f32[128,256]{1,0:T(8,128)S(1)} %get-tuple-element.37), channel_id=1, source_target_pairs={{0,8},{8,0},{16,24},{24,16},{1,9},{9,1},{17,25},{25,17},{2,10},{10... | collective-permute-start | bytes 393224 | tf_op jit(solution)/shard_map/ppermute | solution.py:172
  20.1 1.5 %collective-permute-start.5 = (f32[128,256]{1,0:T(8,128)S(1)}, f32[128,256]{1,0:T(8,128)S(1)}, u32[]{:S(2)}, u32[]{:S(2)}) collective-permute-start(f32[128,256]{1,0:T(8,128)S(1)} %get-tuple-element.38), channel_id=1, source_target_pairs={{0,16},{8,24},{16,0},{24,8},{1,17},{9,25},{17,1},{25,9},{2,18},{10... | collective-permute-start | bytes 393224 | tf_op jit(solution)/shard_map/ppermute | solution.py:172
  21.7 0.5 collective-permute-start.6
  22.1 2.8 %collective-permute-done.4.refs_1_ = f32[128,256]{1,0:T(8,128)S(1)} collective-permute-done((f32[128,256]{1,0:T(8,128)S(1)}, f32[128,256]{1,0:T(8,128)S(1)}, u32[]{:S(2)}, u32[]{:S(2)}) %collective-permute-start.4) | collective-permute-done | bytes 131104 | tf_op jit(solution)/shard_map/ppermute | solution.py:172
  25.0 3.6 %collective-permute-done.5.refs_2_ = f32[128,256]{1,0:T(8,128)S(1)} collective-permute-done((f32[128,256]{1,0:T(8,128)S(1)}, f32[128,256]{1,0:T(8,128)S(1)}, u32[]{:S(2)}, u32[]{:S(2)}) %collective-permute-start.5) | collective-permute-done | bytes 131104 | tf_op jit(solution)/shard_map/ppermute | solution.py:172
  28.6 0.0 collective-permute-done.6.refs_3_
  28.6 0.6 shard_map.123
  29.2 1.6 %collective-permute-start.9 = (f32[128,256]{1,0:T(8,128)S(1)}, f32[128,256]{1,0:T(8,128)S(1)}, u32[]{:S(2)}, u32[]{:S(2)}) collective-permute-start(f32[128,256]{1,0:T(8,128)S(1)} %get-tuple-element.47.refs_0_), channel_id=1, source_target_pairs={{0,24},{8,16},{16,8},{24,0},{1,25},{9,17},{17,9},{25,1},{2,26},{10... | collective-permute-start | bytes 393224 | tf_op jit(solution)/shard_map/ppermute | solution.py:172
  30.7 1.2 %collective-permute-start.8 = (f32[128,256]{1,0:T(8,128)S(1)}, f32[128,256]{1,0:T(8,128)S(1)}, u32[]{:S(2)}, u32[]{:S(2)}) collective-permute-start(f32[128,256]{1,0:T(8,128)S(1)} %get-tuple-element.47.refs_0_), channel_id=1, source_target_pairs={{0,16},{8,24},{16,0},{24,8},{1,17},{9,25},{17,1},{25,9},{2,18},{10... | collective-permute-start | bytes 393224 | tf_op jit(solution)/shard_map/ppermute | solution.py:172
  31.9 0.8 %collective-permute-start.7 = (f32[128,256]{1,0:T(8,128)S(1)}, f32[128,256]{1,0:T(8,128)S(1)}, u32[]{:S(2)}, u32[]{:S(2)}) collective-permute-start(f32[128,256]{1,0:T(8,128)S(1)} %get-tuple-element.47.refs_0_), channel_id=1, source_target_pairs={{0,8},{8,0},{16,24},{24,16},{1,9},{9,1},{17,25},{25,17},{2,10},{10... | collective-permute-start | bytes 393224 | tf_op jit(solution)/shard_map/ppermute | solution.py:172
  32.7 0.0 collective-permute-start.14
  32.7 3.7 %collective-permute-done.9.refs_3_ = f32[128,256]{1,0:T(8,128)S(1)} collective-permute-done((f32[128,256]{1,0:T(8,128)S(1)}, f32[128,256]{1,0:T(8,128)S(1)}, u32[]{:S(2)}, u32[]{:S(2)}) %collective-permute-start.9) | collective-permute-done | bytes 131104 | tf_op jit(solution)/shard_map/ppermute | solution.py:172
  36.4 1.2 %collective-permute-done.8.refs_2_ = f32[128,256]{1,0:T(8,128)S(1)} collective-permute-done((f32[128,256]{1,0:T(8,128)S(1)}, f32[128,256]{1,0:T(8,128)S(1)}, u32[]{:S(2)}, u32[]{:S(2)}) %collective-permute-start.8) | collective-permute-done | bytes 131104 | tf_op jit(solution)/shard_map/ppermute | solution.py:172
  37.6 0.2 collective-permute-done.7.refs_1_
  37.8 0.4 shard_map.125
  38.2 0.1 collective-permute-start.10
  38.3 2.4 %collective-permute-start.11 = (f32[64,256]{1,0:T(8,128)S(1)}, f32[64,256]{1,0:T(8,128)S(1)}, u32[]{:S(2)}, u32[]{:S(2)}) collective-permute-start(f32[64,256]{1,0:T(8,128)S(1)} %get-tuple-element.50), channel_id=1, source_target_pairs={{0,4},{1,5},{2,6},{3,7},{4,0},{5,1},{6,2},{7,3},{8,12},{9,13},{10,... | collective-permute-start | bytes 196616 | tf_op jit(solution)/shard_map/ppermute | solution.py:172
  40.7 2.0 %collective-permute-start.12 = (f32[64,256]{1,0:T(8,128)S(1)}, f32[64,256]{1,0:T(8,128)S(1)}, u32[]{:S(2)}, u32[]{:S(2)}) collective-permute-start(f32[64,256]{1,0:T(8,128)S(1)} %get-tuple-element.51), channel_id=1, source_target_pairs={{0,6},{1,7},{2,4},{3,5},{4,2},{5,3},{6,0},{7,1},{8,14},{9,15},{10,... | collective-permute-start | bytes 196616 | tf_op jit(solution)/shard_map/ppermute | solution.py:172
  42.7 0.0 collective-permute-done.14
  42.7 1.9 %collective-permute-start.17 = (f32[40,256]{1,0:T(8,128)S(1)}, f32[40,256]{1,0:T(8,128)S(1)}, u32[]{:S(2)}, u32[]{:S(2)}) collective-permute-start(f32[40,256]{1,0:T(8,128)S(1)} %get-tuple-element.56), channel_id=1, source_target_pairs={{0,6},{1,7},{2,4},{3,5},{4,2},{5,3},{6,0},{7,1},{8,14},{9,15},{10,... | collective-permute-start | bytes 122888 | tf_op jit(solution)/shard_map/ppermute | solution.py:172
  44.6 0.0 collective-permute-start.16
  44.6 0.0 collective-permute-done.10
  44.6 2.6 %collective-permute-start.15 = (f32[40,256]{1,0:T(8,128)S(1)}, f32[40,256]{1,0:T(8,128)S(1)}, u32[]{:S(2)}, u32[]{:S(2)}) collective-permute-start(f32[40,256]{1,0:T(8,128)S(1)} %get-tuple-element.58), channel_id=1, source_target_pairs={{0,2},{1,3},{2,0},{3,1},{4,6},{5,7},{6,4},{7,5},{8,10},{9,11},{10,... | collective-permute-start | bytes 122888 | tf_op jit(solution)/shard_map/ppermute | solution.py:172
  47.2 0.2 collective-permute-done.11
  47.4 1.3 %collective-permute-done.17 = f32[40,256]{1,0:T(8,128)S(1)} collective-permute-done((f32[40,256]{1,0:T(8,128)S(1)}, f32[40,256]{1,0:T(8,128)S(1)}, u32[]{:S(2)}, u32[]{:S(2)}) %collective-permute-start.17) | collective-permute-done | bytes 40992 | tf_op jit(solution)/shard_map/ppermute | solution.py:172
  48.7 2.0 %collective-permute-done.16 = f32[40,256]{1,0:T(8,128)S(1)} collective-permute-done((f32[40,256]{1,0:T(8,128)S(1)}, f32[40,256]{1,0:T(8,128)S(1)}, u32[]{:S(2)}, u32[]{:S(2)}) %collective-permute-start.16) | collective-permute-done | bytes 40992 | tf_op jit(solution)/shard_map/ppermute | solution.py:172
  50.7 0.0 collective-permute-done.15
  50.8 1.8 %collective-permute-start.20 = (f32[40,256]{1,0:T(8,128)S(1)}, f32[40,256]{1,0:T(8,128)S(1)}, u32[]{:S(2)}, u32[]{:S(2)}) collective-permute-start(f32[40,256]{1,0:T(8,128)S(1)} %fusion), channel_id=1, source_target_pairs={{0,24},{8,16},{16,8},{24,0},{1,25},{9,17},{17,9},{25,1},{2,26},{10... | collective-permute-start | bytes 122888 | tf_op jit(solution)/shard_map/ppermute | solution.py:172
  52.5 1.6 %collective-permute-start.19 = (f32[40,256]{1,0:T(8,128)S(1)}, f32[40,256]{1,0:T(8,128)S(1)}, u32[]{:S(2)}, u32[]{:S(2)}) collective-permute-start(f32[40,256]{1,0:T(8,128)S(1)} %fusion), channel_id=1, source_target_pairs={{0,16},{8,24},{16,0},{24,8},{1,17},{9,25},{17,1},{25,9},{2,18},{10... | collective-permute-start | bytes 122888 | tf_op jit(solution)/shard_map/ppermute | solution.py:172
  54.1 0.2 collective-permute-start.18
  54.3 0.0 collective-permute-done.12
  54.3 1.8 %collective-permute-done.20 = f32[40,256]{1,0:T(8,128)S(1)} collective-permute-done((f32[40,256]{1,0:T(8,128)S(1)}, f32[40,256]{1,0:T(8,128)S(1)}, u32[]{:S(2)}, u32[]{:S(2)}) %collective-permute-start.20) | collective-permute-done | bytes 40992 | tf_op jit(solution)/shard_map/ppermute | solution.py:172
  56.1 0.4 collective-permute-done.19
  56.5 1.6 %collective-permute-done.18 = f32[40,256]{1,0:T(8,128)S(1)} collective-permute-done((f32[40,256]{1,0:T(8,128)S(1)}, f32[40,256]{1,0:T(8,128)S(1)}, u32[]{:S(2)}, u32[]{:S(2)}) %collective-permute-start.18) | collective-permute-done | bytes 40992 | tf_op jit(solution)/shard_map/ppermute | solution.py:172
  58.1 2.3 %collective-permute-start.23 = (f32[32,256]{1,0:T(8,128)S(1)}, f32[32,256]{1,0:T(8,128)S(1)}, u32[]{:S(2)}, u32[]{:S(2)}) collective-permute-start(f32[32,256]{1,0:T(8,128)S(1)} %slice.100), channel_id=1, source_target_pairs={{0,6},{1,7},{2,4},{3,5},{4,2},{5,3},{6,0},{7,1},{8,14},{9,15},{10,... | collective-permute-start | bytes 98312 | tf_op jit(solution)/shard_map/ppermute | solution.py:172
  60.5 0.0 collective-permute-start.22
  60.5 2.1 %collective-permute-start.21 = (f32[32,256]{1,0:T(8,128)S(1)}, f32[32,256]{1,0:T(8,128)S(1)}, u32[]{:S(2)}, u32[]{:S(2)}) collective-permute-start(f32[32,256]{1,0:T(8,128)S(1)} %slice.100), channel_id=1, source_target_pairs={{0,2},{1,3},{2,0},{3,1},{4,6},{5,7},{6,4},{7,5},{8,10},{9,11},{10,... | collective-permute-start | bytes 98312 | tf_op jit(solution)/shard_map/ppermute | solution.py:172
  62.6 0.1 collective-permute-start.13
  62.7 1.2 %collective-permute-done.23 = f32[32,256]{1,0:T(8,128)S(1)} collective-permute-done((f32[32,256]{1,0:T(8,128)S(1)}, f32[32,256]{1,0:T(8,128)S(1)}, u32[]{:S(2)}, u32[]{:S(2)}) %collective-permute-start.23) | collective-permute-done | bytes 32800 | tf_op jit(solution)/shard_map/ppermute | solution.py:172
  63.9 1.4 %collective-permute-done.22 = f32[32,256]{1,0:T(8,128)S(1)} collective-permute-done((f32[32,256]{1,0:T(8,128)S(1)}, f32[32,256]{1,0:T(8,128)S(1)}, u32[]{:S(2)}, u32[]{:S(2)}) %collective-permute-start.22) | collective-permute-done | bytes 32800 | tf_op jit(solution)/shard_map/ppermute | solution.py:172
  65.3 0.0 collective-permute-done.21
  65.3 0.1 collective-permute-start.24
  65.4 0.7 %shard_map.124 = f32[128,256]{1,0:T(8,128)} custom-call(f32[128,256]{1,0:T(8,128)S(1)} %get-tuple-element.43.pre_ref), custom_call_target="tpu_custom_call" | custom-call | bytes 262144 | tf_op jit(solution)/shard_map/pallas_call | solution.py:39
  66.1 0.0 collective-permute-done.13.partner_ref
  66.1 1.1 %shard_map.126 = f32[128,256]{1,0:T(8,128)} custom-call(s32[1,256]{1,0:T(1,128)S(1)} %get-tuple-element.44.wanted_ref, bf16[256,256]{1,0:T(8,128)(2,1)S(1)} %get-tuple-element.40.refs_4_.high_ref, bf16[256,256]{1,0:T(8,128)(2,1)S(1)} %get-tuple-element.41.refs_5_.low_ref, f32[128,256]{1,0:T(8,128)S(1)} %pad_maximum_fusion.2.own_ref, ...), custom_call_target="tpu_custom_call" | custom-call | flops 50331648 | bytes 656384 | tf_op jit(solution)/shard_map/pallas_call | solution.py:39
  67.2 0.0 collective-permute-done.24.partner_ref
  67.2 0.7 %shard_map.127 = (f32[256,256]{1,0:T(8,128)}, f32[1,256]{1,0:T(1,128)}) custom-call(f32[40,256]{1,0:T(8,128)S(1)} %add_add_fusion.summed_ref, f32[128,256]{1,0:T(8,128)S(1)} %pad_maximum_fusion.4.own_ref, f32[128,256]{1,0:T(8,128)S(1)} %collective-permute-done.24.partner_ref), custom_call_target="tpu_custom_call" | custom-call | bytes 566272 | tf_op jit(solution)/shard_map/pallas_call | solution.py:39
  (24 shorter events, 0.2 us)
Async XLA Ops:
  1.8 5.7 %collective-permute-start = (f32[64,256]{1,0:T(8,128)S(1)}, f32[64,256]{1,0:T(8,128)S(1)}, u32[]{:S(2)}, u32[]{:S(2)}) collective-permute-start(f32[64,256]{1,0:T(8,128)S(1)} %get-tuple-element.33), channel_id=1, source_target_pairs={{0,2},{1,3},{2,0},{3,1},{4,6},{5,7},{6,4},{7,5},{8,10},{9,11},{10,... | collective-permute-start | bytes 196616 | tf_op jit(solution)/shard_map/ppermute | solution.py:172
  5.0 7.3 %collective-permute-start.1 = (f32[64,256]{1,0:T(8,128)S(1)}, f32[64,256]{1,0:T(8,128)S(1)}, u32[]{:S(2)}, u32[]{:S(2)}) collective-permute-start(f32[64,256]{1,0:T(8,128)S(1)} %get-tuple-element.34), channel_id=1, source_target_pairs={{0,4},{1,5},{2,6},{3,7},{4,0},{5,1},{6,2},{7,3},{8,12},{9,13},{10,... | collective-permute-start | bytes 196616 | tf_op jit(solution)/shard_map/ppermute | solution.py:172
  7.5 6.1 %collective-permute-start.2 = (f32[64,256]{1,0:T(8,128)S(1)}, f32[64,256]{1,0:T(8,128)S(1)}, u32[]{:S(2)}, u32[]{:S(2)}) collective-permute-start(f32[64,256]{1,0:T(8,128)S(1)} %get-tuple-element.35), channel_id=1, source_target_pairs={{0,6},{1,7},{2,4},{3,5},{4,2},{5,3},{6,0},{7,1},{8,14},{9,15},{10,... | collective-permute-start | bytes 196616 | tf_op jit(solution)/shard_map/ppermute | solution.py:172
  7.6 6.8 %copy-start.1 = (f32[256,256]{1,0:T(8,128)S(1)}, f32[256,256]{1,0:T(8,128)}, u32[]{:S(2)}) copy-start(f32[256,256]{1,0:T(8,128)} %weight_ref.1) | copy-start | bytes 786436
  13.6 0.8 %copy-start.5 = (s32[1,1,64]{2,1,0:T(1,128)S(1)}, s32[1,1,64]{2,1,0:T(1,128)}, u32[]{:S(2)}) copy-start(s32[1,1,64]{2,1,0:T(1,128)} %param.15) | copy-start | bytes 772
  13.7 4.5 %collective-permute-start.3 = (f32[128,256]{1,0:T(8,128)S(1)}, f32[128,256]{1,0:T(8,128)S(1)}, u32[]{:S(2)}, u32[]{:S(2)}) collective-permute-start(f32[128,256]{1,0:T(8,128)S(1)} %pad_maximum_fusion.1), channel_id=1, source_target_pairs={{0,1},{1,0},{2,3},{3,2},{4,5},{5,4},{6,7},{7,6},{8,9},{9,8},{10,11... | collective-permute-start | bytes 393224 | tf_op jit(solution)/shard_map/ppermute | solution.py:172
  14.4 0.7 %copy-start.3 = (f32[256]{0:T(256)S(1)}, f32[256]{0:T(256)}, u32[]{:S(2)}) copy-start(f32[256]{0:T(256)} %param.11) | copy-start | bytes 3076
  14.4 0.7 copy-start.4
  15.1 1.2 %copy-start = (f32[1,1,64,4096]{3,2,1,0:T(8,128)S(1)}, f32[1,1,64,4096]{3,2,1,0:T(8,128)}, u32[]{:S(2)}) copy-start(f32[1,1,64,4096]{3,2,1,0:T(8,128)} %param.13) | copy-start | bytes 3145732
  18.2 10.4 %copy-start.2 = (f32[128,256]{1,0:T(8,128)S(1)}, f32[128,256]{1,0:T(8,128)}, u32[]{:S(2)}) copy-start(f32[128,256]{1,0:T(8,128)} %refs_7_.1) | copy-start | bytes 393220
  18.6 6.4 %collective-permute-start.4 = (f32[128,256]{1,0:T(8,128)S(1)}, f32[128,256]{1,0:T(8,128)S(1)}, u32[]{:S(2)}, u32[]{:S(2)}) collective-permute-start(f32[128,256]{1,0:T(8,128)S(1)} %get-tuple-element.37), channel_id=1, source_target_pairs={{0,8},{8,0},{16,24},{24,16},{1,9},{9,1},{17,25},{25,17},{2,10},{10... | collective-permute-start | bytes 393224 | tf_op jit(solution)/shard_map/ppermute | solution.py:172
  20.1 8.4 %collective-permute-start.5 = (f32[128,256]{1,0:T(8,128)S(1)}, f32[128,256]{1,0:T(8,128)S(1)}, u32[]{:S(2)}, u32[]{:S(2)}) collective-permute-start(f32[128,256]{1,0:T(8,128)S(1)} %get-tuple-element.38), channel_id=1, source_target_pairs={{0,16},{8,24},{16,0},{24,8},{1,17},{9,25},{17,1},{25,9},{2,18},{10... | collective-permute-start | bytes 393224 | tf_op jit(solution)/shard_map/ppermute | solution.py:172
  21.7 6.9 %collective-permute-start.6 = (f32[128,256]{1,0:T(8,128)S(1)}, f32[128,256]{1,0:T(8,128)S(1)}, u32[]{:S(2)}, u32[]{:S(2)}) collective-permute-start(f32[128,256]{1,0:T(8,128)S(1)} %get-tuple-element.39), channel_id=1, source_target_pairs={{0,24},{8,16},{16,8},{24,0},{1,25},{9,17},{17,9},{25,1},{2,26},{10... | collective-permute-start | bytes 393224 | tf_op jit(solution)/shard_map/ppermute | solution.py:172
  29.2 7.2 %collective-permute-start.9 = (f32[128,256]{1,0:T(8,128)S(1)}, f32[128,256]{1,0:T(8,128)S(1)}, u32[]{:S(2)}, u32[]{:S(2)}) collective-permute-start(f32[128,256]{1,0:T(8,128)S(1)} %get-tuple-element.47.refs_0_), channel_id=1, source_target_pairs={{0,24},{8,16},{16,8},{24,0},{1,25},{9,17},{17,9},{25,1},{2,26},{10... | collective-permute-start | bytes 393224 | tf_op jit(solution)/shard_map/ppermute | solution.py:172
  30.7 6.9 %collective-permute-start.8 = (f32[128,256]{1,0:T(8,128)S(1)}, f32[128,256]{1,0:T(8,128)S(1)}, u32[]{:S(2)}, u32[]{:S(2)}) collective-permute-start(f32[128,256]{1,0:T(8,128)S(1)} %get-tuple-element.47.refs_0_), channel_id=1, source_target_pairs={{0,16},{8,24},{16,0},{24,8},{1,17},{9,25},{17,1},{25,9},{2,18},{10... | collective-permute-start | bytes 393224 | tf_op jit(solution)/shard_map/ppermute | solution.py:172
  31.9 5.9 %collective-permute-start.7 = (f32[128,256]{1,0:T(8,128)S(1)}, f32[128,256]{1,0:T(8,128)S(1)}, u32[]{:S(2)}, u32[]{:S(2)}) collective-permute-start(f32[128,256]{1,0:T(8,128)S(1)} %get-tuple-element.47.refs_0_), channel_id=1, source_target_pairs={{0,8},{8,0},{16,24},{24,16},{1,9},{9,1},{17,25},{25,17},{2,10},{10... | collective-permute-start | bytes 393224 | tf_op jit(solution)/shard_map/ppermute | solution.py:172
  32.7 10.0 %collective-permute-start.14 = (f32[160,256]{1,0:T(8,128)S(1)}, f32[160,256]{1,0:T(8,128)S(1)}, u32[]{:S(2)}, u32[]{:S(2)}) collective-permute-start(f32[160,256]{1,0:T(8,128)S(1)} %get-tuple-element.53), channel_id=1, source_target_pairs={{0,1},{1,0},{2,3},{3,2},{4,5},{5,4},{6,7},{7,6},{8,9},{9,8},{10,11... | collective-permute-start | bytes 491528 | tf_op jit(solution)/shard_map/ppermute | solution.py:172
  38.2 6.4 %collective-permute-start.10 = (f32[64,256]{1,0:T(8,128)S(1)}, f32[64,256]{1,0:T(8,128)S(1)}, u32[]{:S(2)}, u32[]{:S(2)}) collective-permute-start(f32[64,256]{1,0:T(8,128)S(1)} %get-tuple-element.49), channel_id=1, source_target_pairs={{0,2},{1,3},{2,0},{3,1},{4,6},{5,7},{6,4},{7,5},{8,10},{9,11},{10,... | collective-permute-start | bytes 196616 | tf_op jit(solution)/shard_map/ppermute | solution.py:172
  38.3 9.1 %collective-permute-start.11 = (f32[64,256]{1,0:T(8,128)S(1)}, f32[64,256]{1,0:T(8,128)S(1)}, u32[]{:S(2)}, u32[]{:S(2)}) collective-permute-start(f32[64,256]{1,0:T(8,128)S(1)} %get-tuple-element.50), channel_id=1, source_target_pairs={{0,4},{1,5},{2,6},{3,7},{4,0},{5,1},{6,2},{7,3},{8,12},{9,13},{10,... | collective-permute-start | bytes 196616 | tf_op jit(solution)/shard_map/ppermute | solution.py:172
  40.7 13.7 %collective-permute-start.12 = (f32[64,256]{1,0:T(8,128)S(1)}, f32[64,256]{1,0:T(8,128)S(1)}, u32[]{:S(2)}, u32[]{:S(2)}) collective-permute-start(f32[64,256]{1,0:T(8,128)S(1)} %get-tuple-element.51), channel_id=1, source_target_pairs={{0,6},{1,7},{2,4},{3,5},{4,2},{5,3},{6,0},{7,1},{8,14},{9,15},{10,... | collective-permute-start | bytes 196616 | tf_op jit(solution)/shard_map/ppermute | solution.py:172
  42.7 6.0 %collective-permute-start.17 = (f32[40,256]{1,0:T(8,128)S(1)}, f32[40,256]{1,0:T(8,128)S(1)}, u32[]{:S(2)}, u32[]{:S(2)}) collective-permute-start(f32[40,256]{1,0:T(8,128)S(1)} %get-tuple-element.56), channel_id=1, source_target_pairs={{0,6},{1,7},{2,4},{3,5},{4,2},{5,3},{6,0},{7,1},{8,14},{9,15},{10,... | collective-permute-start | bytes 122888 | tf_op jit(solution)/shard_map/ppermute | solution.py:172
  44.6 6.1 %collective-permute-start.16 = (f32[40,256]{1,0:T(8,128)S(1)}, f32[40,256]{1,0:T(8,128)S(1)}, u32[]{:S(2)}, u32[]{:S(2)}) collective-permute-start(f32[40,256]{1,0:T(8,128)S(1)} %get-tuple-element.57), channel_id=1, source_target_pairs={{0,4},{1,5},{2,6},{3,7},{4,0},{5,1},{6,2},{7,3},{8,12},{9,13},{10,... | collective-permute-start | bytes 122888 | tf_op jit(solution)/shard_map/ppermute | solution.py:172
  44.6 6.1 %collective-permute-start.15 = (f32[40,256]{1,0:T(8,128)S(1)}, f32[40,256]{1,0:T(8,128)S(1)}, u32[]{:S(2)}, u32[]{:S(2)}) collective-permute-start(f32[40,256]{1,0:T(8,128)S(1)} %get-tuple-element.58), channel_id=1, source_target_pairs={{0,2},{1,3},{2,0},{3,1},{4,6},{5,7},{6,4},{7,5},{8,10},{9,11},{10,... | collective-permute-start | bytes 122888 | tf_op jit(solution)/shard_map/ppermute | solution.py:172
  50.8 5.3 %collective-permute-start.20 = (f32[40,256]{1,0:T(8,128)S(1)}, f32[40,256]{1,0:T(8,128)S(1)}, u32[]{:S(2)}, u32[]{:S(2)}) collective-permute-start(f32[40,256]{1,0:T(8,128)S(1)} %fusion), channel_id=1, source_target_pairs={{0,24},{8,16},{16,8},{24,0},{1,25},{9,17},{17,9},{25,1},{2,26},{10... | collective-permute-start | bytes 122888 | tf_op jit(solution)/shard_map/ppermute | solution.py:172
  52.5 4.0 %collective-permute-start.19 = (f32[40,256]{1,0:T(8,128)S(1)}, f32[40,256]{1,0:T(8,128)S(1)}, u32[]{:S(2)}, u32[]{:S(2)}) collective-permute-start(f32[40,256]{1,0:T(8,128)S(1)} %fusion), channel_id=1, source_target_pairs={{0,16},{8,24},{16,0},{24,8},{1,17},{9,25},{17,1},{25,9},{2,18},{10... | collective-permute-start | bytes 122888 | tf_op jit(solution)/shard_map/ppermute | solution.py:172
  54.1 4.0 %collective-permute-start.18 = (f32[40,256]{1,0:T(8,128)S(1)}, f32[40,256]{1,0:T(8,128)S(1)}, u32[]{:S(2)}, u32[]{:S(2)}) collective-permute-start(f32[40,256]{1,0:T(8,128)S(1)} %fusion), channel_id=1, source_target_pairs={{0,8},{8,0},{16,24},{24,16},{1,9},{9,1},{17,25},{25,17},{2,10},{10... | collective-permute-start | bytes 122888 | tf_op jit(solution)/shard_map/ppermute | solution.py:172
  58.1 5.8 %collective-permute-start.23 = (f32[32,256]{1,0:T(8,128)S(1)}, f32[32,256]{1,0:T(8,128)S(1)}, u32[]{:S(2)}, u32[]{:S(2)}) collective-permute-start(f32[32,256]{1,0:T(8,128)S(1)} %slice.100), channel_id=1, source_target_pairs={{0,6},{1,7},{2,4},{3,5},{4,2},{5,3},{6,0},{7,1},{8,14},{9,15},{10,... | collective-permute-start | bytes 98312 | tf_op jit(solution)/shard_map/ppermute | solution.py:172
  60.5 4.8 %collective-permute-start.22 = (f32[32,256]{1,0:T(8,128)S(1)}, f32[32,256]{1,0:T(8,128)S(1)}, u32[]{:S(2)}, u32[]{:S(2)}) collective-permute-start(f32[32,256]{1,0:T(8,128)S(1)} %slice.100), channel_id=1, source_target_pairs={{0,4},{1,5},{2,6},{3,7},{4,0},{5,1},{6,2},{7,3},{8,12},{9,13},{10,... | collective-permute-start | bytes 98312 | tf_op jit(solution)/shard_map/ppermute | solution.py:172
  60.5 4.8 %collective-permute-start.21 = (f32[32,256]{1,0:T(8,128)S(1)}, f32[32,256]{1,0:T(8,128)S(1)}, u32[]{:S(2)}, u32[]{:S(2)}) collective-permute-start(f32[32,256]{1,0:T(8,128)S(1)} %slice.100), channel_id=1, source_target_pairs={{0,2},{1,3},{2,0},{3,1},{4,6},{5,7},{6,4},{7,5},{8,10},{9,11},{10,... | collective-permute-start | bytes 98312 | tf_op jit(solution)/shard_map/ppermute | solution.py:172
  62.6 3.5 %collective-permute-start.13 = (f32[128,256]{1,0:T(8,128)S(1)}, f32[128,256]{1,0:T(8,128)S(1)}, u32[]{:S(2)}, u32[]{:S(2)}) collective-permute-start(f32[128,256]{1,0:T(8,128)S(1)} %pad_maximum_fusion.3), channel_id=1, source_target_pairs={{0,1},{1,0},{2,3},{3,2},{4,5},{5,4},{6,7},{7,6},{8,9},{9,8},{10,11... | collective-permute-start | bytes 393224 | tf_op jit(solution)/shard_map/ppermute | solution.py:172
  65.3 1.9 %collective-permute-start.24 = (f32[128,256]{1,0:T(8,128)S(1)}, f32[128,256]{1,0:T(8,128)S(1)}, u32[]{:S(2)}, u32[]{:S(2)}) collective-permute-start(f32[128,256]{1,0:T(8,128)S(1)} %pad_maximum_fusion.4.own_ref), channel_id=1, source_target_pairs={{0,1},{1,0},{2,3},{3,2},{4,5},{5,4},{6,7},{7,6},{8,9},{9,8},{10,11... | collective-permute-start | bytes 393224 | tf_op jit(solution)/shard_map/ppermute | solution.py:172

commit v5 on v4

--- a/solution.py
+++ b/solution.py
@@ -94,11 +94,11 @@
     ]
     for copy in copies:
         copy.start()
-    for copy in copies:
-        copy.wait()
-    pick = one_hot(wanted_ref[...], feat_ref.shape[0])
+    copies[1].wait()
+    pick = one_hot(wanted_ref[...], feat_ref.shape[0]).T
+    copies[0].wait()
     high, low = split(feat_ref[...])
-    buffer[...] = mm(pick, high, TN) + mm(pick, low, TN)
+    buffer[...] = mm(pick, high, NN) + mm(pick, low, NN)
     put_pairs(outs, buffer, me, outs[0].shape[0] // 2)
 
 

time: 68.1 us -> 68.1 us (level)
  no operation moved by 1% of the time
where the time goes in v5:
time: 68.1 us; the launch traced here: 67.9 us
  starting transfers between devices  29.9 us (44%)
  waiting for transfers between devices  27.5 us (40%)
  Pallas kernels  6.9 us (10%)
  local copies, waits for them, and re-layouts  1.95 us (3%)
  between operations  1.52 us (2%)
    ppermute x25, starting transfers between devices, exchange(): return lax.ppermute(value, axis, [(i, i ^ shift) for i in range(size)])  29.9 us
    ppermute x25, waiting for transfers between devices, exchange(): return lax.ppermute(value, axis, [(i, i ^ shift) for i in range(size)])  27.5 us
    pallas_call x8, Pallas kernels, call(): pl.pallas_call(kernel, out_shape=outs, in_specs=[pl.BlockSpec(memory_spac...  6.9 us
    unnamed x12, local copies, waits for them, and re-layouts  1.89 us
  transfers between devices with their start and end apart: 25, of which 15 were waited for; matrix products, arithmetic and copies ran while one was open for 0% of the time, Pallas kernels for 6%

profile of v5, /device:TPU:0, one launch (start us, length us, event | category | flops | bytes accessed | tf_op | source)
XLA Modules:
  0.0 67.9 jit_solution(3729939921297994247)
XLA Ops:
  0.6 1.2 %shard_map.121 = (f32[64,256]{1,0:T(8,128)S(1)}, f32[64,256]{1,0:T(8,128)S(1)}, f32[64,256]{1,0:T(8,128)S(1)}, f32[64,256]{1,0:T(8,128)S(1)}, s32[1,256]{1,0:T(1,128)S(1)}) custom-call(s32[1,2048]{1,0:T(1,128)} %list_hbm.1, f32[128,256]{1,0:T(8,128)} %feat_hbm.1), custom_call_target="tpu_custom_call" | custom-call | bytes 402432 | tf_op jit(solution)/shard_map/pallas_call | solution.py:39
  1.8 3.1 %collective-permute-start = (f32[64,256]{1,0:T(8,128)S(1)}, f32[64,256]{1,0:T(8,128)S(1)}, u32[]{:S(2)}, u32[]{:S(2)}) collective-permute-start(f32[64,256]{1,0:T(8,128)S(1)} %get-tuple-element.33), channel_id=1, source_target_pairs={{0,2},{1,3},{2,0},{3,1},{4,6},{5,7},{6,4},{7,5},{8,10},{9,11},{10,... | collective-permute-start | bytes 196616 | tf_op jit(solution)/shard_map/ppermute | solution.py:172
  4.9 2.6 %collective-permute-start.1 = (f32[64,256]{1,0:T(8,128)S(1)}, f32[64,256]{1,0:T(8,128)S(1)}, u32[]{:S(2)}, u32[]{:S(2)}) collective-permute-start(f32[64,256]{1,0:T(8,128)S(1)} %get-tuple-element.34), channel_id=1, source_target_pairs={{0,4},{1,5},{2,6},{3,7},{4,0},{5,1},{6,2},{7,3},{8,12},{9,13},{10,... | collective-permute-start | bytes 196616 | tf_op jit(solution)/shard_map/ppermute | solution.py:172
  7.5 0.0 collective-permute-start.2
  7.5 0.0 collective-permute-done
  7.5 0.0 copy-start.1
  7.6 4.6 %collective-permute-done.1 = f32[64,256]{1,0:T(8,128)S(1)} collective-permute-done((f32[64,256]{1,0:T(8,128)S(1)}, f32[64,256]{1,0:T(8,128)S(1)}, u32[]{:S(2)}, u32[]{:S(2)}) %collective-permute-start.1) | collective-permute-done | bytes 65568 | tf_op jit(solution)/shard_map/ppermute | solution.py:172
  12.2 1.4 %collective-permute-done.2 = f32[64,256]{1,0:T(8,128)S(1)} collective-permute-done((f32[64,256]{1,0:T(8,128)S(1)}, f32[64,256]{1,0:T(8,128)S(1)}, u32[]{:S(2)}, u32[]{:S(2)}) %collective-permute-start.2) | collective-permute-done | bytes 65568 | tf_op jit(solution)/shard_map/ppermute | solution.py:172
  13.6 0.1 collective-permute-start.3
  14.3 0.0 copy-start.3
  14.3 0.0 copy-start.4
  14.4 0.6 copy-done.3
  15.0 1.2 %copy-done = f32[1,1,64,4096]{3,2,1,0:T(8,128)S(1)} copy-done((f32[1,1,64,4096]{3,2,1,0:T(8,128)S(1)}, f32[1,1,64,4096]{3,2,1,0:T(8,128)}, u32[]{:S(2)}) %copy-start) | copy-done | bytes 1048600
  16.2 1.9 %shard_map.120 = (bf16[512,256]{1,0:T(8,128)(2,1)S(1)}, bf16[512,256]{1,0:T(8,128)(2,1)S(1)}, bf16[256,512]{1,0:T(8,128)(2,1)S(1)}, bf16[256,512]{1,0:T(8,128)(2...) custom-call(s32[1,1]{1,0:T(1,128)S(6)} %copy.13.live_ref, ...), custom_call_target="tpu_custom_call" | custom-call | flops 33554432 | bytes 2624004 | tf_op jit(solution)/shard_map/pallas_call | solution.py:39
  18.1 0.0 collective-permute-done.3.partner_ref
  18.1 0.0 copy-start.2
  18.2 0.4 shard_map.122
  18.5 1.6 %collective-permute-start.4 = (f32[128,256]{1,0:T(8,128)S(1)}, f32[128,256]{1,0:T(8,128)S(1)}, u32[]{:S(2)}, u32[]{:S(2)}) collective-permute-start(f32[128,256]{1,0:T(8,128)S(1)} %get-tuple-element.37), channel_id=1, source_target_pairs={{0,8},{8,0},{16,24},{24,16},{1,9},{9,1},{17,25},{25,17},{2,10},{10... | collective-permute-start | bytes 393224 | tf_op jit(solution)/shard_map/ppermute | solution.py:172
  20.1 1.5 %collective-permute-start.5 = (f32[128,256]{1,0:T(8,128)S(1)}, f32[128,256]{1,0:T(8,128)S(1)}, u32[]{:S(2)}, u32[]{:S(2)}) collective-permute-start(f32[128,256]{1,0:T(8,128)S(1)} %get-tuple-element.38), channel_id=1, source_target_pairs={{0,16},{8,24},{16,0},{24,8},{1,17},{9,25},{17,1},{25,9},{2,18},{10... | collective-permute-start | bytes 393224 | tf_op jit(solution)/shard_map/ppermute | solution.py:172
  21.6 0.5 collective-permute-start.6
  22.1 2.8 %collective-permute-done.4.refs_1_ = f32[128,256]{1,0:T(8,128)S(1)} collective-permute-done((f32[128,256]{1,0:T(8,128)S(1)}, f32[128,256]{1,0:T(8,128)S(1)}, u32[]{:S(2)}, u32[]{:S(2)}) %collective-permute-start.4) | collective-permute-done | bytes 131104 | tf_op jit(solution)/shard_map/ppermute | solution.py:172
  24.9 3.6 %collective-permute-done.5.refs_2_ = f32[128,256]{1,0:T(8,128)S(1)} collective-permute-done((f32[128,256]{1,0:T(8,128)S(1)}, f32[128,256]{1,0:T(8,128)S(1)}, u32[]{:S(2)}, u32[]{:S(2)}) %collective-permute-start.5) | collective-permute-done | bytes 131104 | tf_op jit(solution)/shard_map/ppermute | solution.py:172
  28.5 0.0 collective-permute-done.6.refs_3_
  28.5 0.6 shard_map.123
  29.1 1.6 %collective-permute-start.9 = (f32[128,256]{1,0:T(8,128)S(1)}, f32[128,256]{1,0:T(8,128)S(1)}, u32[]{:S(2)}, u32[]{:S(2)}) collective-permute-start(f32[128,256]{1,0:T(8,128)S(1)} %get-tuple-element.47.refs_0_), channel_id=1, source_target_pairs={{0,24},{8,16},{16,8},{24,0},{1,25},{9,17},{17,9},{25,1},{2,26},{10... | collective-permute-start | bytes 393224 | tf_op jit(solution)/shard_map/ppermute | solution.py:172
  30.7 1.2 %collective-permute-start.8 = (f32[128,256]{1,0:T(8,128)S(1)}, f32[128,256]{1,0:T(8,128)S(1)}, u32[]{:S(2)}, u32[]{:S(2)}) collective-permute-start(f32[128,256]{1,0:T(8,128)S(1)} %get-tuple-element.47.refs_0_), channel_id=1, source_target_pairs={{0,16},{8,24},{16,0},{24,8},{1,17},{9,25},{17,1},{25,9},{2,18},{10... | collective-permute-start | bytes 393224 | tf_op jit(solution)/shard_map/ppermute | solution.py:172
  31.9 0.8 %collective-permute-start.7 = (f32[128,256]{1,0:T(8,128)S(1)}, f32[128,256]{1,0:T(8,128)S(1)}, u32[]{:S(2)}, u32[]{:S(2)}) collective-permute-start(f32[128,256]{1,0:T(8,128)S(1)} %get-tuple-element.47.refs_0_), channel_id=1, source_target_pairs={{0,8},{8,0},{16,24},{24,16},{1,9},{9,1},{17,25},{25,17},{2,10},{10... | collective-permute-start | bytes 393224 | tf_op jit(solution)/shard_map/ppermute | solution.py:172
  32.7 0.0 collective-permute-start.14
  32.7 3.7 %collective-permute-done.9.refs_3_ = f32[128,256]{1,0:T(8,128)S(1)} collective-permute-done((f32[128,256]{1,0:T(8,128)S(1)}, f32[128,256]{1,0:T(8,128)S(1)}, u32[]{:S(2)}, u32[]{:S(2)}) %collective-permute-start.9) | collective-permute-done | bytes 131104 | tf_op jit(solution)/shard_map/ppermute | solution.py:172
  36.4 1.2 %collective-permute-done.8.refs_2_ = f32[128,256]{1,0:T(8,128)S(1)} collective-permute-done((f32[128,256]{1,0:T(8,128)S(1)}, f32[128,256]{1,0:T(8,128)S(1)}, u32[]{:S(2)}, u32[]{:S(2)}) %collective-permute-start.8) | collective-permute-done | bytes 131104 | tf_op jit(solution)/shard_map/ppermute | solution.py:172
  37.6 0.2 collective-permute-done.7.refs_1_
  37.8 0.4 shard_map.125
  38.2 0.1 collective-permute-start.10
  38.3 2.4 %collective-permute-start.11 = (f32[64,256]{1,0:T(8,128)S(1)}, f32[64,256]{1,0:T(8,128)S(1)}, u32[]{:S(2)}, u32[]{:S(2)}) collective-permute-start(f32[64,256]{1,0:T(8,128)S(1)} %get-tuple-element.50), channel_id=1, source_target_pairs={{0,4},{1,5},{2,6},{3,7},{4,0},{5,1},{6,2},{7,3},{8,12},{9,13},{10,... | collective-permute-start | bytes 196616 | tf_op jit(solution)/shard_map/ppermute | solution.py:172
  40.6 2.0 %collective-permute-start.12 = (f32[64,256]{1,0:T(8,128)S(1)}, f32[64,256]{1,0:T(8,128)S(1)}, u32[]{:S(2)}, u32[]{:S(2)}) collective-permute-start(f32[64,256]{1,0:T(8,128)S(1)} %get-tuple-element.51), channel_id=1, source_target_pairs={{0,6},{1,7},{2,4},{3,5},{4,2},{5,3},{6,0},{7,1},{8,14},{9,15},{10,... | collective-permute-start | bytes 196616 | tf_op jit(solution)/shard_map/ppermute | solution.py:172
  42.6 0.0 collective-permute-done.14
  42.7 1.9 %collective-permute-start.17 = (f32[40,256]{1,0:T(8,128)S(1)}, f32[40,256]{1,0:T(8,128)S(1)}, u32[]{:S(2)}, u32[]{:S(2)}) collective-permute-start(f32[40,256]{1,0:T(8,128)S(1)} %get-tuple-element.56), channel_id=1, source_target_pairs={{0,6},{1,7},{2,4},{3,5},{4,2},{5,3},{6,0},{7,1},{8,14},{9,15},{10,... | collective-permute-start | bytes 122888 | tf_op jit(solution)/shard_map/ppermute | solution.py:172
  44.6 0.0 collective-permute-start.16
  44.6 0.0 collective-permute-done.10
  44.6 2.6 %collective-permute-start.15 = (f32[40,256]{1,0:T(8,128)S(1)}, f32[40,256]{1,0:T(8,128)S(1)}, u32[]{:S(2)}, u32[]{:S(2)}) collective-permute-start(f32[40,256]{1,0:T(8,128)S(1)} %get-tuple-element.58), channel_id=1, source_target_pairs={{0,2},{1,3},{2,0},{3,1},{4,6},{5,7},{6,4},{7,5},{8,10},{9,11},{10,... | collective-permute-start | bytes 122888 | tf_op jit(solution)/shard_map/ppermute | solution.py:172
  47.2 0.2 collective-permute-done.11
  47.4 1.3 %collective-permute-done.17 = f32[40,256]{1,0:T(8,128)S(1)} collective-permute-done((f32[40,256]{1,0:T(8,128)S(1)}, f32[40,256]{1,0:T(8,128)S(1)}, u32[]{:S(2)}, u32[]{:S(2)}) %collective-permute-start.17) | collective-permute-done | bytes 40992 | tf_op jit(solution)/shard_map/ppermute | solution.py:172
  48.7 2.0 %collective-permute-done.16 = f32[40,256]{1,0:T(8,128)S(1)} collective-permute-done((f32[40,256]{1,0:T(8,128)S(1)}, f32[40,256]{1,0:T(8,128)S(1)}, u32[]{:S(2)}, u32[]{:S(2)}) %collective-permute-start.16) | collective-permute-done | bytes 40992 | tf_op jit(solution)/shard_map/ppermute | solution.py:172
  50.7 0.0 collective-permute-done.15
  50.7 1.8 %collective-permute-start.20 = (f32[40,256]{1,0:T(8,128)S(1)}, f32[40,256]{1,0:T(8,128)S(1)}, u32[]{:S(2)}, u32[]{:S(2)}) collective-permute-start(f32[40,256]{1,0:T(8,128)S(1)} %fusion), channel_id=1, source_target_pairs={{0,24},{8,16},{16,8},{24,0},{1,25},{9,17},{17,9},{25,1},{2,26},{10... | collective-permute-start | bytes 122888 | tf_op jit(solution)/shard_map/ppermute | solution.py:172
  52.5 1.6 %collective-permute-start.19 = (f32[40,256]{1,0:T(8,128)S(1)}, f32[40,256]{1,0:T(8,128)S(1)}, u32[]{:S(2)}, u32[]{:S(2)}) collective-permute-start(f32[40,256]{1,0:T(8,128)S(1)} %fusion), channel_id=1, source_target_pairs={{0,16},{8,24},{16,0},{24,8},{1,17},{9,25},{17,1},{25,9},{2,18},{10... | collective-permute-start | bytes 122888 | tf_op jit(solution)/shard_map/ppermute | solution.py:172
  54.1 0.2 collective-permute-start.18
  54.3 0.0 collective-permute-done.12
  54.3 1.8 %collective-permute-done.20 = f32[40,256]{1,0:T(8,128)S(1)} collective-permute-done((f32[40,256]{1,0:T(8,128)S(1)}, f32[40,256]{1,0:T(8,128)S(1)}, u32[]{:S(2)}, u32[]{:S(2)}) %collective-permute-start.20) | collective-permute-done | bytes 40992 | tf_op jit(solution)/shard_map/ppermute | solution.py:172
  56.0 0.4 collective-permute-done.19
  56.5 1.6 %collective-permute-done.18 = f32[40,256]{1,0:T(8,128)S(1)} collective-permute-done((f32[40,256]{1,0:T(8,128)S(1)}, f32[40,256]{1,0:T(8,128)S(1)}, u32[]{:S(2)}, u32[]{:S(2)}) %collective-permute-start.18) | collective-permute-done | bytes 40992 | tf_op jit(solution)/shard_map/ppermute | solution.py:172
  58.1 2.3 %collective-permute-start.23 = (f32[32,256]{1,0:T(8,128)S(1)}, f32[32,256]{1,0:T(8,128)S(1)}, u32[]{:S(2)}, u32[]{:S(2)}) collective-permute-start(f32[32,256]{1,0:T(8,128)S(1)} %slice.100), channel_id=1, source_target_pairs={{0,6},{1,7},{2,4},{3,5},{4,2},{5,3},{6,0},{7,1},{8,14},{9,15},{10,... | collective-permute-start | bytes 98312 | tf_op jit(solution)/shard_map/ppermute | solution.py:172
  60.4 0.0 collective-permute-start.22
  60.4 2.1 %collective-permute-start.21 = (f32[32,256]{1,0:T(8,128)S(1)}, f32[32,256]{1,0:T(8,128)S(1)}, u32[]{:S(2)}, u32[]{:S(2)}) collective-permute-start(f32[32,256]{1,0:T(8,128)S(1)} %slice.100), channel_id=1, source_target_pairs={{0,2},{1,3},{2,0},{3,1},{4,6},{5,7},{6,4},{7,5},{8,10},{9,11},{10,... | collective-permute-start | bytes 98312 | tf_op jit(solution)/shard_map/ppermute | solution.py:172
  62.6 0.1 collective-permute-start.13
  62.6 1.2 %collective-permute-done.23 = f32[32,256]{1,0:T(8,128)S(1)} collective-permute-done((f32[32,256]{1,0:T(8,128)S(1)}, f32[32,256]{1,0:T(8,128)S(1)}, u32[]{:S(2)}, u32[]{:S(2)}) %collective-permute-start.23) | collective-permute-done | bytes 32800 | tf_op jit(solution)/shard_map/ppermute | solution.py:172
  63.9 1.4 %collective-permute-done.22 = f32[32,256]{1,0:T(8,128)S(1)} collective-permute-done((f32[32,256]{1,0:T(8,128)S(1)}, f32[32,256]{1,0:T(8,128)S(1)}, u32[]{:S(2)}, u32[]{:S(2)}) %collective-permute-start.22) | collective-permute-done | bytes 32800 | tf_op jit(solution)/shard_map/ppermute | solution.py:172
  65.2 0.0 collective-permute-done.21
  65.3 0.1 collective-permute-start.24
  65.3 0.7 %shard_map.124 = f32[128,256]{1,0:T(8,128)} custom-call(f32[128,256]{1,0:T(8,128)S(1)} %get-tuple-element.43.pre_ref), custom_call_target="tpu_custom_call" | custom-call | bytes 262144 | tf_op jit(solution)/shard_map/pallas_call | solution.py:39
  66.0 0.0 collective-permute-done.13.partner_ref
  66.1 1.1 %shard_map.126 = f32[128,256]{1,0:T(8,128)} custom-call(s32[1,256]{1,0:T(1,128)S(1)} %get-tuple-element.44.wanted_ref, bf16[256,256]{1,0:T(8,128)(2,1)S(1)} %get-tuple-element.40.refs_4_.high_ref, bf16[256,256]{1,0:T(8,128)(2,1)S(1)} %get-tuple-element.41.refs_5_.low_ref, f32[128,256]{1,0:T(8,128)S(1)} %pad_maximum_fusion.2.own_ref, ...), custom_call_target="tpu_custom_call" | custom-call | flops 50331648 | bytes 656384 | tf_op jit(solution)/shard_map/pallas_call | solution.py:39
  67.2 0.0 collective-permute-done.24.partner_ref
  67.2 0.7 %shard_map.127 = (f32[256,256]{1,0:T(8,128)}, f32[1,256]{1,0:T(1,128)}) custom-call(f32[40,256]{1,0:T(8,128)S(1)} %add_add_fusion.summed_ref, f32[128,256]{1,0:T(8,128)S(1)} %pad_maximum_fusion.4.own_ref, f32[128,256]{1,0:T(8,128)S(1)} %collective-permute-done.24.partner_ref), custom_call_target="tpu_custom_call" | custom-call | bytes 566272 | tf_op jit(solution)/shard_map/pallas_call | solution.py:39
  (24 shorter events, 0.2 us)
Async XLA Ops:
  1.8 5.7 %collective-permute-start = (f32[64,256]{1,0:T(8,128)S(1)}, f32[64,256]{1,0:T(8,128)S(1)}, u32[]{:S(2)}, u32[]{:S(2)}) collective-permute-start(f32[64,256]{1,0:T(8,128)S(1)} %get-tuple-element.33), channel_id=1, source_target_pairs={{0,2},{1,3},{2,0},{3,1},{4,6},{5,7},{6,4},{7,5},{8,10},{9,11},{10,... | collective-permute-start | bytes 196616 | tf_op jit(solution)/shard_map/ppermute | solution.py:172
  4.9 7.3 %collective-permute-start.1 = (f32[64,256]{1,0:T(8,128)S(1)}, f32[64,256]{1,0:T(8,128)S(1)}, u32[]{:S(2)}, u32[]{:S(2)}) collective-permute-start(f32[64,256]{1,0:T(8,128)S(1)} %get-tuple-element.34), channel_id=1, source_target_pairs={{0,4},{1,5},{2,6},{3,7},{4,0},{5,1},{6,2},{7,3},{8,12},{9,13},{10,... | collective-permute-start | bytes 196616 | tf_op jit(solution)/shard_map/ppermute | solution.py:172
  7.5 6.1 %collective-permute-start.2 = (f32[64,256]{1,0:T(8,128)S(1)}, f32[64,256]{1,0:T(8,128)S(1)}, u32[]{:S(2)}, u32[]{:S(2)}) collective-permute-start(f32[64,256]{1,0:T(8,128)S(1)} %get-tuple-element.35), channel_id=1, source_target_pairs={{0,6},{1,7},{2,4},{3,5},{4,2},{5,3},{6,0},{7,1},{8,14},{9,15},{10,... | collective-permute-start | bytes 196616 | tf_op jit(solution)/shard_map/ppermute | solution.py:172
  7.5 6.8 %copy-start.1 = (f32[256,256]{1,0:T(8,128)S(1)}, f32[256,256]{1,0:T(8,128)}, u32[]{:S(2)}) copy-start(f32[256,256]{1,0:T(8,128)} %weight_ref.1) | copy-start | bytes 786436
  13.6 0.8 %copy-start.5 = (s32[1,1,64]{2,1,0:T(1,128)S(1)}, s32[1,1,64]{2,1,0:T(1,128)}, u32[]{:S(2)}) copy-start(s32[1,1,64]{2,1,0:T(1,128)} %param.15) | copy-start | bytes 772
  13.6 4.5 %collective-permute-start.3 = (f32[128,256]{1,0:T(8,128)S(1)}, f32[128,256]{1,0:T(8,128)S(1)}, u32[]{:S(2)}, u32[]{:S(2)}) collective-permute-start(f32[128,256]{1,0:T(8,128)S(1)} %pad_maximum_fusion.1), channel_id=1, source_target_pairs={{0,1},{1,0},{2,3},{3,2},{4,5},{5,4},{6,7},{7,6},{8,9},{9,8},{10,11... | collective-permute-start | bytes 393224 | tf_op jit(solution)/shard_map/ppermute | solution.py:172
  14.3 0.7 %copy-start.3 = (f32[256]{0:T(256)S(1)}, f32[256]{0:T(256)}, u32[]{:S(2)}) copy-start(f32[256]{0:T(256)} %param.11) | copy-start | bytes 3076
  14.3 0.7 copy-start.4
  15.0 1.2 %copy-start = (f32[1,1,64,4096]{3,2,1,0:T(8,128)S(1)}, f32[1,1,64,4096]{3,2,1,0:T(8,128)}, u32[]{:S(2)}) copy-start(f32[1,1,64,4096]{3,2,1,0:T(8,128)} %param.13) | copy-start | bytes 3145732
  18.1 10.4 %copy-start.2 = (f32[128,256]{1,0:T(8,128)S(1)}, f32[128,256]{1,0:T(8,128)}, u32[]{:S(2)}) copy-start(f32[128,256]{1,0:T(8,128)} %refs_7_.1) | copy-start | bytes 393220
  18.5 6.4 %collective-permute-start.4 = (f32[128,256]{1,0:T(8,128)S(1)}, f32[128,256]{1,0:T(8,128)S(1)}, u32[]{:S(2)}, u32[]{:S(2)}) collective-permute-start(f32[128,256]{1,0:T(8,128)S(1)} %get-tuple-element.37), channel_id=1, source_target_pairs={{0,8},{8,0},{16,24},{24,16},{1,9},{9,1},{17,25},{25,17},{2,10},{10... | collective-permute-start | bytes 393224 | tf_op jit(solution)/shard_map/ppermute | solution.py:172
  20.1 8.4 %collective-permute-start.5 = (f32[128,256]{1,0:T(8,128)S(1)}, f32[128,256]{1,0:T(8,128)S(1)}, u32[]{:S(2)}, u32[]{:S(2)}) collective-permute-start(f32[128,256]{1,0:T(8,128)S(1)} %get-tuple-element.38), channel_id=1, source_target_pairs={{0,16},{8,24},{16,0},{24,8},{1,17},{9,25},{17,1},{25,9},{2,18},{10... | collective-permute-start | bytes 393224 | tf_op jit(solution)/shard_map/ppermute | solution.py:172
  21.6 6.9 %collective-permute-start.6 = (f32[128,256]{1,0:T(8,128)S(1)}, f32[128,256]{1,0:T(8,128)S(1)}, u32[]{:S(2)}, u32[]{:S(2)}) collective-permute-start(f32[128,256]{1,0:T(8,128)S(1)} %get-tuple-element.39), channel_id=1, source_target_pairs={{0,24},{8,16},{16,8},{24,0},{1,25},{9,17},{17,9},{25,1},{2,26},{10... | collective-permute-start | bytes 393224 | tf_op jit(solution)/shard_map/ppermute | solution.py:172
  29.1 7.2 %collective-permute-start.9 = (f32[128,256]{1,0:T(8,128)S(1)}, f32[128,256]{1,0:T(8,128)S(1)}, u32[]{:S(2)}, u32[]{:S(2)}) collective-permute-start(f32[128,256]{1,0:T(8,128)S(1)} %get-tuple-element.47.refs_0_), channel_id=1, source_target_pairs={{0,24},{8,16},{16,8},{24,0},{1,25},{9,17},{17,9},{25,1},{2,26},{10... | collective-permute-start | bytes 393224 | tf_op jit(solution)/shard_map/ppermute | solution.py:172
  30.7 6.9 %collective-permute-start.8 = (f32[128,256]{1,0:T(8,128)S(1)}, f32[128,256]{1,0:T(8,128)S(1)}, u32[]{:S(2)}, u32[]{:S(2)}) collective-permute-start(f32[128,256]{1,0:T(8,128)S(1)} %get-tuple-element.47.refs_0_), channel_id=1, source_target_pairs={{0,16},{8,24},{16,0},{24,8},{1,17},{9,25},{17,1},{25,9},{2,18},{10... | collective-permute-start | bytes 393224 | tf_op jit(solution)/shard_map/ppermute | solution.py:172
  31.9 5.9 %collective-permute-start.7 = (f32[128,256]{1,0:T(8,128)S(1)}, f32[128,256]{1,0:T(8,128)S(1)}, u32[]{:S(2)}, u32[]{:S(2)}) collective-permute-start(f32[128,256]{1,0:T(8,128)S(1)} %get-tuple-element.47.refs_0_), channel_id=1, source_target_pairs={{0,8},{8,0},{16,24},{24,16},{1,9},{9,1},{17,25},{25,17},{2,10},{10... | collective-permute-start | bytes 393224 | tf_op jit(solution)/shard_map/ppermute | solution.py:172
  32.7 10.0 %collective-permute-start.14 = (f32[160,256]{1,0:T(8,128)S(1)}, f32[160,256]{1,0:T(8,128)S(1)}, u32[]{:S(2)}, u32[]{:S(2)}) collective-permute-start(f32[160,256]{1,0:T(8,128)S(1)} %get-tuple-element.53), channel_id=1, source_target_pairs={{0,1},{1,0},{2,3},{3,2},{4,5},{5,4},{6,7},{7,6},{8,9},{9,8},{10,11... | collective-permute-start | bytes 491528 | tf_op jit(solution)/shard_map/ppermute | solution.py:172
  38.2 6.4 %collective-permute-start.10 = (f32[64,256]{1,0:T(8,128)S(1)}, f32[64,256]{1,0:T(8,128)S(1)}, u32[]{:S(2)}, u32[]{:S(2)}) collective-permute-start(f32[64,256]{1,0:T(8,128)S(1)} %get-tuple-element.49), channel_id=1, source_target_pairs={{0,2},{1,3},{2,0},{3,1},{4,6},{5,7},{6,4},{7,5},{8,10},{9,11},{10,... | collective-permute-start | bytes 196616 | tf_op jit(solution)/shard_map/ppermute | solution.py:172
  38.3 9.1 %collective-permute-start.11 = (f32[64,256]{1,0:T(8,128)S(1)}, f32[64,256]{1,0:T(8,128)S(1)}, u32[]{:S(2)}, u32[]{:S(2)}) collective-permute-start(f32[64,256]{1,0:T(8,128)S(1)} %get-tuple-element.50), channel_id=1, source_target_pairs={{0,4},{1,5},{2,6},{3,7},{4,0},{5,1},{6,2},{7,3},{8,12},{9,13},{10,... | collective-permute-start | bytes 196616 | tf_op jit(solution)/shard_map/ppermute | solution.py:172
  40.6 13.7 %collective-permute-start.12 = (f32[64,256]{1,0:T(8,128)S(1)}, f32[64,256]{1,0:T(8,128)S(1)}, u32[]{:S(2)}, u32[]{:S(2)}) collective-permute-start(f32[64,256]{1,0:T(8,128)S(1)} %get-tuple-element.51), channel_id=1, source_target_pairs={{0,6},{1,7},{2,4},{3,5},{4,2},{5,3},{6,0},{7,1},{8,14},{9,15},{10,... | collective-permute-start | bytes 196616 | tf_op jit(solution)/shard_map/ppermute | solution.py:172
  42.7 6.0 %collective-permute-start.17 = (f32[40,256]{1,0:T(8,128)S(1)}, f32[40,256]{1,0:T(8,128)S(1)}, u32[]{:S(2)}, u32[]{:S(2)}) collective-permute-start(f32[40,256]{1,0:T(8,128)S(1)} %get-tuple-element.56), channel_id=1, source_target_pairs={{0,6},{1,7},{2,4},{3,5},{4,2},{5,3},{6,0},{7,1},{8,14},{9,15},{10,... | collective-permute-start | bytes 122888 | tf_op jit(solution)/shard_map/ppermute | solution.py:172
  44.6 6.1 %collective-permute-start.16 = (f32[40,256]{1,0:T(8,128)S(1)}, f32[40,256]{1,0:T(8,128)S(1)}, u32[]{:S(2)}, u32[]{:S(2)}) collective-permute-start(f32[40,256]{1,0:T(8,128)S(1)} %get-tuple-element.57), channel_id=1, source_target_pairs={{0,4},{1,5},{2,6},{3,7},{4,0},{5,1},{6,2},{7,3},{8,12},{9,13},{10,... | collective-permute-start | bytes 122888 | tf_op jit(solution)/shard_map/ppermute | solution.py:172
  44.6 6.1 %collective-permute-start.15 = (f32[40,256]{1,0:T(8,128)S(1)}, f32[40,256]{1,0:T(8,128)S(1)}, u32[]{:S(2)}, u32[]{:S(2)}) collective-permute-start(f32[40,256]{1,0:T(8,128)S(1)} %get-tuple-element.58), channel_id=1, source_target_pairs={{0,2},{1,3},{2,0},{3,1},{4,6},{5,7},{6,4},{7,5},{8,10},{9,11},{10,... | collective-permute-start | bytes 122888 | tf_op jit(solution)/shard_map/ppermute | solution.py:172
  50.7 5.3 %collective-permute-start.20 = (f32[40,256]{1,0:T(8,128)S(1)}, f32[40,256]{1,0:T(8,128)S(1)}, u32[]{:S(2)}, u32[]{:S(2)}) collective-permute-start(f32[40,256]{1,0:T(8,128)S(1)} %fusion), channel_id=1, source_target_pairs={{0,24},{8,16},{16,8},{24,0},{1,25},{9,17},{17,9},{25,1},{2,26},{10... | collective-permute-start | bytes 122888 | tf_op jit(solution)/shard_map/ppermute | solution.py:172
  52.5 4.0 %collective-permute-start.19 = (f32[40,256]{1,0:T(8,128)S(1)}, f32[40,256]{1,0:T(8,128)S(1)}, u32[]{:S(2)}, u32[]{:S(2)}) collective-permute-start(f32[40,256]{1,0:T(8,128)S(1)} %fusion), channel_id=1, source_target_pairs={{0,16},{8,24},{16,0},{24,8},{1,17},{9,25},{17,1},{25,9},{2,18},{10... | collective-permute-start | bytes 122888 | tf_op jit(solution)/shard_map/ppermute | solution.py:172
  54.1 4.0 %collective-permute-start.18 = (f32[40,256]{1,0:T(8,128)S(1)}, f32[40,256]{1,0:T(8,128)S(1)}, u32[]{:S(2)}, u32[]{:S(2)}) collective-permute-start(f32[40,256]{1,0:T(8,128)S(1)} %fusion), channel_id=1, source_target_pairs={{0,8},{8,0},{16,24},{24,16},{1,9},{9,1},{17,25},{25,17},{2,10},{10... | collective-permute-start | bytes 122888 | tf_op jit(solution)/shard_map/ppermute | solution.py:172
  58.1 5.8 %collective-permute-start.23 = (f32[32,256]{1,0:T(8,128)S(1)}, f32[32,256]{1,0:T(8,128)S(1)}, u32[]{:S(2)}, u32[]{:S(2)}) collective-permute-start(f32[32,256]{1,0:T(8,128)S(1)} %slice.100), channel_id=1, source_target_pairs={{0,6},{1,7},{2,4},{3,5},{4,2},{5,3},{6,0},{7,1},{8,14},{9,15},{10,... | collective-permute-start | bytes 98312 | tf_op jit(solution)/shard_map/ppermute | solution.py:172
  60.4 4.8 %collective-permute-start.22 = (f32[32,256]{1,0:T(8,128)S(1)}, f32[32,256]{1,0:T(8,128)S(1)}, u32[]{:S(2)}, u32[]{:S(2)}) collective-permute-start(f32[32,256]{1,0:T(8,128)S(1)} %slice.100), channel_id=1, source_target_pairs={{0,4},{1,5},{2,6},{3,7},{4,0},{5,1},{6,2},{7,3},{8,12},{9,13},{10,... | collective-permute-start | bytes 98312 | tf_op jit(solution)/shard_map/ppermute | solution.py:172
  60.4 4.8 %collective-permute-start.21 = (f32[32,256]{1,0:T(8,128)S(1)}, f32[32,256]{1,0:T(8,128)S(1)}, u32[]{:S(2)}, u32[]{:S(2)}) collective-permute-start(f32[32,256]{1,0:T(8,128)S(1)} %slice.100), channel_id=1, source_target_pairs={{0,2},{1,3},{2,0},{3,1},{4,6},{5,7},{6,4},{7,5},{8,10},{9,11},{10,... | collective-permute-start | bytes 98312 | tf_op jit(solution)/shard_map/ppermute | solution.py:172
  62.6 3.5 %collective-permute-start.13 = (f32[128,256]{1,0:T(8,128)S(1)}, f32[128,256]{1,0:T(8,128)S(1)}, u32[]{:S(2)}, u32[]{:S(2)}) collective-permute-start(f32[128,256]{1,0:T(8,128)S(1)} %pad_maximum_fusion.3), channel_id=1, source_target_pairs={{0,1},{1,0},{2,3},{3,2},{4,5},{5,4},{6,7},{7,6},{8,9},{9,8},{10,11... | collective-permute-start | bytes 393224 | tf_op jit(solution)/shard_map/ppermute | solution.py:172
  65.3 1.9 %collective-permute-start.24 = (f32[128,256]{1,0:T(8,128)S(1)}, f32[128,256]{1,0:T(8,128)S(1)}, u32[]{:S(2)}, u32[]{:S(2)}) collective-permute-start(f32[128,256]{1,0:T(8,128)S(1)} %pad_maximum_fusion.4.own_ref), channel_id=1, source_target_pairs={{0,1},{1,0},{2,3},{3,2},{4,5},{5,4},{6,7},{7,6},{8,9},{9,8},{10,11... | collective-permute-start | bytes 393224 | tf_op jit(solution)/shard_map/ppermute | solution.py:172
